TPU v7x, 256 devices: a whole 4x4x8 slice. The times are simulated.
256 devices in a mesh: slab: 64 (over x_lo, z, y), coil: 4 (over x_hi, core).
Axes of the slice: x: 4 (x_hi: 2, x_lo: 2; x = x_hi * 2 + x_lo), y: 4, z: 8, core: 2. Of those that a mesh axis runs over, the one named last changes fastest.
Arguments:
- init_image: float32 [2, 64, 256, 256], P(None, 'coil', 'slab'), may hold values from -6 to 6
- sens: float32 [2, 8, 64, 256, 256], P(None, 'coil', None, 'slab'), may hold values from -1.5 to 1.5
- kspace: float32 [2, 8, 64, 256, 256], P(None, 'coil', 'slab'), may hold values from -6 to 6
- mask: int32 [256, 256], replicated, may hold values 0 or 1
- weights: float32 [1, 48, 2, 3, 3, 3], replicated, may hold values from -0.3125 to 0.3125
- step_sizes: float32 [1], replicated, may hold values from 0.5 to 2
- recon_cotangent: float32 [2, 64, 256, 256], P(None, 'coil', 'slab'), may hold values from -0.009 to 0.009
Outputs:
- recon: float32 [2, 64, 256, 256], P(None, 'coil', 'slab')
- filter_grads: float32 [1, 48, 2, 3, 3, 3], replicated
- step_grads: float32 [1], replicated
All inputs are finite; a program needn't handle non-finite values.
Results may differ from a plain program's by a relative error of at most 0.0003.
Values sent between devices are 32-bit elements; how exact they have to be, the bound alone decides.
No kernel may reach another device: no remote copies, remote signals or barrier semaphores. Data moves between devices by JAX's collectives and lax.ppermute only.
A program may use at most 128 MiB of HBM per device.

v0:
```python
import jax
import jax.numpy as jnp
import numpy as np
from jax import lax
from jax.experimental import pallas as pl
from jax.experimental.pallas import tpu as pltpu
from jax.sharding import PartitionSpec as P

AXES = ("slab", "coil")
BF = jnp.bfloat16
F32 = jnp.float32


def device(coil, quarter, low):
    return (quarter * 16 + low) * 4 + coil


def spread_pairs(turn):
    return [
        (device(c, q, low), device((q + turn) % 4, c, low))
        for c in range(4)
        for q in range(4)
        for low in range(16)
    ]


def return_pairs(turn):
    return [
        (device(c, b, low), device(b, (c + turn) % 4, low))
        for c in range(4)
        for b in range(4)
        for low in range(16)
    ]


def rotated(pieces, start):
    twice = jnp.concatenate([pieces, pieces], axis=0)
    return lax.dynamic_slice_in_dim(twice, start, 4, axis=0)


def split(value):
    high = value.astype(BF)
    return high, (value - high.astype(F32)).astype(BF)


def split_outside(value):
    high = lax.reduce_precision(value, 8, 7)
    return high.astype(BF), (value - high).astype(BF)


def shifted(value, step):
    if step == 0:
        return value
    lane = lax.broadcasted_iota(jnp.int32, value.shape, value.ndim - 1)
    turned = pltpu.roll(value, step % 256, value.ndim - 1)
    edge = 0 if step > 0 else 255
    return jnp.where(lane == edge, 0.0, turned)


def filter_tables(weights):
    taps = np.zeros((3, 6, 8), np.float32)
    for d in range(3):
        for y in range(6):
            taps[d, y, y + d] = 1.0
    kernel = weights[0]
    ahead = sum(
        kernel[:, :, :, d][:, :, :, :, None, None] * taps[d] for d in range(3)
    )
    ahead = ahead.transpose(4, 0, 3, 2, 1, 5).reshape(288, 144)
    back = np.zeros((3, 4, 6), np.float32)
    for d in range(3):
        for y in range(4):
            back[d, y, y + 2 - d] = 1.0
    behind = sum(
        kernel[:, :, :, d][:, :, :, :, None, None] * back[d] for d in range(3)
    )
    behind = behind.transpose(2, 3, 1, 4, 5, 0).reshape(72, 288)
    high, low = split_outside(ahead)
    wide = jnp.concatenate([high, low, high], axis=1)
    high, low = split_outside(behind)
    turned = jnp.concatenate(
        [
            jnp.concatenate([high, high], axis=1),
            jnp.concatenate([low, jnp.zeros_like(low)], axis=1),
        ],
        axis=0,
    )
    return wide, turned


def conv_kernel(
    edge, init, grad, before, after, lower, upper, wide, turned, base, sums,
    xs, gs, xb, gb, acc,
):
    gs[:, :, 0:1] = jnp.zeros((18, 2, 1, 256), F32)
    gs[:, :, 7:8] = jnp.zeros((18, 2, 1, 256), F32)
    for i in range(2):
        xs[2:18, i, 2:6] = init[i]
        xs[2:18, i, 0:2] = before[i, :, 0:2]
        xs[2:18, i, 6:8] = after[i, :, 0:2]
        xs[0:2, i] = lower[2 * i : 2 * i + 2]
        xs[18:20, i] = upper[2 * i : 2 * i + 2]
        gs[1:17, i, 2:6] = grad[i]
        gs[1:17, i, 1:2] = before[i, :, 2:3]
        gs[1:17, i, 6:7] = after[i, :, 2:3]
        gs[0:1, i, 1:7] = lower[4 + i : 5 + i, 0:6]
        gs[17:18, i, 1:7] = upper[4 + i : 5 + i, 0:6]
    for plain, packed, count in ((xs, xb, 320), (gs, gb, 288)):
        value = plain[...].reshape(count, 256)
        for d in range(3):
            high, low = split(shifted(value, 1 - d))
            packed[d, 0] = high
            packed[d, 1] = low
    acc[...] = jnp.zeros_like(acc)
    sums[...] = jnp.zeros_like(sums)
    row = lax.broadcasted_iota(jnp.int32, (288, 256), 0)
    keep = jnp.where(row < 48, edge[0], jnp.where(row >= 240, edge[1], 1.0))

    def window(packed, place, part):
        start = pl.multiple_of(place * 16, 16)
        return jnp.concatenate(
            [packed[d, part, pl.ds(start, 48)] for d in range(3)], axis=0
        )

    def forward(place, table, packed):
        high = window(packed, place, 0)
        low = window(packed, place, 1)
        data = jnp.concatenate([high, high, low], axis=0)
        return jnp.dot(table, data, preferred_element_type=F32), high, low

    def scatter(place, high, low):
        data = jnp.concatenate([high, low], axis=0)
        product = jnp.dot(turned[...], data, preferred_element_type=F32)
        product = product[:72] + product[72:]
        for r in range(3):
            for d in range(3):
                first = (r * 3 + d) * 8
                acc[d, pl.ds(place + r, 1)] += product[first : first + 8][None]

    for place, scale in ((0, edge[2]), (17, edge[3])):
        response, _, _ = forward(place, wide[...], xb)
        high, low = split(jnp.tanh(response) * (keep * scale))
        scatter(place, high, low)

    def step(r, carry):
        response, xh, xl = forward(r + 1, wide[...], xb)
        linear, gh, gl = forward(r, wide[48:240], gb)
        active = jnp.tanh(response) * keep
        core = active[48:240]
        weighted = (1.0 - core * core) * linear
        high, low = split(active)
        wh, wl = split(weighted)
        ch, cl = high[48:240], low[48:240]
        left = jnp.concatenate([gh, gh, gl, xh, xh, xl], axis=1)
        right = jnp.concatenate([ch, cl, ch, wh, wl, wh], axis=1)
        sums[...] += lax.dot_general(
            left, right, (((1,), (1,)), ((), ())), preferred_element_type=F32
        )
        scatter(r + 1, high, low)
        return carry

    lax.fori_loop(0, 16, step, 0)
    total = (
        shifted(acc[0, 2:18].reshape(128, 256), -1)
        + acc[1, 2:18].reshape(128, 256)
        + shifted(acc[2, 2:18].reshape(128, 256), 1)
    ).reshape(16, 8, 256)
    for i in range(2):
        base[i] = init[i] - total[:, 4 * i : 4 * i + 4]


def conv_call(edge, init, grad, before, after, lower, upper, wide, turned):
    vm = pl.BlockSpec(memory_space=pltpu.VMEM)
    return pl.pallas_call(
        conv_kernel,
        out_shape=(
            jax.ShapeDtypeStruct((2, 16, 4, 256), F32),
            jax.ShapeDtypeStruct((144, 192), F32),
        ),
        in_specs=[pl.BlockSpec(memory_space=pltpu.SMEM)] + [vm] * 8,
        out_specs=(vm, vm),
        scratch_shapes=[
            pltpu.VMEM((20, 2, 8, 256), F32),
            pltpu.VMEM((18, 2, 8, 256), F32),
            pltpu.VMEM((3, 2, 320, 256), BF),
            pltpu.VMEM((3, 2, 288, 256), BF),
            pltpu.VMEM((3, 20, 8, 256), F32),
        ],
        cost_estimate=pl.CostEstimate(
            flops=6000000000, bytes_accessed=2000000, transcendentals=1300000
        ),
    )(edge, init, grad, before, after, lower, upper, wide, turned)


def diagonal(sums):
    cube = sums.reshape(3, 3, 2, 8, 4, 48)
    taps = [
        sum(cube[:, :, :, y + 1 + d, y] for y in range(4)) for d in range(3)
    ]
    return jnp.stack(taps, axis=3)


def tables():
    place = np.arange(256)
    mixed = place % 64 * 4 + place // 64
    made = []
    for first, second in ((place, place), (place, mixed), (mixed, place)):
        angle = (first[:, None] * second[None, :] % 256) * (2.0 * np.pi / 256)
        for table in (np.cos(angle) / 16.0, np.sin(angle) / 16.0):
            table = np.asarray(table, np.float32)
            high = table.astype(BF)
            made.append(high)
            made.append((table - high.astype(np.float32)).astype(BF))
    return made


def transform_kernel(
    coil, maps, p0, p1, p2, p3, kspace, mask, ch, cl, sh, sl, yh, yl, zh, zl,
    uh, ul, wh, wl, o0, o1, o2, o3, rows, right, left, lhs, rhs,
):
    here = coil[0]
    pieces = (p0, p1, p2, p3)
    outs = (o0, o1, o2, o3)
    for a in range(4):
        @pl.when(here == a)
        def _():
            for q in range(4):
                rows[q] = pieces[(a - q) % 4][...]
    for part, cosine, sine in ((0, ch, sh), (1, cl, sl)):
        right[part, :256, :256] = cosine[...]
        right[part, :256, 256:] = -sine[...]
        right[part, 256:, :256] = sine[...]
        right[part, 256:, 256:] = cosine[...]
    for part, cosine, sine in ((0, yh, zh), (1, yl, zl), (2, uh, wh), (3, ul, wl)):
        left[part, :256, :256] = cosine[...]
        left[part, :256, 256:] = sine[...]
        left[part, 256:, :256] = -sine[...]
        left[part, 256:, 256:] = cosine[...]

    def halves(load):
        return jnp.concatenate(
            [
                jnp.concatenate([load(y, h) for h in range(2)], axis=1)
                for y in range(4)
            ],
            axis=0,
        )

    def map_of(part, c):
        return halves(
            lambda y, h: maps[pl.ds((y * 4 + part * 2 + c) * 2 + h, 64, stride=40), :]
        )

    def image_of(part):
        return halves(lambda y, h: rows[y, pl.ds(part * 2 + h, 64, stride=4), :])

    def transform(pairs, side):
        for c in range(2):
            for part in range(2):
                high, low = split(pairs[c][part])
                lhs[0, c * 256 : c * 256 + 256, part * 256 : part * 256 + 256] = high
                lhs[1, c * 256 : c * 256 + 256, part * 256 : part * 256 + 256] = low
        for c in range(2):
            block = slice(c * 256, c * 256 + 256)
            value = (
                jnp.dot(lhs[0, block], right[0], preferred_element_type=F32)
                + jnp.dot(lhs[1, block], right[0], preferred_element_type=F32)
                + jnp.dot(lhs[0, block], right[1], preferred_element_type=F32)
            )
            for part in range(2):
                high, low = split(value[:, part * 256 : part * 256 + 256])
                rhs[0, part * 256 : part * 256 + 256, block] = high
                rhs[1, part * 256 : part * 256 + 256, block] = low
        out = []
        for part in range(2):
            block = slice(part * 256, part * 256 + 256)
            out.append(
                jnp.dot(left[side, block], rhs[0], preferred_element_type=F32)
                + jnp.dot(left[side, block], rhs[1], preferred_element_type=F32)
                + jnp.dot(left[side + 1, block], rhs[0], preferred_element_type=F32)
            )
        return [
            [out[part][:, c * 256 : c * 256 + 256] for part in range(2)]
            for c in range(2)
        ]

    vr, vi = image_of(0), image_of(1)
    pairs = []
    for c in range(2):
        sr, si = map_of(0, c), map_of(1, c)
        pairs.append([sr * vr - si * vi, sr * vi + si * vr])
    pairs = transform(pairs, 0)
    keep = mask[...].astype(F32)

    pairs = [
        [
            (pairs[c][0] - kspace[0, c]) * keep,
            (kspace[1, c] - pairs[c][1]) * keep,
        ]
        for c in range(2)
    ]
    pairs = transform(pairs, 2)
    back_re = 0.0
    back_im = 0.0
    for c in range(2):
        sr, si = map_of(0, c), map_of(1, c)
        xr, xi = pairs[c][0], -pairs[c][1]
        back_re = back_re + sr * xr + si * xi
        back_im = back_im + sr * xi - si * xr
    back = (back_re, back_im)
    for a in range(4):
        @pl.when(here == a)
        def _():
            for j in range(4):
                q = (a + j) % 4
                for part in range(2):
                    for h in range(2):
                        outs[j][pl.ds(part * 2 + h, 64, stride=4), :] = back[part][
                            q * 64 : q * 64 + 64, h * 128 : h * 128 + 128
                        ]


def transform_call(coil, maps, pieces, kspace, mask):
    vm = pl.BlockSpec(memory_space=pltpu.VMEM)
    consts = tables()
    return pl.pallas_call(
        transform_kernel,
        out_shape=tuple(jax.ShapeDtypeStruct((256, 128), F32) for _ in range(4)),
        in_specs=[pl.BlockSpec(memory_space=pltpu.SMEM)] + [vm] * 19,
        out_specs=(vm,) * 4,
        scratch_shapes=[
            pltpu.VMEM((4, 256, 128), F32),
            pltpu.VMEM((2, 512, 512), BF),
            pltpu.VMEM((4, 512, 512), BF),
            pltpu.VMEM((2, 512, 512), BF),
            pltpu.VMEM((2, 512, 512), BF),
        ],
        cost_estimate=pl.CostEstimate(
            flops=6000000000, bytes_accessed=5000000, transcendentals=0
        ),
    )(coil, maps, *pieces, kspace, mask, *[jnp.asarray(t) for t in consts])


def halos(state, grad, slab_count):
    up = [(i, i + 1) for i in range(slab_count - 1)]
    down = [(i + 1, i) for i in range(slab_count - 1)]
    high = jnp.concatenate([state[:, :, 2:], grad[:, :, 3:]], axis=2)
    low = jnp.concatenate([state[:, :, :2], grad[:, :, :1]], axis=2)
    before = lax.ppermute(high, "slab", up)
    after = lax.ppermute(low, "slab", down)

    def planes(at, last):
        rows = jnp.concatenate(
            [before[:, at, :2], state[:, at], after[:, at, :2]], axis=2
        ).reshape(4, 8, 256)
        edge = jnp.concatenate(
            [before[:, last, 2:], grad[:, last], after[:, last, 2:]], axis=1
        )
        return jnp.concatenate([rows, jnp.pad(edge, ((0, 0), (0, 2), (0, 0)))], axis=0)

    up = [(i, i + 1) for i in range(3)]
    down = [(i + 1, i) for i in range(3)]
    lower = lax.ppermute(planes(slice(14, 16), 15), "coil", up)
    upper = lax.ppermute(planes(slice(0, 2), 0), "coil", down)
    return before, after, lower, upper


def on_device(init_image, sens, kspace, mask, weights, step_sizes, recon_cotangent):
    slab_count = lax.axis_size("slab")
    coil = lax.axis_index("coil")
    slab = lax.axis_index("slab")
    maps = sens.transpose(2, 3, 0, 1, 4).reshape(64, 16, 2, 128)
    images = jnp.stack([init_image, recon_cotangent]).transpose(3, 2, 0, 1, 4)
    payload = jnp.concatenate([maps, images.reshape(64, 4, 2, 128)], axis=1)
    received = lax.all_to_all(payload, "slab", split_axis=0, concat_axis=0, tiled=True)

    before, after, lower, upper = halos(init_image, recon_cotangent, slab_count)
    wide, turned = filter_tables(weights)
    edge = jnp.stack([slab > 0, slab < slab_count - 1, coil > 0, coil < 3]).astype(F32)
    base, sums = conv_call(
        edge, init_image, recon_cotangent, before, after, lower, upper, wide, turned
    )
    partial = jnp.pad(-diagonal(sums).reshape(2592), (0, 224)).reshape(256, 11)
    chunk = jnp.sum(
        lax.all_to_all(partial, AXES, split_axis=0, concat_axis=0, tiled=True), axis=0
    )

    state_rows = received[:, 16:18].reshape(256, 128)
    grad_rows = received[:, 18:20].reshape(256, 128)
    pieces = [lax.ppermute(state_rows, AXES, spread_pairs(turn)) for turn in range(4)]
    parts = transform_call(
        coil.reshape(1), received.reshape(2560, 128), pieces, kspace[:, :, 0], mask
    )
    total = sum(
        lax.ppermute(parts[turn], AXES, return_pairs(turn)) for turn in range(4)
    )
    product = jnp.sum(total * grad_rows)
    rider = jnp.concatenate([chunk, -product[None], jnp.zeros((244,), F32)])
    rider = jnp.broadcast_to(rider.reshape(1, 1, 2, 128), (64, 1, 2, 128))
    sent = jnp.concatenate([total.reshape(64, 2, 2, 128), rider], axis=1)
    arrived = lax.all_to_all(sent, "slab", split_axis=0, concat_axis=0, tiled=True)
    combined = arrived[:, :2].reshape(4, 16, 2, 256).transpose(2, 1, 0, 3)
    recon = base - step_sizes[0] * combined
    riders = arrived[:, 2, 0, :12]
    small = jnp.concatenate([riders[:, :11].reshape(704), jnp.sum(riders[:, 11])[None]])
    small = jnp.pad(small, (0, 319)).reshape(8, 128)
    others = [small] + [
        lax.ppermute(small, "coil", [(i, (i + turn) % 4) for i in range(4)])
        for turn in range(1, 4)
    ]
    reverse = jnp.stack([others[0], others[3], others[2], others[1]])
    ordered = rotated(reverse, (4 - coil) % 4).reshape(4, 1024)
    step_grads = jnp.sum(ordered[:, 704])[None]
    grads = ordered[:, :704].reshape(4, 64, 11).transpose(1, 0, 2).reshape(2816)[:2592]
    grads = grads.reshape(3, 3, 2, 3, 48).transpose(4, 2, 1, 3, 0)
    return recon, grads[None], step_grads


def solution(mesh):
    return jax.shard_map(
        on_device,
        mesh=mesh,
        in_specs=(
            P(None, "coil", "slab", None),
            P(None, "coil", None, "slab", None),
            P(None, "coil", "slab", None, None),
            P(),
            P(),
            P(),
            P(None, "coil", "slab", None),
        ),
        out_specs=(P(None, "coil", "slab", None), P(), P()),
        check_vma=False,
    )
```

profile of v0, /device:TPU:1, one launch (start us, length us, event | category | flops | bytes accessed | tf_op | source)
XLA Modules:
  0.0 153.1 jit_solution(8793458725672538060)
XLA Ops:
  0.6 1.1 fusion.7
  2.8 4.0 %collective-permute-start = (f32[2,16,3,256]{3,1,2,0:T(8,128)S(1)}, f32[2,16,3,256]{3,1,2,0:T(8,128)S(1)}, u32[]{:S(2)}, u32[]{:S(2)}) collective-permute-start(f32[2,16,3,256]{3,1,2,0:T(8,128)S(1)} %pad_maximum_fusion.3), channel_id=1, source_target_pairs={{0,4},{4,8},{8,12},{12,16},{16,20},{20,24},{24,28},{28,32},{32,36}... | collective-permute-start | bytes 294920 | tf_op jit(solution)/shard_map/ppermute | solution.py:349
  6.9 1.3 collective-permute-start.1
  10.3 1.6 %copy.147 = f32[64,20,2,128]{3,2,1,0:T(2,128)} copy(f32[64,20,2,128]{3,2,0,1:T(2,128)S(1)} %pad_maximum_fusion) | data formatting | bytes 2621440 | tf_op jit(solution)/shard_map/concatenate | solution.py:374
  11.9 14.4 %all-to-all-start = ((f32[64,20,2,128]{3,2,1,0:T(2,128)}), f32[64,20,2,128]{3,2,1,0:T(2,128)S(1)}, u32[]{:S(2)}, u32[]{:S(2)}) async-start(f32[64,20,2,128]{3,2,1,0:T(2,128)} %copy.147), calls=%async_computation | async-start | bytes 2621440 | tf_op jit(solution)/shard_map/all_to_all | solution.py:375
  29.5 3.4 %collective-permute-start.3 = (f32[6,8,256]{2,1,0:T(8,128)S(1)}, f32[6,8,256]{2,1,0:T(8,128)S(1)}, u32[]{:S(2)}, u32[]{:S(2)}) collective-permute-start(f32[6,8,256]{2,1,0:T(8,128)S(1)} %pad_maximum_fusion.6), channel_id=1, source_target_pairs={{1,0},{2,1},{3,2},{5,4},{6,5},{7,6},{9,8},{10,9},{11,10},{13,12},{... | collective-permute-start | bytes 147464 | tf_op jit(solution)/shard_map/ppermute | solution.py:364
  32.9 4.3 %collective-permute-start.2 = (f32[6,8,256]{2,1,0:T(8,128)S(1)}, f32[6,8,256]{2,1,0:T(8,128)S(1)}, u32[]{:S(2)}, u32[]{:S(2)}) collective-permute-start(f32[6,8,256]{2,1,0:T(8,128)S(1)} %pad_maximum_fusion.5), channel_id=1, source_target_pairs={{0,1},{1,2},{2,3},{4,5},{5,6},{6,7},{8,9},{9,10},{10,11},{12,13},{... | collective-permute-start | bytes 147464 | tf_op jit(solution)/shard_map/ppermute | solution.py:363
  40.5 15.1 %shard_map.256 = (f32[2,16,4,256]{3,2,1,0:T(4,128)}, f32[144,192]{1,0:T(8,128)}) custom-call(f32[4]{0:T(128)} %add_convert_fusion.edge, f32[2,16,4,256]{3,2,1,0:T(4,128)} %init.1, f32[2,16,4,256]{3,2,1,0:T(4,128)} %grad.1, f32[2,16,3,256]{3,2,1,0:T(4,128)} %copy.143.before, f32[2,16,3,256]{3,2,1,0:T(4,128)} %copy.144.after, f32[6,8,256]{2,1,0:T(8,128)} %copy-done.17, ...), custom_call_target="tpu_custom_call" | custom-call | flops 6000000000 | bytes 2000000 | tf_op jit(solution)/shard_map/pallas_call | solution.py:174
  55.6 1.1 reshape.229
  56.9 1.0 all-to-all-done
  58.0 7.5 %collective-permute-start.4 = (f32[256,128]{1,0:T(8,128)S(1)}, f32[256,128]{1,0:T(8,128)S(1)}, u32[]{:S(2)}, u32[]{:S(2)}) collective-permute-start(f32[256,128]{1,0:T(8,128)S(1)} %bitcast.131), channel_id=1, source_target_pairs={{0,0},{4,4},{8,8},{12,12},{16,16},{20,20},{24,24},{28,28},{32,32},... | collective-permute-start | bytes 393224 | tf_op jit(solution)/shard_map/ppermute | solution.py:390
  65.6 3.7 %collective-permute-start.6 = (f32[256,128]{1,0:T(8,128)S(1)}, f32[256,128]{1,0:T(8,128)S(1)}, u32[]{:S(2)}, u32[]{:S(2)}) collective-permute-start(f32[256,128]{1,0:T(8,128)S(1)} %bitcast.133), channel_id=1, source_target_pairs={{0,2},{4,6},{8,10},{12,14},{16,18},{20,22},{24,26},{28,30},{32,34}... | collective-permute-start | bytes 393224 | tf_op jit(solution)/shard_map/ppermute | solution.py:390
  69.3 1.5 collective-permute-start.7
  70.8 4.1 %collective-permute-done.6.p2 = f32[256,128]{1,0:T(8,128)S(1)} collective-permute-done((f32[256,128]{1,0:T(8,128)S(1)}, f32[256,128]{1,0:T(8,128)S(1)}, u32[]{:S(2)}, u32[]{:S(2)}) %collective-permute-start.6) | collective-permute-done | bytes 131104 | tf_op jit(solution)/shard_map/ppermute | solution.py:390
  75.8 7.3 %shard_map.257 = (f32[256,128]{1,0:T(8,128)}, f32[256,128]{1,0:T(8,128)}, f32[256,128]{1,0:T(8,128)}, f32[256,128]{1,0:T(8,128)}) custom-call(s32[1]{0:T(128)} %bitcast.23.coil, f32[2560,128]{1,0:T(8,128)} %bitcast.118, f32[256,128]{1,0:T(8,128)} %copy-done.12, f32[256,128]{1,0:T(8,128)} %copy-done.13, f32[256,128]{1,0:T(8,128)} %copy-done.14, ...), custom_call_target="tpu_custom_call" | custom-call | flops 6000000000 | bytes 5000000 | tf_op jit(solution)/shard_map/pallas_call | solution.py:326
  83.0 5.1 %collective-permute-start.10 = (f32[256,128]{1,0:T(8,128)}, f32[256,128]{1,0:T(8,128)S(1)}, u32[]{:S(2)}, u32[]{:S(2)}) collective-permute-start(f32[256,128]{1,0:T(8,128)} %get-tuple-element.12), channel_id=1, source_target_pairs={{0,128},{4,132},{8,136},{12,140},{16,144},{20,148},{24,152},{28,15... | collective-permute-start | bytes 393224 | tf_op jit(solution)/shard_map/ppermute | solution.py:395
  88.1 1.7 %collective-permute-start.11 = (f32[256,128]{1,0:T(8,128)}, f32[256,128]{1,0:T(8,128)S(1)}, u32[]{:S(2)}, u32[]{:S(2)}) collective-permute-start(f32[256,128]{1,0:T(8,128)} %get-tuple-element.13), channel_id=1, source_target_pairs={{0,192},{4,196},{8,200},{12,204},{16,208},{20,212},{24,216},{28,22... | collective-permute-start | bytes 393224 | tf_op jit(solution)/shard_map/ppermute | solution.py:395
  89.8 6.6 %collective-permute-start.8 = (f32[256,128]{1,0:T(8,128)}, f32[256,128]{1,0:T(8,128)S(1)}, u32[]{:S(2)}, u32[]{:S(2)}) collective-permute-start(f32[256,128]{1,0:T(8,128)} %get-tuple-element.10), channel_id=1, source_target_pairs={{0,0},{4,4},{8,8},{12,12},{16,16},{20,20},{24,24},{28,28},{32,32},... | collective-permute-start | bytes 393224 | tf_op jit(solution)/shard_map/ppermute | solution.py:395
  96.4 1.1 collective-permute-start.9
  97.9 25.8 %all_to_all.19 = f32[256,1,11]{2,1,0:T(1,128)S(1)} all-to-all(f32[256,1,11]{2,1,0:T(1,128)S(1)} %bitcast.122), channel_id=1, replica_groups=mesh['slab'=64,'coil'=4] {'slab','coil'}, dimensions={0} | all-to-all | bytes 22528 | tf_op jit(solution)/shard_map/all_to_all | solution.py:385
  126.2 4.6 %all-to-all-start.2 = ((f32[64,3,2,128]{3,2,1,0:T(2,128)}), f32[64,3,2,128]{3,2,1,0:T(2,128)S(1)}, u32[]{:S(2)}, u32[]{:S(2)}) async-start(f32[64,3,2,128]{3,2,1,0:T(2,128)} %pad_maximum_fusion.2), calls=%async_computation.2 | async-start | bytes 393216 | tf_op jit(solution)/shard_map/all_to_all | solution.py:401
  131.5 9.9 %all-to-all-done.2 = f32[64,3,2,128]{3,2,1,0:T(2,128)S(1)} async-done(((f32[64,3,2,128]{3,2,1,0:T(2,128)}), f32[64,3,2,128]{3,2,1,0:T(2,128)S(1)}, u32[]{:S(2)}, u32[]{:S(2)}) %all-to-all-start.2) | async-done | bytes 196640 | tf_op jit(solution)/shard_map/all_to_all | solution.py:401
  142.9 2.6 %collective-permute-start.12 = (f32[8,128]{1,0:T(8,128)S(1)}, f32[8,128]{1,0:T(8,128)S(1)}, u32[]{:S(2)}, u32[]{:S(2)}) collective-permute-start(f32[8,128]{1,0:T(8,128)S(1)} %fusion.3), channel_id=1, source_target_pairs={{0,3},{1,0},{2,1},{3,2},{4,7},{5,4},{6,5},{7,6},{8,11},{9,8},{10,9... | collective-permute-start | bytes 12296 | tf_op jit(solution)/shard_map/ppermute | solution.py:408
  146.4 2.3 %collective-permute-start.14 = (f32[8,128]{1,0:T(8,128)S(1)}, f32[8,128]{1,0:T(8,128)S(1)}, u32[]{:S(2)}, u32[]{:S(2)}) collective-permute-start(f32[8,128]{1,0:T(8,128)S(1)} %fusion.3), channel_id=1, source_target_pairs={{0,1},{1,2},{2,3},{3,0},{4,5},{5,6},{6,7},{7,4},{8,9},{9,10},{10,1... | collective-permute-start | bytes 12296 | tf_op jit(solution)/shard_map/ppermute | solution.py:408
  (136 shorter events, 19.4 us)
Async XLA Ops:
  0.6 7.6 %copy-start.1 = (f32[2,2,64,4,256]{4,3,2,1,0:T(4,128)S(1)}, f32[2,2,64,4,256]{4,3,2,1,0:T(4,128)}, u32[]{:S(2)}) copy-start(f32[2,2,64,4,256]{4,3,2,1,0:T(4,128)} %param.26) | copy-start | bytes 3145732
  2.8 26.4 %collective-permute-start = (f32[2,16,3,256]{3,1,2,0:T(8,128)S(1)}, f32[2,16,3,256]{3,1,2,0:T(8,128)S(1)}, u32[]{:S(2)}, u32[]{:S(2)}) collective-permute-start(f32[2,16,3,256]{3,1,2,0:T(8,128)S(1)} %pad_maximum_fusion.3), channel_id=1, source_target_pairs={{0,4},{4,8},{8,12},{12,16},{16,20},{20,24},{24,28},{28,32},{32,36}... | collective-permute-start | bytes 294920 | tf_op jit(solution)/shard_map/ppermute | solution.py:349
  6.9 22.4 %collective-permute-start.1 = (f32[2,16,3,256]{3,1,2,0:T(8,128)S(1)}, f32[2,16,3,256]{3,1,2,0:T(8,128)S(1)}, u32[]{:S(2)}, u32[]{:S(2)}) collective-permute-start(f32[2,16,3,256]{3,1,2,0:T(8,128)S(1)} %pad_maximum_fusion.4), channel_id=1, source_target_pairs={{4,0},{8,4},{12,8},{16,12},{20,16},{24,20},{28,24},{32,28},{36,32}... | collective-permute-start | bytes 294920 | tf_op jit(solution)/shard_map/ppermute | solution.py:350
  11.9 14.4 %copy-start.5 = (f32[1,48,2,3,3,3]{1,2,5,4,3,0:T(2,128)S(1)}, f32[1,48,2,3,3,3]{1,2,5,4,3,0:T(2,128)}, u32[]{:S(2)}) copy-start(f32[1,48,2,3,3,3]{1,2,5,4,3,0:T(2,128)} %param.29) | copy-start | bytes 31108
  11.9 14.4 %copy-start.6 = (f32[6,8]{0,1:T(8,128)S(1)}, f32[6,8]{0,1:T(8,128)}, u32[]{:S(2)}) copy-start(f32[6,8]{0,1:T(8,128)} %constant.70.clone) | copy-start | bytes 580
  11.9 14.4 %copy-start.7 = (f32[6,8]{0,1:T(8,128)S(1)}, f32[6,8]{0,1:T(8,128)}, u32[]{:S(2)}) copy-start(f32[6,8]{0,1:T(8,128)} %constant.71.clone) | copy-start | bytes 580
  11.9 14.4 %copy-start.8 = (f32[6,8]{0,1:T(8,128)S(1)}, f32[6,8]{0,1:T(8,128)}, u32[]{:S(2)}) copy-start(f32[6,8]{0,1:T(8,128)} %constant.72.clone) | copy-start | bytes 580
  11.9 46.0 %all-to-all-start = ((f32[64,20,2,128]{3,2,1,0:T(2,128)}), f32[64,20,2,128]{3,2,1,0:T(2,128)S(1)}, u32[]{:S(2)}, u32[]{:S(2)}) async-start(f32[64,20,2,128]{3,2,1,0:T(2,128)} %copy.147), calls=%async_computation | async-start | bytes 2621440 | tf_op jit(solution)/shard_map/all_to_all | solution.py:375
  29.5 9.8 %collective-permute-start.3 = (f32[6,8,256]{2,1,0:T(8,128)S(1)}, f32[6,8,256]{2,1,0:T(8,128)S(1)}, u32[]{:S(2)}, u32[]{:S(2)}) collective-permute-start(f32[6,8,256]{2,1,0:T(8,128)S(1)} %pad_maximum_fusion.6), channel_id=1, source_target_pairs={{1,0},{2,1},{3,2},{5,4},{6,5},{7,6},{9,8},{10,9},{11,10},{13,12},{... | collective-permute-start | bytes 147464 | tf_op jit(solution)/shard_map/ppermute | solution.py:364
  32.9 6.4 %collective-permute-start.2 = (f32[6,8,256]{2,1,0:T(8,128)S(1)}, f32[6,8,256]{2,1,0:T(8,128)S(1)}, u32[]{:S(2)}, u32[]{:S(2)}) collective-permute-start(f32[6,8,256]{2,1,0:T(8,128)S(1)} %pad_maximum_fusion.5), channel_id=1, source_target_pairs={{0,1},{1,2},{2,3},{4,5},{5,6},{6,7},{8,9},{9,10},{10,11},{12,13},{... | collective-permute-start | bytes 147464 | tf_op jit(solution)/shard_map/ppermute | solution.py:363
  57.9 17.2 %copy-start = (f32[64,20,2,128]{3,2,1,0:T(2,128)}, f32[64,20,2,128]{3,2,1,0:T(2,128)S(1)}, u32[]{:S(2)}) copy-start(f32[64,20,2,128]{3,2,1,0:T(2,128)S(1)} %all-to-all-done) | copy-start | bytes 3932164
  58.0 12.8 %collective-permute-start.4 = (f32[256,128]{1,0:T(8,128)S(1)}, f32[256,128]{1,0:T(8,128)S(1)}, u32[]{:S(2)}, u32[]{:S(2)}) collective-permute-start(f32[256,128]{1,0:T(8,128)S(1)} %bitcast.131), channel_id=1, source_target_pairs={{0,0},{4,4},{8,8},{12,12},{16,16},{20,20},{24,24},{28,28},{32,32},... | collective-permute-start | bytes 393224 | tf_op jit(solution)/shard_map/ppermute | solution.py:390
  65.5 5.3 %collective-permute-start.5 = (f32[256,128]{1,0:T(8,128)S(1)}, f32[256,128]{1,0:T(8,128)S(1)}, u32[]{:S(2)}, u32[]{:S(2)}) collective-permute-start(f32[256,128]{1,0:T(8,128)S(1)} %bitcast.132), channel_id=1, source_target_pairs={{0,1},{4,5},{8,9},{12,13},{16,17},{20,21},{24,25},{28,29},{32,33},... | collective-permute-start | bytes 393224 | tf_op jit(solution)/shard_map/ppermute | solution.py:390
  65.6 9.4 %collective-permute-start.6 = (f32[256,128]{1,0:T(8,128)S(1)}, f32[256,128]{1,0:T(8,128)S(1)}, u32[]{:S(2)}, u32[]{:S(2)}) collective-permute-start(f32[256,128]{1,0:T(8,128)S(1)} %bitcast.133), channel_id=1, source_target_pairs={{0,2},{4,6},{8,10},{12,14},{16,18},{20,22},{24,26},{28,30},{32,34}... | collective-permute-start | bytes 393224 | tf_op jit(solution)/shard_map/ppermute | solution.py:390
  69.3 5.8 %collective-permute-start.7 = (f32[256,128]{1,0:T(8,128)S(1)}, f32[256,128]{1,0:T(8,128)S(1)}, u32[]{:S(2)}, u32[]{:S(2)}) collective-permute-start(f32[256,128]{1,0:T(8,128)S(1)} %bitcast.134), channel_id=1, source_target_pairs={{0,3},{4,7},{8,11},{12,15},{16,19},{20,23},{24,27},{28,31},{32,35}... | collective-permute-start | bytes 393224 | tf_op jit(solution)/shard_map/ppermute | solution.py:390
  83.0 40.9 %collective-permute-start.10 = (f32[256,128]{1,0:T(8,128)}, f32[256,128]{1,0:T(8,128)S(1)}, u32[]{:S(2)}, u32[]{:S(2)}) collective-permute-start(f32[256,128]{1,0:T(8,128)} %get-tuple-element.12), channel_id=1, source_target_pairs={{0,128},{4,132},{8,136},{12,140},{16,144},{20,148},{24,152},{28,15... | collective-permute-start | bytes 393224 | tf_op jit(solution)/shard_map/ppermute | solution.py:395
  88.1 35.8 %collective-permute-start.11 = (f32[256,128]{1,0:T(8,128)}, f32[256,128]{1,0:T(8,128)S(1)}, u32[]{:S(2)}, u32[]{:S(2)}) collective-permute-start(f32[256,128]{1,0:T(8,128)} %get-tuple-element.13), channel_id=1, source_target_pairs={{0,192},{4,196},{8,200},{12,204},{16,208},{20,212},{24,216},{28,22... | collective-permute-start | bytes 393224 | tf_op jit(solution)/shard_map/ppermute | solution.py:395
  89.8 34.1 %collective-permute-start.8 = (f32[256,128]{1,0:T(8,128)}, f32[256,128]{1,0:T(8,128)S(1)}, u32[]{:S(2)}, u32[]{:S(2)}) collective-permute-start(f32[256,128]{1,0:T(8,128)} %get-tuple-element.10), channel_id=1, source_target_pairs={{0,0},{4,4},{8,8},{12,12},{16,16},{20,20},{24,24},{28,28},{32,32},... | collective-permute-start | bytes 393224 | tf_op jit(solution)/shard_map/ppermute | solution.py:395
  96.4 27.6 %collective-permute-start.9 = (f32[256,128]{1,0:T(8,128)}, f32[256,128]{1,0:T(8,128)S(1)}, u32[]{:S(2)}, u32[]{:S(2)}) collective-permute-start(f32[256,128]{1,0:T(8,128)} %get-tuple-element.11), channel_id=1, source_target_pairs={{0,64},{4,68},{8,72},{12,76},{16,80},{20,84},{24,88},{28,92},{32,9... | collective-permute-start | bytes 393224 | tf_op jit(solution)/shard_map/ppermute | solution.py:395
  124.0 25.0 %copy-start.4 = (f32[2,16,4,256]{3,2,1,0:T(4,128)S(1)}, f32[2,16,4,256]{3,2,1,0:T(4,128)}, u32[]{:S(2)}) copy-start(f32[2,16,4,256]{3,2,1,0:T(4,128)} %get-tuple-element.9) | copy-start | bytes 393220
  126.2 15.1 %all-to-all-start.2 = ((f32[64,3,2,128]{3,2,1,0:T(2,128)}), f32[64,3,2,128]{3,2,1,0:T(2,128)S(1)}, u32[]{:S(2)}, u32[]{:S(2)}) async-start(f32[64,3,2,128]{3,2,1,0:T(2,128)} %pad_maximum_fusion.2), calls=%async_computation.2 | async-start | bytes 393216 | tf_op jit(solution)/shard_map/all_to_all | solution.py:401
  142.9 7.6 %collective-permute-start.12 = (f32[8,128]{1,0:T(8,128)S(1)}, f32[8,128]{1,0:T(8,128)S(1)}, u32[]{:S(2)}, u32[]{:S(2)}) collective-permute-start(f32[8,128]{1,0:T(8,128)S(1)} %fusion.3), channel_id=1, source_target_pairs={{0,3},{1,0},{2,1},{3,2},{4,7},{5,4},{6,5},{7,6},{8,11},{9,8},{10,9... | collective-permute-start | bytes 12296 | tf_op jit(solution)/shard_map/ppermute | solution.py:408
  145.5 5.0 %collective-permute-start.13 = (f32[8,128]{1,0:T(8,128)S(1)}, f32[8,128]{1,0:T(8,128)S(1)}, u32[]{:S(2)}, u32[]{:S(2)}) collective-permute-start(f32[8,128]{1,0:T(8,128)S(1)} %fusion.3), channel_id=1, source_target_pairs={{0,2},{1,3},{2,0},{3,1},{4,6},{5,7},{6,4},{7,5},{8,10},{9,11},{10,... | collective-permute-start | bytes 12296 | tf_op jit(solution)/shard_map/ppermute | solution.py:408
  146.4 4.1 %collective-permute-start.14 = (f32[8,128]{1,0:T(8,128)S(1)}, f32[8,128]{1,0:T(8,128)S(1)}, u32[]{:S(2)}, u32[]{:S(2)}) collective-permute-start(f32[8,128]{1,0:T(8,128)S(1)} %fusion.3), channel_id=1, source_target_pairs={{0,1},{1,2},{2,3},{3,0},{4,5},{5,6},{6,7},{7,4},{8,9},{9,10},{10,1... | collective-permute-start | bytes 12296 | tf_op jit(solution)/shard_map/ppermute | solution.py:408
  (11 other events, 15.1 us)
where the time goes:
time: 154 us; the launch traced here: 153 us
  starting transfers between devices  65.1 us (42%)
  blocking collectives  25.8 us (17%)
  Pallas kernels  22.4 us (15%)
  waiting for transfers between devices  15.2 us (10%)
  local copies, waits for them, and re-layouts  12.3 us (8%)
  other arithmetic  9.66 us (6%)
  between operations  2.69 us (2%)
    all_to_all x1, blocking collectives, on_device(): lax.all_to_all(partial, AXES, split_axis=0, concat_axis=0, tiled=True)  25.8 us
    pallas_call x1, Pallas kernels, conv_call(): pl.pallas_call(conv_kernel, out_shape=(jax.ShapeDtypeStruct((2, 16, 4, 25...  15.1 us
    ppermute x4, starting transfers between devices, on_device(): lax.ppermute(parts[turn], AXES, return_pairs(turn))  14.5 us
    all_to_all x1, starting transfers between devices, on_device(): lax.all_to_all(payload, 'slab', split_axis=0, concat_axis=0, tiled=True)  14.4 us
    ppermute x4, starting transfers between devices, on_device(): lax.ppermute(state_rows, AXES, spread_pairs(turn))  12.8 us
    all_to_all x1, waiting for transfers between devices, on_device(): lax.all_to_all(sent, 'slab', split_axis=0, concat_axis=0, tiled=True)  9.85 us
    pallas_call x1, Pallas kernels, transform_call(): pl.pallas_call(transform_kernel, out_shape=tuple((jax.ShapeDtypeStruct((2...  7.27 us
    ppermute x3, starting transfers between devices, on_device(): lax.ppermute(small, 'coil', [(i, (i + turn) % 4) for i in range(4)])  5.83 us
  transfers between devices with their start and end apart: 17, of which 4 were waited for; matrix products, arithmetic and copies ran while one was open for 7% of the time, Pallas kernels for 10%

commit v1 on v0

--- a/solution.py
+++ b/solution.py
@@ -11,13 +11,18 @@
 F32 = jnp.float32
 
 
-def device(coil, quarter, low):
-    return (quarter * 16 + low) * 4 + coil
+def holder(coil, quarter, low):
+    z = (low // 4 - 1 + 2 * (coil % 2)) % 4 * 2 + quarter % 2
+    return (quarter // 2 * 32 + z * 4 + low % 4) * 4 + coil
+
+
+def reader(coil, group, low):
+    return (group * 16 + low) * 4 + coil
 
 
 def spread_pairs(turn):
     return [
-        (device(c, q, low), device((q + turn) % 4, c, low))
+        (holder(c, q, low), reader((q + turn) % 4, c, low))
         for c in range(4)
         for q in range(4)
         for low in range(16)
@@ -26,16 +31,17 @@
 
 def return_pairs(turn):
     return [
-        (device(c, b, low), device(b, (c + turn) % 4, low))
+        (reader(c, b, low), holder(b, (c + turn) % 4, low))
         for c in range(4)
         for b in range(4)
         for low in range(16)
     ]
 
 
-def rotated(pieces, start):
-    twice = jnp.concatenate([pieces, pieces], axis=0)
-    return lax.dynamic_slice_in_dim(twice, start, 4, axis=0)
+def turned_by_core(data, coil, axis, sign):
+    even = jnp.roll(data, sign, axis)
+    odd = jnp.roll(data, -sign, axis)
+    return jnp.where(coil % 2 == 0, even, odd)
 
 
 def split(value):
@@ -137,10 +143,13 @@
                 first = (r * 3 + d) * 8
                 acc[d, pl.ds(place + r, 1)] += product[first : first + 8][None]
 
-    for place, scale in ((0, edge[2]), (17, edge[3])):
+    def border(k, carry):
+        place = 17 * k
+        scale = jnp.where(k == 0, edge[2], edge[3])
         response, _, _ = forward(place, wide[...], xb)
         high, low = split(jnp.tanh(response) * (keep * scale))
         scatter(place, high, low)
+        return carry
 
     def step(r, carry):
         response, xh, xl = forward(r + 1, wide[...], xb)
@@ -159,6 +168,7 @@
         scatter(r + 1, high, low)
         return carry
 
+    lax.fori_loop(0, 2, border, 0)
     lax.fori_loop(0, 16, step, 0)
     total = (
         shifted(acc[0, 2:18].reshape(128, 256), -1)
@@ -370,8 +380,10 @@
     coil = lax.axis_index("coil")
     slab = lax.axis_index("slab")
     maps = sens.transpose(2, 3, 0, 1, 4).reshape(64, 16, 2, 128)
-    images = jnp.stack([init_image, recon_cotangent]).transpose(3, 2, 0, 1, 4)
-    payload = jnp.concatenate([maps, images.reshape(64, 4, 2, 128)], axis=1)
+    images = jnp.stack([init_image, recon_cotangent]).reshape(2, 2, 4, 4, 2, 2, 256)
+    images = images.transpose(4, 2, 5, 3, 0, 1, 6)
+    images = turned_by_core(images, coil, 1, -1).reshape(64, 4, 2, 128)
+    payload = jnp.concatenate([maps, images], axis=1)
     received = lax.all_to_all(payload, "slab", split_axis=0, concat_axis=0, tiled=True)
 
     before, after, lower, upper = halos(init_image, recon_cotangent, slab_count)
@@ -380,10 +392,10 @@
     base, sums = conv_call(
         edge, init_image, recon_cotangent, before, after, lower, upper, wide, turned
     )
-    partial = jnp.pad(-diagonal(sums).reshape(2592), (0, 224)).reshape(256, 11)
-    chunk = jnp.sum(
-        lax.all_to_all(partial, AXES, split_axis=0, concat_axis=0, tiled=True), axis=0
-    )
+    partial = jnp.pad(-diagonal(sums).reshape(2592), (0, 32)).reshape(64, 1, 41)
+    partial = jnp.broadcast_to(partial, (64, 4, 41)).reshape(256, 41)
+    chunk = lax.all_to_all(partial, AXES, split_axis=0, concat_axis=0, tiled=True)
+    chunk = jnp.sum(chunk, axis=0)
 
     state_rows = received[:, 16:18].reshape(256, 128)
     grad_rows = received[:, 18:20].reshape(256, 128)
@@ -395,23 +407,20 @@
         lax.ppermute(parts[turn], AXES, return_pairs(turn)) for turn in range(4)
     )
     product = jnp.sum(total * grad_rows)
-    rider = jnp.concatenate([chunk, -product[None], jnp.zeros((244,), F32)])
+    rider = jnp.concatenate([chunk, -product[None], jnp.zeros((214,), F32)])
     rider = jnp.broadcast_to(rider.reshape(1, 1, 2, 128), (64, 1, 2, 128))
     sent = jnp.concatenate([total.reshape(64, 2, 2, 128), rider], axis=1)
     arrived = lax.all_to_all(sent, "slab", split_axis=0, concat_axis=0, tiled=True)
-    combined = arrived[:, :2].reshape(4, 16, 2, 256).transpose(2, 1, 0, 3)
-    recon = base - step_sizes[0] * combined
-    riders = arrived[:, 2, 0, :12]
-    small = jnp.concatenate([riders[:, :11].reshape(704), jnp.sum(riders[:, 11])[None]])
-    small = jnp.pad(small, (0, 319)).reshape(8, 128)
-    others = [small] + [
-        lax.ppermute(small, "coil", [(i, (i + turn) % 4) for i in range(4)])
-        for turn in range(1, 4)
-    ]
-    reverse = jnp.stack([others[0], others[3], others[2], others[1]])
-    ordered = rotated(reverse, (4 - coil) % 4).reshape(4, 1024)
-    step_grads = jnp.sum(ordered[:, 704])[None]
-    grads = ordered[:, :704].reshape(4, 64, 11).transpose(1, 0, 2).reshape(2816)[:2592]
+    own = jnp.sum(arrived[:, 2, 0, 41])[None]
+    step_grads = own
+    for turn in range(1, 4):
+        step_grads = step_grads + lax.ppermute(
+            own, "coil", [(i, (i + turn) % 4) for i in range(4)]
+        )
+    combined = arrived[:, :2].reshape(2, 4, 2, 4, 2, 256)
+    combined = turned_by_core(combined, coil, 1, 1).transpose(4, 1, 3, 0, 2, 5)
+    recon = base - step_sizes[0] * combined.reshape(2, 16, 4, 256)
+    grads = arrived[:, 2, 0, :41].reshape(2624)[:2592]
     grads = grads.reshape(3, 3, 2, 3, 48).transpose(4, 2, 1, 3, 0)
     return recon, grads[None], step_grads
 

time: 154 us -> 156 us (1.013)
  blocking collectives: 25.8 us -> 22.1 us
  between operations: 2.69 us -> 6.37 us
  waiting for transfers between devices: 15.2 us -> 18.1 us
  other arithmetic: 9.66 us -> 6.97 us
  local copies, waits for them, and re-layouts: 12.3 us -> 14.2 us
    all_to_all x1, blocking collectives: 25.8 us -> 22.1 us  [on_device(): lax.all_to_all(partial, AXES, split_axis=0, concat_axis=0, tiled=True)]
    ppermute x4, starting transfers between devices: 12.8 us -> 16.1 us  [on_device(): lax.ppermute(state_rows, AXES, spread_pairs(turn))]
    ppermute x4, starting transfers between devices: 14.5 us -> 11.4 us  [on_device(): lax.ppermute(parts[turn], AXES, return_pairs(turn))]
    ppermute x4, waiting for transfers between devices: 4.29 us -> 7.31 us  [on_device(): lax.ppermute(state_rows, AXES, spread_pairs(turn))]
    unnamed x48 -> x39, local copies, waits for them, and re-layouts: 3.14 us -> 3.37 us
  transfers between devices with their start and end apart: 17 -> 17, of which waited for: 4 -> 5; matrix products, arithmetic and copies ran while one was open for 7% -> 9% of each run, Pallas kernels for 10% -> 10%
where the time goes in v1:
time: 156 us
  starting transfers between devices  65.1 us (42%)
  Pallas kernels  22.8 us (15%)
  blocking collectives  22.1 us (14%)
  waiting for transfers between devices  18.1 us (12%)
  local copies, waits for them, and re-layouts  14.2 us (9%)
  other arithmetic  6.97 us (4%)
  between operations  6.37 us (4%)
    all_to_all x1, blocking collectives, on_device(): lax.all_to_all(partial, AXES, split_axis=0, concat_axis=0, tiled=True)  22.1 us
    ppermute x4, starting transfers between devices, on_device(): lax.ppermute(state_rows, AXES, spread_pairs(turn))  16.1 us
    pallas_call x1, Pallas kernels, conv_call(): pl.pallas_call(conv_kernel, out_shape=(jax.ShapeDtypeStruct((2, 16, 4, 25...  15.5 us
    all_to_all x1, starting transfers between devices, on_device(): lax.all_to_all(payload, 'slab', split_axis=0, concat_axis=0, tiled=True)  14.4 us
    ppermute x4, starting transfers between devices, on_device(): lax.ppermute(parts[turn], AXES, return_pairs(turn))  11.4 us
    all_to_all x1, waiting for transfers between devices, on_device(): lax.all_to_all(sent, 'slab', split_axis=0, concat_axis=0, tiled=True)  9.87 us
    ppermute x4, waiting for transfers between devices, on_device(): lax.ppermute(state_rows, AXES, spread_pairs(turn))  7.31 us
    pallas_call x1, Pallas kernels, transform_call(): pl.pallas_call(transform_kernel, out_shape=tuple((jax.ShapeDtypeStruct((2...  7.28 us
  transfers between devices with their start and end apart: 17, of which 5 were waited for; matrix products, arithmetic and copies ran while one was open for 9% of the time, Pallas kernels for 10%

profile of v1, /device:TPU:1, one launch (start us, length us, event | category | flops | bytes accessed | tf_op | source)
XLA Modules:
  0.0 155.6 jit_solution(11468454172657901383)
XLA Ops:
  0.6 1.1 fusion.12
  2.8 4.0 %collective-permute-start = (f32[2,16,3,256]{3,1,2,0:T(8,128)S(1)}, f32[2,16,3,256]{3,1,2,0:T(8,128)S(1)}, u32[]{:S(2)}, u32[]{:S(2)}) collective-permute-start(f32[2,16,3,256]{3,1,2,0:T(8,128)S(1)} %pad_maximum_fusion.3), channel_id=1, source_target_pairs={{0,4},{4,8},{8,12},{12,16},{16,20},{20,24},{24,28},{28,32},{32,36}... | collective-permute-start | bytes 294920 | tf_op jit(solution)/shard_map/ppermute | solution.py:359
  6.9 1.3 collective-permute-start.1
  12.1 1.6 %copy.188 = f32[64,20,2,128]{3,2,1,0:T(2,128)} copy(f32[64,20,2,128]{3,2,0,1:T(2,128)S(1)} %pad_maximum_fusion) | data formatting | bytes 2621440 | tf_op jit(solution)/shard_map/concatenate | solution.py:386
  13.7 14.4 %all-to-all-start = ((f32[64,20,2,128]{3,2,1,0:T(2,128)}), f32[64,20,2,128]{3,2,1,0:T(2,128)S(1)}, u32[]{:S(2)}, u32[]{:S(2)}) async-start(f32[64,20,2,128]{3,2,1,0:T(2,128)} %copy.188), calls=%async_computation | async-start | bytes 2621440 | tf_op jit(solution)/shard_map/all_to_all | solution.py:387
  31.8 3.4 %collective-permute-start.3 = (f32[6,8,256]{2,1,0:T(8,128)S(1)}, f32[6,8,256]{2,1,0:T(8,128)S(1)}, u32[]{:S(2)}, u32[]{:S(2)}) collective-permute-start(f32[6,8,256]{2,1,0:T(8,128)S(1)} %pad_maximum_fusion.6), channel_id=1, source_target_pairs={{1,0},{2,1},{3,2},{5,4},{6,5},{7,6},{9,8},{10,9},{11,10},{13,12},{... | collective-permute-start | bytes 147464 | tf_op jit(solution)/shard_map/ppermute | solution.py:374
  35.3 4.3 %collective-permute-start.2 = (f32[6,8,256]{2,1,0:T(8,128)S(1)}, f32[6,8,256]{2,1,0:T(8,128)S(1)}, u32[]{:S(2)}, u32[]{:S(2)}) collective-permute-start(f32[6,8,256]{2,1,0:T(8,128)S(1)} %pad_maximum_fusion.5), channel_id=1, source_target_pairs={{0,1},{1,2},{2,3},{4,5},{5,6},{6,7},{8,9},{9,10},{10,11},{12,13},{... | collective-permute-start | bytes 147464 | tf_op jit(solution)/shard_map/ppermute | solution.py:373
  42.9 15.5 %shard_map.256 = (f32[2,16,4,256]{3,2,1,0:T(4,128)}, f32[144,192]{1,0:T(8,128)}) custom-call(f32[4]{0:T(128)} %add_convert_fusion.edge, f32[2,16,4,256]{3,2,1,0:T(4,128)} %init.1, f32[2,16,4,256]{3,2,1,0:T(4,128)} %grad.1, f32[2,16,3,256]{3,2,1,0:T(4,128)} %copy.183.before, f32[2,16,3,256]{3,2,1,0:T(4,128)} %copy.184.after, f32[6,8,256]{2,1,0:T(8,128)} %copy-done.16, ...), custom_call_target="tpu_custom_call" | custom-call | flops 6000000000 | bytes 2000000 | tf_op jit(solution)/shard_map/pallas_call | solution.py:184
  58.3 1.1 reshape.225
  59.7 5.9 %collective-permute-start.4 = (f32[256,128]{1,0:T(8,128)S(1)}, f32[256,128]{1,0:T(8,128)S(1)}, u32[]{:S(2)}, u32[]{:S(2)}) collective-permute-start(f32[256,128]{1,0:T(8,128)S(1)} %bitcast.97), channel_id=1, source_target_pairs={{96,0},{100,4},{104,8},{108,12},{0,16},{4,20},{8,24},{12,28},{32,3... | collective-permute-start | bytes 393224 | tf_op jit(solution)/shard_map/ppermute | solution.py:402
  65.6 1.9 %collective-permute-start.5 = (f32[256,128]{1,0:T(8,128)S(1)}, f32[256,128]{1,0:T(8,128)S(1)}, u32[]{:S(2)}, u32[]{:S(2)}) collective-permute-start(f32[256,128]{1,0:T(8,128)S(1)} %bitcast.98), channel_id=1, source_target_pairs={{96,1},{100,5},{104,9},{108,13},{0,17},{4,21},{8,25},{12,29},{32,3... | collective-permute-start | bytes 393224 | tf_op jit(solution)/shard_map/ppermute | solution.py:402
  67.5 6.4 %collective-permute-start.6 = (f32[256,128]{1,0:T(8,128)S(1)}, f32[256,128]{1,0:T(8,128)S(1)}, u32[]{:S(2)}, u32[]{:S(2)}) collective-permute-start(f32[256,128]{1,0:T(8,128)S(1)} %bitcast.99), channel_id=1, source_target_pairs={{96,2},{100,6},{104,10},{108,14},{0,18},{4,22},{8,26},{12,30},{32,... | collective-permute-start | bytes 393224 | tf_op jit(solution)/shard_map/ppermute | solution.py:402
  73.9 1.9 %collective-permute-start.7 = (f32[256,128]{1,0:T(8,128)S(1)}, f32[256,128]{1,0:T(8,128)S(1)}, u32[]{:S(2)}, u32[]{:S(2)}) collective-permute-start(f32[256,128]{1,0:T(8,128)S(1)} %bitcast.100), channel_id=1, source_target_pairs={{96,3},{100,7},{104,11},{108,15},{0,19},{4,23},{8,27},{12,31},{32,... | collective-permute-start | bytes 393224 | tf_op jit(solution)/shard_map/ppermute | solution.py:402
  75.9 3.7 %collective-permute-done.6.p2 = f32[256,128]{1,0:T(8,128)S(1)} collective-permute-done((f32[256,128]{1,0:T(8,128)S(1)}, f32[256,128]{1,0:T(8,128)S(1)}, u32[]{:S(2)}, u32[]{:S(2)}) %collective-permute-start.6) | collective-permute-done | bytes 131104 | tf_op jit(solution)/shard_map/ppermute | solution.py:402
  79.6 3.6 %collective-permute-done.7.p3 = f32[256,128]{1,0:T(8,128)S(1)} collective-permute-done((f32[256,128]{1,0:T(8,128)S(1)}, f32[256,128]{1,0:T(8,128)S(1)}, u32[]{:S(2)}, u32[]{:S(2)}) %collective-permute-start.7) | collective-permute-done | bytes 131104 | tf_op jit(solution)/shard_map/ppermute | solution.py:402
  83.9 7.3 %shard_map.257 = (f32[256,128]{1,0:T(8,128)}, f32[256,128]{1,0:T(8,128)}, f32[256,128]{1,0:T(8,128)}, f32[256,128]{1,0:T(8,128)}) custom-call(s32[1]{0:T(128)} %bitcast.23.coil, f32[2560,128]{1,0:T(8,128)} %bitcast.89, f32[256,128]{1,0:T(8,128)} %copy-done.11, f32[256,128]{1,0:T(8,128)} %copy-done.12, f32[256,128]{1,0:T(8,128)} %copy-done.13, ...), custom_call_target="tpu_custom_call" | custom-call | flops 6000000000 | bytes 5000000 | tf_op jit(solution)/shard_map/pallas_call | solution.py:336
  91.9 2.7 %collective-permute-start.11 = (f32[256,128]{1,0:T(8,128)}, f32[256,128]{1,0:T(8,128)S(1)}, u32[]{:S(2)}, u32[]{:S(2)}) collective-permute-start(f32[256,128]{1,0:T(8,128)} %get-tuple-element.13), channel_id=1, source_target_pairs={{0,240},{4,244},{8,248},{12,252},{16,144},{20,148},{24,152},{28,15... | collective-permute-start | bytes 393224 | tf_op jit(solution)/shard_map/ppermute | solution.py:407
  94.6 5.0 %collective-permute-start.8 = (f32[256,128]{1,0:T(8,128)}, f32[256,128]{1,0:T(8,128)S(1)}, u32[]{:S(2)}, u32[]{:S(2)}) collective-permute-start(f32[256,128]{1,0:T(8,128)} %get-tuple-element.10), channel_id=1, source_target_pairs={{0,96},{4,100},{8,104},{12,108},{16,0},{20,4},{24,8},{28,12},{32,3... | collective-permute-start | bytes 393224 | tf_op jit(solution)/shard_map/ppermute | solution.py:407
  99.7 2.9 %collective-permute-start.9 = (f32[256,128]{1,0:T(8,128)}, f32[256,128]{1,0:T(8,128)S(1)}, u32[]{:S(2)}, u32[]{:S(2)}) collective-permute-start(f32[256,128]{1,0:T(8,128)} %get-tuple-element.11), channel_id=1, source_target_pairs={{0,112},{4,116},{8,120},{12,124},{16,16},{20,20},{24,24},{28,28},{... | collective-permute-start | bytes 393224 | tf_op jit(solution)/shard_map/ppermute | solution.py:407
  102.9 22.1 %all_to_all.19 = f32[256,1,41]{2,1,0:T(1,128)S(1)} all-to-all(f32[256,1,41]{2,1,0:T(1,128)S(1)} %bitcast.91), channel_id=1, replica_groups=mesh['slab'=64,'coil'=4] {'slab','coil'}, dimensions={0} | all-to-all | bytes 83968 | tf_op jit(solution)/shard_map/all_to_all | solution.py:397
  127.5 4.8 %all-to-all-start.2 = ((f32[64,3,2,128]{3,2,1,0:T(2,128)}), f32[64,3,2,128]{3,2,1,0:T(2,128)S(1)}, u32[]{:S(2)}, u32[]{:S(2)}) async-start(f32[64,3,2,128]{3,2,1,0:T(2,128)} %pad_maximum_fusion.2), calls=%async_computation.2 | async-start | bytes 393216 | tf_op jit(solution)/shard_map/all_to_all | solution.py:413
  132.9 9.9 %all-to-all-done.2 = f32[64,3,2,128]{3,2,1,0:T(2,128)S(1)} async-done(((f32[64,3,2,128]{3,2,1,0:T(2,128)}), f32[64,3,2,128]{3,2,1,0:T(2,128)S(1)}, u32[]{:S(2)}, u32[]{:S(2)}) %all-to-all-start.2) | async-done | bytes 196640 | tf_op jit(solution)/shard_map/all_to_all | solution.py:413
  143.5 3.4 %collective-permute-start.12 = (f32[1]{0:T(128)}, f32[1]{0:T(128)}, u32[]{:S(2)}, u32[]{:S(2)}) collective-permute-start(f32[1]{0:T(128)} %bitcast.40), channel_id=1, source_target_pairs={{0,1},{1,2},{2,3},{3,0},{4,5},{5,6},{6,7},{7,4},{8,9},{9,10},{10,1... | collective-permute-start | bytes 20 | tf_op jit(solution)/shard_map/ppermute | solution.py:417
  146.9 2.1 %collective-permute-start.13 = (f32[1]{0:T(128)}, f32[1]{0:T(128)}, u32[]{:S(2)}, u32[]{:S(2)}) collective-permute-start(f32[1]{0:T(128)} %bitcast.40), channel_id=1, source_target_pairs={{0,2},{1,3},{2,0},{3,1},{4,6},{5,7},{6,4},{7,5},{8,10},{9,11},{10,... | collective-permute-start | bytes 20 | tf_op jit(solution)/shard_map/ppermute | solution.py:417
  (128 shorter events, 19.1 us)
Async XLA Ops:
  0.6 8.6 %copy-start.2 = (f32[2,16,4,256]{3,2,1,0:T(4,128)S(1)}, f32[2,16,4,256]{3,2,1,0:T(4,128)}, u32[]{:S(2)}) copy-start(f32[2,16,4,256]{3,2,1,0:T(4,128)} %grad.1) | copy-start | bytes 393220
  2.8 28.8 %collective-permute-start = (f32[2,16,3,256]{3,1,2,0:T(8,128)S(1)}, f32[2,16,3,256]{3,1,2,0:T(8,128)S(1)}, u32[]{:S(2)}, u32[]{:S(2)}) collective-permute-start(f32[2,16,3,256]{3,1,2,0:T(8,128)S(1)} %pad_maximum_fusion.3), channel_id=1, source_target_pairs={{0,4},{4,8},{8,12},{12,16},{16,20},{20,24},{24,28},{28,32},{32,36}... | collective-permute-start | bytes 294920 | tf_op jit(solution)/shard_map/ppermute | solution.py:359
  6.9 24.8 %collective-permute-start.1 = (f32[2,16,3,256]{3,1,2,0:T(8,128)S(1)}, f32[2,16,3,256]{3,1,2,0:T(8,128)S(1)}, u32[]{:S(2)}, u32[]{:S(2)}) collective-permute-start(f32[2,16,3,256]{3,1,2,0:T(8,128)S(1)} %pad_maximum_fusion.4), channel_id=1, source_target_pairs={{4,0},{8,4},{12,8},{16,12},{20,16},{24,20},{28,24},{32,28},{36,32}... | collective-permute-start | bytes 294920 | tf_op jit(solution)/shard_map/ppermute | solution.py:360
  13.6 14.4 %copy-start.4 = (f32[1,48,2,3,3,3]{1,2,5,4,3,0:T(2,128)S(1)}, f32[1,48,2,3,3,3]{1,2,5,4,3,0:T(2,128)}, u32[]{:S(2)}) copy-start(f32[1,48,2,3,3,3]{1,2,5,4,3,0:T(2,128)} %param.29) | copy-start | bytes 31108
  13.6 14.4 %copy-start.5 = (f32[6,8]{0,1:T(8,128)S(1)}, f32[6,8]{0,1:T(8,128)}, u32[]{:S(2)}) copy-start(f32[6,8]{0,1:T(8,128)} %constant.71.clone) | copy-start | bytes 580
  13.6 14.4 %copy-start.6 = (f32[6,8]{0,1:T(8,128)S(1)}, f32[6,8]{0,1:T(8,128)}, u32[]{:S(2)}) copy-start(f32[6,8]{0,1:T(8,128)} %constant.72.clone) | copy-start | bytes 580
  13.6 14.4 %copy-start.7 = (f32[6,8]{0,1:T(8,128)S(1)}, f32[6,8]{0,1:T(8,128)}, u32[]{:S(2)}) copy-start(f32[6,8]{0,1:T(8,128)} %constant.73.clone) | copy-start | bytes 580
  13.7 46.0 %all-to-all-start = ((f32[64,20,2,128]{3,2,1,0:T(2,128)}), f32[64,20,2,128]{3,2,1,0:T(2,128)S(1)}, u32[]{:S(2)}, u32[]{:S(2)}) async-start(f32[64,20,2,128]{3,2,1,0:T(2,128)} %copy.188), calls=%async_computation | async-start | bytes 2621440 | tf_op jit(solution)/shard_map/all_to_all | solution.py:387
  31.8 9.8 %collective-permute-start.3 = (f32[6,8,256]{2,1,0:T(8,128)S(1)}, f32[6,8,256]{2,1,0:T(8,128)S(1)}, u32[]{:S(2)}, u32[]{:S(2)}) collective-permute-start(f32[6,8,256]{2,1,0:T(8,128)S(1)} %pad_maximum_fusion.6), channel_id=1, source_target_pairs={{1,0},{2,1},{3,2},{5,4},{6,5},{7,6},{9,8},{10,9},{11,10},{13,12},{... | collective-permute-start | bytes 147464 | tf_op jit(solution)/shard_map/ppermute | solution.py:374
  35.3 6.4 %collective-permute-start.2 = (f32[6,8,256]{2,1,0:T(8,128)S(1)}, f32[6,8,256]{2,1,0:T(8,128)S(1)}, u32[]{:S(2)}, u32[]{:S(2)}) collective-permute-start(f32[6,8,256]{2,1,0:T(8,128)S(1)} %pad_maximum_fusion.5), channel_id=1, source_target_pairs={{0,1},{1,2},{2,3},{4,5},{5,6},{6,7},{8,9},{9,10},{10,11},{12,13},{... | collective-permute-start | bytes 147464 | tf_op jit(solution)/shard_map/ppermute | solution.py:373
  59.7 23.5 %copy-start = (f32[64,20,2,128]{3,2,1,0:T(2,128)}, f32[64,20,2,128]{3,2,1,0:T(2,128)S(1)}, u32[]{:S(2)}) copy-start(f32[64,20,2,128]{3,2,1,0:T(2,128)S(1)} %all-to-all-done) | copy-start | bytes 3932164
  59.7 16.1 %collective-permute-start.4 = (f32[256,128]{1,0:T(8,128)S(1)}, f32[256,128]{1,0:T(8,128)S(1)}, u32[]{:S(2)}, u32[]{:S(2)}) collective-permute-start(f32[256,128]{1,0:T(8,128)S(1)} %bitcast.97), channel_id=1, source_target_pairs={{96,0},{100,4},{104,8},{108,12},{0,16},{4,20},{8,24},{12,28},{32,3... | collective-permute-start | bytes 393224 | tf_op jit(solution)/shard_map/ppermute | solution.py:402
  65.6 10.3 %collective-permute-start.5 = (f32[256,128]{1,0:T(8,128)S(1)}, f32[256,128]{1,0:T(8,128)S(1)}, u32[]{:S(2)}, u32[]{:S(2)}) collective-permute-start(f32[256,128]{1,0:T(8,128)S(1)} %bitcast.98), channel_id=1, source_target_pairs={{96,1},{100,5},{104,9},{108,13},{0,17},{4,21},{8,25},{12,29},{32,3... | collective-permute-start | bytes 393224 | tf_op jit(solution)/shard_map/ppermute | solution.py:402
  67.5 12.1 %collective-permute-start.6 = (f32[256,128]{1,0:T(8,128)S(1)}, f32[256,128]{1,0:T(8,128)S(1)}, u32[]{:S(2)}, u32[]{:S(2)}) collective-permute-start(f32[256,128]{1,0:T(8,128)S(1)} %bitcast.99), channel_id=1, source_target_pairs={{96,2},{100,6},{104,10},{108,14},{0,18},{4,22},{8,26},{12,30},{32,... | collective-permute-start | bytes 393224 | tf_op jit(solution)/shard_map/ppermute | solution.py:402
  73.9 9.3 %collective-permute-start.7 = (f32[256,128]{1,0:T(8,128)S(1)}, f32[256,128]{1,0:T(8,128)S(1)}, u32[]{:S(2)}, u32[]{:S(2)}) collective-permute-start(f32[256,128]{1,0:T(8,128)S(1)} %bitcast.100), channel_id=1, source_target_pairs={{96,3},{100,7},{104,11},{108,15},{0,19},{4,23},{8,27},{12,31},{32,... | collective-permute-start | bytes 393224 | tf_op jit(solution)/shard_map/ppermute | solution.py:402
  91.1 34.2 %collective-permute-start.10 = (f32[256,128]{1,0:T(8,128)}, f32[256,128]{1,0:T(8,128)S(1)}, u32[]{:S(2)}, u32[]{:S(2)}) collective-permute-start(f32[256,128]{1,0:T(8,128)} %get-tuple-element.12), channel_id=1, source_target_pairs={{0,224},{4,228},{8,232},{12,236},{16,128},{20,132},{24,136},{28,14... | collective-permute-start | bytes 393224 | tf_op jit(solution)/shard_map/ppermute | solution.py:407
  91.9 33.4 %collective-permute-start.11 = (f32[256,128]{1,0:T(8,128)}, f32[256,128]{1,0:T(8,128)S(1)}, u32[]{:S(2)}, u32[]{:S(2)}) collective-permute-start(f32[256,128]{1,0:T(8,128)} %get-tuple-element.13), channel_id=1, source_target_pairs={{0,240},{4,244},{8,248},{12,252},{16,144},{20,148},{24,152},{28,15... | collective-permute-start | bytes 393224 | tf_op jit(solution)/shard_map/ppermute | solution.py:407
  94.6 30.7 %collective-permute-start.8 = (f32[256,128]{1,0:T(8,128)}, f32[256,128]{1,0:T(8,128)S(1)}, u32[]{:S(2)}, u32[]{:S(2)}) collective-permute-start(f32[256,128]{1,0:T(8,128)} %get-tuple-element.10), channel_id=1, source_target_pairs={{0,96},{4,100},{8,104},{12,108},{16,0},{20,4},{24,8},{28,12},{32,3... | collective-permute-start | bytes 393224 | tf_op jit(solution)/shard_map/ppermute | solution.py:407
  99.7 25.6 %collective-permute-start.9 = (f32[256,128]{1,0:T(8,128)}, f32[256,128]{1,0:T(8,128)S(1)}, u32[]{:S(2)}, u32[]{:S(2)}) collective-permute-start(f32[256,128]{1,0:T(8,128)} %get-tuple-element.11), channel_id=1, source_target_pairs={{0,112},{4,116},{8,120},{12,124},{16,16},{20,20},{24,24},{28,28},{... | collective-permute-start | bytes 393224 | tf_op jit(solution)/shard_map/ppermute | solution.py:407
  127.5 23.0 %copy-start.3 = (f32[2,16,4,256]{3,2,1,0:T(4,128)S(1)}, f32[2,16,4,256]{3,2,1,0:T(4,128)}, u32[]{:S(2)}) copy-start(f32[2,16,4,256]{3,2,1,0:T(4,128)} %get-tuple-element.9) | copy-start | bytes 393220
  127.5 15.3 %all-to-all-start.2 = ((f32[64,3,2,128]{3,2,1,0:T(2,128)}), f32[64,3,2,128]{3,2,1,0:T(2,128)S(1)}, u32[]{:S(2)}, u32[]{:S(2)}) async-start(f32[64,3,2,128]{3,2,1,0:T(2,128)} %pad_maximum_fusion.2), calls=%async_computation.2 | async-start | bytes 393216 | tf_op jit(solution)/shard_map/all_to_all | solution.py:413
  143.5 7.6 %collective-permute-start.12 = (f32[1]{0:T(128)}, f32[1]{0:T(128)}, u32[]{:S(2)}, u32[]{:S(2)}) collective-permute-start(f32[1]{0:T(128)} %bitcast.40), channel_id=1, source_target_pairs={{0,1},{1,2},{2,3},{3,0},{4,5},{5,6},{6,7},{7,4},{8,9},{9,10},{10,1... | collective-permute-start | bytes 20 | tf_op jit(solution)/shard_map/ppermute | solution.py:417
  146.9 5.4 %collective-permute-start.13 = (f32[1]{0:T(128)}, f32[1]{0:T(128)}, u32[]{:S(2)}, u32[]{:S(2)}) collective-permute-start(f32[1]{0:T(128)} %bitcast.40), channel_id=1, source_target_pairs={{0,2},{1,3},{2,0},{3,1},{4,6},{5,7},{6,4},{7,5},{8,10},{9,11},{10,... | collective-permute-start | bytes 20 | tf_op jit(solution)/shard_map/ppermute | solution.py:417
  148.9 4.8 %collective-permute-start.14 = (f32[1]{0:T(128)}, f32[1]{0:T(128)}, u32[]{:S(2)}, u32[]{:S(2)}) collective-permute-start(f32[1]{0:T(128)} %bitcast.40), channel_id=1, source_target_pairs={{0,3},{1,0},{2,1},{3,2},{4,7},{5,4},{6,5},{7,6},{8,11},{9,8},{10,9... | collective-permute-start | bytes 20 | tf_op jit(solution)/shard_map/ppermute | solution.py:417
  (10 other events, 25.2 us)

commit v2 on v1

--- a/solution.py
+++ b/solution.py
@@ -12,30 +12,30 @@
 
 
 def holder(coil, quarter, low):
-    z = (low // 4 - 1 + 2 * (coil % 2)) % 4 * 2 + quarter % 2
-    return (quarter // 2 * 32 + z * 4 + low % 4) * 4 + coil
+    z = (low // 4 * 2 - 2 + 4 * (coil % 2) + low % 2) % 8
+    y = low % 4 // 2 * 2 + quarter % 2
+    return (quarter // 2 * 32 + z * 4 + y) * 4 + coil
 
 
 def reader(coil, group, low):
     return (group * 16 + low) * 4 + coil
 
 
-def spread_pairs(turn):
+def far_pairs(turn):
     return [
-        (holder(c, q, low), reader((q + turn) % 4, c, low))
+        (holder(c, q, low), reader((q // 2 ^ turn) * 2 + q % 2, c, low))
         for c in range(4)
         for q in range(4)
         for low in range(16)
     ]
 
 
-def return_pairs(turn):
-    return [
-        (reader(c, b, low), holder(b, (c + turn) % 4, low))
-        for c in range(4)
-        for b in range(4)
-        for low in range(16)
-    ]
+def back_pairs(turn):
+    return [(to, at) for at, to in far_pairs(turn)]
+
+
+CORES = [(i, i ^ 1) for i in range(4)]
+GROUPS = [[x * 32 + e + 2 * k for k in range(16)] for x in range(2) for e in range(2)]
 
 
 def turned_by_core(data, coil, axis, sign):
@@ -212,7 +212,8 @@
 
 def tables():
     place = np.arange(256)
-    mixed = place % 64 * 4 + place // 64
+    mixed = (place // 128 * 32 + place // 64 % 2 + place % 16 * 2) * 4
+    mixed = mixed + place // 16 % 4
     made = []
     for first, second in ((place, place), (place, mixed), (mixed, place)):
         angle = (first[:, None] * second[None, :] % 256) * (2.0 * np.pi / 256)
@@ -225,17 +226,20 @@
 
 
 def transform_kernel(
-    coil, maps, p0, p1, p2, p3, kspace, mask, ch, cl, sh, sl, yh, yl, zh, zl,
-    uh, ul, wh, wl, o0, o1, o2, o3, rows, right, left, lhs, rhs,
+    coil, maps, p0, p1, p2, p3, kspace, mask, extra, ch, cl, sh, sl, yh, yl, zh, zl,
+    uh, ul, wh, wl, kept, sent, rows, right, left, lhs, rhs,
 ):
     here = coil[0]
     pieces = (p0, p1, p2, p3)
-    outs = (o0, o1, o2, o3)
+
+    def slot(a, q):
+        return (q // 2 ^ a // 2) + 2 * (q % 2 ^ a % 2)
+
     for a in range(4):
         @pl.when(here == a)
         def _():
             for q in range(4):
-                rows[q] = pieces[(a - q) % 4][...]
+                rows[q] = pieces[slot(a, q)][...]
     for part, cosine, sine in ((0, ch, sh), (1, cl, sl)):
         right[part, :256, :256] = cosine[...]
         right[part, :256, 256:] = -sine[...]
@@ -250,19 +254,25 @@
     def halves(load):
         return jnp.concatenate(
             [
-                jnp.concatenate([load(y, h) for h in range(2)], axis=1)
+                jnp.concatenate([load(q, y, h) for h in range(2)], axis=1)
+                for q in range(4)
                 for y in range(4)
             ],
             axis=0,
         )
 
     def map_of(part, c):
-        return halves(
-            lambda y, h: maps[pl.ds((y * 4 + part * 2 + c) * 2 + h, 64, stride=40), :]
-        )
-
-    def image_of(part):
-        return halves(lambda y, h: rows[y, pl.ds(part * 2 + h, 64, stride=4), :])
+        def load(q, y, h):
+            first = (q // 2 * 32 + q % 2) * 32 + (y * 4 + part * 2 + c) * 2 + h
+            return maps[pl.ds(first, 16, stride=64), :]
+
+        return halves(load)
+
+    def image_of(which, part):
+        def load(q, y, h):
+            return rows[q, pl.ds((which * 8 + part * 4 + y) * 2 + h, 16, stride=32), :]
+
+        return halves(load)
 
     def transform(pairs, side):
         for c in range(2):
@@ -294,7 +304,7 @@
             for c in range(2)
         ]
 
-    vr, vi = image_of(0), image_of(1)
+    vr, vi = image_of(0, 0), image_of(0, 1)
     pairs = []
     for c in range(2):
         sr, si = map_of(0, c), map_of(1, c)
@@ -318,28 +328,40 @@
         back_re = back_re + sr * xr + si * xi
         back_im = back_im + sr * xi - si * xr
     back = (back_re, back_im)
+    product = jnp.sum(
+        back_re * image_of(1, 0) + back_im * image_of(1, 1), axis=0, keepdims=True
+    )
+    product = product[:, :128] + product[:, 128:]
+    for out in (kept, sent):
+        for t in range(2):
+            out[t, 256:280] = extra[...]
+            out[t, 278:279] = -product
     for a in range(4):
         @pl.when(here == a)
         def _():
-            for j in range(4):
-                q = (a + j) % 4
+            for q in range(4):
+                place = slot(a, q)
+                out = sent if place >= 2 else kept
                 for part in range(2):
-                    for h in range(2):
-                        outs[j][pl.ds(part * 2 + h, 64, stride=4), :] = back[part][
-                            q * 64 : q * 64 + 64, h * 128 : h * 128 + 128
-                        ]
-
-
-def transform_call(coil, maps, pieces, kspace, mask):
+                    for y in range(4):
+                        for h in range(2):
+                            first = (part * 4 + y) * 2 + h
+                            out[place % 2, pl.ds(first, 16, stride=16), :] = back[part][
+                                q * 64 + y * 16 : q * 64 + y * 16 + 16,
+                                h * 128 : h * 128 + 128,
+                            ]
+
+
+def transform_call(coil, maps, pieces, kspace, mask, extra):
     vm = pl.BlockSpec(memory_space=pltpu.VMEM)
     consts = tables()
     return pl.pallas_call(
         transform_kernel,
-        out_shape=tuple(jax.ShapeDtypeStruct((256, 128), F32) for _ in range(4)),
-        in_specs=[pl.BlockSpec(memory_space=pltpu.SMEM)] + [vm] * 19,
-        out_specs=(vm,) * 4,
+        out_shape=tuple(jax.ShapeDtypeStruct((2, 280, 128), F32) for _ in range(2)),
+        in_specs=[pl.BlockSpec(memory_space=pltpu.SMEM)] + [vm] * 20,
+        out_specs=(vm,) * 2,
         scratch_shapes=[
-            pltpu.VMEM((4, 256, 128), F32),
+            pltpu.VMEM((4, 512, 128), F32),
             pltpu.VMEM((2, 512, 512), BF),
             pltpu.VMEM((4, 512, 512), BF),
             pltpu.VMEM((2, 512, 512), BF),
@@ -348,7 +370,7 @@
         cost_estimate=pl.CostEstimate(
             flops=6000000000, bytes_accessed=5000000, transcendentals=0
         ),
-    )(coil, maps, *pieces, kspace, mask, *[jnp.asarray(t) for t in consts])
+    )(coil, maps, *pieces, kspace, mask, extra, *[jnp.asarray(t) for t in consts])
 
 
 def halos(state, grad, slab_count):
@@ -379,12 +401,16 @@
     slab_count = lax.axis_size("slab")
     coil = lax.axis_index("coil")
     slab = lax.axis_index("slab")
-    maps = sens.transpose(2, 3, 0, 1, 4).reshape(64, 16, 2, 128)
-    images = jnp.stack([init_image, recon_cotangent]).reshape(2, 2, 4, 4, 2, 2, 256)
-    images = images.transpose(4, 2, 5, 3, 0, 1, 6)
-    images = turned_by_core(images, coil, 1, -1).reshape(64, 4, 2, 128)
-    payload = jnp.concatenate([maps, images], axis=1)
-    received = lax.all_to_all(payload, "slab", split_axis=0, concat_axis=0, tiled=True)
+    images = jnp.stack([init_image, recon_cotangent]).reshape(2, 2, 4, 2, 2, 4, 256)
+    images = images.transpose(2, 4, 3, 0, 1, 5, 6)
+    images = turned_by_core(images, coil, 0, -1).reshape(16, 32, 128)
+    images = lax.all_to_all(
+        images, "slab", split_axis=0, concat_axis=0, tiled=True,
+        axis_index_groups=GROUPS,
+    )
+    maps = sens.transpose(2, 3, 0, 1, 4).reshape(64, 32, 128)
+    maps, images = lax.optimization_barrier((maps, images))
+    received = lax.all_to_all(maps, "slab", split_axis=0, concat_axis=0, tiled=True)
 
     before, after, lower, upper = halos(init_image, recon_cotangent, slab_count)
     wide, turned = filter_tables(weights)
@@ -392,35 +418,36 @@
     base, sums = conv_call(
         edge, init_image, recon_cotangent, before, after, lower, upper, wide, turned
     )
-    partial = jnp.pad(-diagonal(sums).reshape(2592), (0, 32)).reshape(64, 1, 41)
-    partial = jnp.broadcast_to(partial, (64, 4, 41)).reshape(256, 41)
-    chunk = lax.all_to_all(partial, AXES, split_axis=0, concat_axis=0, tiled=True)
-    chunk = jnp.sum(chunk, axis=0)
-
-    state_rows = received[:, 16:18].reshape(256, 128)
-    grad_rows = received[:, 18:20].reshape(256, 128)
-    pieces = [lax.ppermute(state_rows, AXES, spread_pairs(turn)) for turn in range(4)]
-    parts = transform_call(
-        coil.reshape(1), received.reshape(2560, 128), pieces, kspace[:, :, 0], mask
-    )
-    total = sum(
-        lax.ppermute(parts[turn], AXES, return_pairs(turn)) for turn in range(4)
-    )
-    product = jnp.sum(total * grad_rows)
-    rider = jnp.concatenate([chunk, -product[None], jnp.zeros((214,), F32)])
-    rider = jnp.broadcast_to(rider.reshape(1, 1, 2, 128), (64, 1, 2, 128))
-    sent = jnp.concatenate([total.reshape(64, 2, 2, 128), rider], axis=1)
-    arrived = lax.all_to_all(sent, "slab", split_axis=0, concat_axis=0, tiled=True)
-    own = jnp.sum(arrived[:, 2, 0, 41])[None]
-    step_grads = own
+    extra = jnp.pad(-diagonal(sums).reshape(2592), (0, 480)).reshape(24, 128)
+
+    held = images.reshape(512, 128)
+    pieces = [lax.ppermute(held, AXES, far_pairs(turn)) for turn in range(2)]
+    pieces = pieces + [lax.ppermute(piece, "coil", CORES) for piece in pieces]
+    kept, sent = transform_call(
+        coil.reshape(1), received.reshape(2048, 128), pieces, kspace[:, :, 0], mask,
+        extra,
+    )
+    kept = kept + lax.ppermute(sent, "coil", CORES)
+    total = lax.ppermute(kept[0], AXES, back_pairs(0)) + lax.ppermute(
+        kept[1], AXES, back_pairs(1)
+    )
+    rider = jnp.broadcast_to(total[None, 256:], (16, 24, 128))
+    sent = jnp.concatenate([total[:256].reshape(16, 16, 128), rider], axis=1)
+    arrived = lax.all_to_all(
+        sent, "slab", split_axis=0, concat_axis=0, tiled=True,
+        axis_index_groups=GROUPS,
+    )
+    own = jnp.sum(arrived[:, 16:], axis=0)
+    riders = own
     for turn in range(1, 4):
-        step_grads = step_grads + lax.ppermute(
+        riders = riders + lax.ppermute(
             own, "coil", [(i, (i + turn) % 4) for i in range(4)]
         )
-    combined = arrived[:, :2].reshape(2, 4, 2, 4, 2, 256)
-    combined = turned_by_core(combined, coil, 1, 1).transpose(4, 1, 3, 0, 2, 5)
+    combined = arrived[:, :16].reshape(4, 2, 2, 2, 4, 256)
+    combined = turned_by_core(combined, coil, 0, 1).transpose(3, 0, 2, 1, 4, 5)
     recon = base - step_sizes[0] * combined.reshape(2, 16, 4, 256)
-    grads = arrived[:, 2, 0, :41].reshape(2624)[:2592]
+    step_grads = jnp.sum(riders[22])[None]
+    grads = riders[:21].reshape(2688)[:2592]
     grads = grads.reshape(3, 3, 2, 3, 48).transpose(4, 2, 1, 3, 0)
     return recon, grads[None], step_grads
 

time: 156 us -> 150 us (0.962)
  blocking collectives: 22.1 us -> 0 us
  waiting for transfers between devices: 18.1 us -> 36.5 us
  between operations: 6.37 us -> 1.95 us
  Pallas kernels: 22.8 us -> 24.4 us
    all_to_all x1 -> x0, blocking collectives: 22.1 us -> none  [on_device(): lax.all_to_all(partial, AXES, split_axis=0, concat_axis=0, tiled=True)]
    ppermute x8 -> x7, starting transfers between devices: 27.5 us -> 17.9 us  [the longest x1 7.84 us: on_device(): lax.ppermute(kept[1], AXES, back_pairs(1))]
    ppermute x8 -> x7, waiting for transfers between devices: 7.32 us -> 16.5 us  [the longest x2 9.15 us: on_device(): pieces = [lax.ppermute(held, AXES, far_pairs(turn)) for turn in range(2)]]
    all_to_all x2 -> x3, starting transfers between devices: 19.1 us -> 26.9 us  [the longest x1 12.4 us: on_device(): lax.all_to_all(images, 'slab', split_axis=0, concat_axis=0, tiled=True, a...]
    all_to_all x2 -> x3, waiting for transfers between devices: 9.96 us -> 16.6 us  [the longest x1 12.9 us: on_device(): lax.all_to_all(sent, 'slab', split_axis=0, concat_axis=0, tiled=True, axi...]
    ppermute x1, waiting for transfers between devices: 0.01 us -> 3.38 us  [halos(): upper = lax.ppermute(planes(slice(0, 2), 0), 'coil', down)]
    ppermute x1, starting transfers between devices: 4.26 us -> 6.32 us  [halos(): lower = lax.ppermute(planes(slice(14, 16), 15), 'coil', up)]
    unnamed x39 -> x41, local copies, waits for them, and re-layouts: 3.37 us -> 5.4 us
  transfers between devices with their start and end apart: 17 -> 17, of which waited for: 5 -> 8; matrix products, arithmetic and copies ran while one was open for 9% -> 8% of each run, Pallas kernels for 10% -> 10%
where the time goes in v2:
time: 150 us
  starting transfers between devices  65.7 us (44%)
  waiting for transfers between devices  36.5 us (24%)
  Pallas kernels  24.4 us (16%)
  local copies, waits for them, and re-layouts  14.4 us (10%)
  other arithmetic  6.8 us (5%)
  between operations  1.95 us (1%)
    pallas_call x1, Pallas kernels, conv_call(): pl.pallas_call(conv_kernel, out_shape=(jax.ShapeDtypeStruct((2, 16, 4, 25...  15.6 us
    all_to_all x1, waiting for transfers between devices, on_device(): lax.all_to_all(sent, 'slab', split_axis=0, concat_axis=0, tiled=True, axi...  12.9 us
    all_to_all x1, starting transfers between devices, on_device(): lax.all_to_all(images, 'slab', split_axis=0, concat_axis=0, tiled=True, a...  12.4 us
    ppermute x2, waiting for transfers between devices, on_device(): pieces = [lax.ppermute(held, AXES, far_pairs(turn)) for turn in range(2)]  9.15 us
    pallas_call x1, Pallas kernels, transform_call(): pl.pallas_call(transform_kernel, out_shape=tuple((jax.ShapeDtypeStruct((2...  8.79 us
    ppermute x1, starting transfers between devices, on_device(): lax.ppermute(kept[1], AXES, back_pairs(1))  7.84 us
    ppermute x3, starting transfers between devices, on_device(): lax.ppermute(own, 'coil', [(i, (i + turn) % 4) for i in range(4)])  7.39 us
    all_to_all x1, starting transfers between devices, on_device(): lax.all_to_all(sent, 'slab', split_axis=0, concat_axis=0, tiled=True, axi...  7.29 us
  transfers between devices with their start and end apart: 17, of which 8 were waited for; matrix products, arithmetic and copies ran while one was open for 8% of the time, Pallas kernels for 10%

profile of v2, /device:TPU:1, one launch (start us, length us, event | category | flops | bytes accessed | tf_op | source)
XLA Modules:
  0.0 149.7 jit_solution(15722951854806724891)
XLA Ops:
  1.8 4.0 %collective-permute-start = (f32[2,16,3,256]{3,1,2,0:T(8,128)S(1)}, f32[2,16,3,256]{3,1,2,0:T(8,128)S(1)}, u32[]{:S(2)}, u32[]{:S(2)}) collective-permute-start(f32[2,16,3,256]{3,1,2,0:T(8,128)S(1)} %pad_maximum_fusion.2), channel_id=1, source_target_pairs={{0,4},{4,8},{8,12},{12,16},{16,20},{20,24},{24,28},{28,32},{32,36}... | collective-permute-start | bytes 294920 | tf_op jit(solution)/shard_map/ppermute | solution.py:381
  6.5 1.3 collective-permute-start.1
  9.0 12.4 %all-to-all-start = ((f32[16,32,128]{2,1,0:T(8,128)}), f32[16,32,128]{2,1,0:T(8,128)S(1)}, u32[]{:S(2)}, u32[]{:S(2)}) async-start(f32[16,32,128]{2,1,0:T(8,128)} %select_n.33), calls=%async_computation | async-start | bytes 524288 | tf_op jit(solution)/shard_map/all_to_all | solution.py:407
  25.5 1.9 %reshape.216 = f32[64,32,128]{2,1,0:T(8,128)} reshape(f32[64,4,2,2,256]{4,3,2,1,0:T(2,128)S(1)} %copy.136) | data formatting | bytes 2097152 | tf_op jit(solution)/shard_map/reshape | solution.py:411
  29.2 3.7 %all-to-all-done = f32[16,32,128]{2,1,0:T(8,128)S(1)} async-done(((f32[16,32,128]{2,1,0:T(8,128)}), f32[16,32,128]{2,1,0:T(8,128)S(1)}, u32[]{:S(2)}, u32[]{:S(2)}) %all-to-all-start) | async-done | bytes 262176 | tf_op jit(solution)/shard_map/all_to_all | solution.py:407
  32.9 7.2 %all-to-all-start.1 = ((f32[64,32,128]{2,1,0:T(8,128)}), f32[64,32,128]{2,1,0:T(8,128)S(1)}, u32[]{:S(2)}, u32[]{:S(2)}) async-start(f32[64,32,128]{2,1,0:T(8,128)} %reshape.216), calls=%async_computation.1 | async-start | bytes 2097152 | tf_op jit(solution)/shard_map/all_to_all | solution.py:413
  40.1 6.3 %collective-permute-start.2 = (f32[6,8,256]{2,1,0:T(8,128)S(1)}, f32[6,8,256]{2,1,0:T(8,128)S(1)}, u32[]{:S(2)}, u32[]{:S(2)}) collective-permute-start(f32[6,8,256]{2,1,0:T(8,128)S(1)} %pad_maximum_fusion.4), channel_id=1, source_target_pairs={{0,1},{1,2},{2,3},{4,5},{5,6},{6,7},{8,9},{9,10},{10,11},{12,13},{... | collective-permute-start | bytes 147464 | tf_op jit(solution)/shard_map/ppermute | solution.py:395
  46.5 1.9 %collective-permute-start.3 = (f32[6,8,256]{2,1,0:T(8,128)S(1)}, f32[6,8,256]{2,1,0:T(8,128)S(1)}, u32[]{:S(2)}, u32[]{:S(2)}) collective-permute-start(f32[6,8,256]{2,1,0:T(8,128)S(1)} %pad_maximum_fusion.5), channel_id=1, source_target_pairs={{1,0},{2,1},{3,2},{5,4},{6,5},{7,6},{9,8},{10,9},{11,10},{13,12},{... | collective-permute-start | bytes 147464 | tf_op jit(solution)/shard_map/ppermute | solution.py:396
  50.5 3.4 %collective-permute-done.3.upper = f32[6,8,256]{2,1,0:T(8,128)S(1)} collective-permute-done((f32[6,8,256]{2,1,0:T(8,128)S(1)}, f32[6,8,256]{2,1,0:T(8,128)S(1)}, u32[]{:S(2)}, u32[]{:S(2)}) %collective-permute-start.3) | collective-permute-done | bytes 49184 | tf_op jit(solution)/shard_map/ppermute | solution.py:396
  54.5 15.6 %shard_map.256 = (f32[2,16,4,256]{3,2,1,0:T(4,128)}, f32[144,192]{1,0:T(8,128)}) custom-call(f32[4]{0:T(128)} %add_convert_fusion.edge, f32[2,16,4,256]{3,2,1,0:T(4,128)} %init.1, f32[2,16,4,256]{3,2,1,0:T(4,128)} %grad.1, f32[2,16,3,256]{3,2,1,0:T(4,128)} %copy.134.before, f32[2,16,3,256]{3,2,1,0:T(4,128)} %copy.135.after, f32[6,8,256]{2,1,0:T(8,128)} %copy-done.16, ...), custom_call_target="tpu_custom_call" | custom-call | flops 6000000000 | bytes 2000000 | tf_op jit(solution)/shard_map/pallas_call | solution.py:184
  71.3 1.9 %collective-permute-start.4 = (f32[512,128]{1,0:T(8,128)S(1)}, f32[512,128]{1,0:T(8,128)S(1)}, u32[]{:S(2)}, u32[]{:S(2)}) collective-permute-start(f32[512,128]{1,0:T(8,128)S(1)} %bitcast.95), channel_id=1, source_target_pairs={{96,0},{112,4},{104,8},{120,12},{0,16},{16,20},{8,24},{24,28},{32,... | collective-permute-start | bytes 786440 | tf_op jit(solution)/shard_map/ppermute | solution.py:424
  73.2 2.8 %collective-permute-start.5 = (f32[512,128]{1,0:T(8,128)S(1)}, f32[512,128]{1,0:T(8,128)S(1)}, u32[]{:S(2)}, u32[]{:S(2)}) collective-permute-start(f32[512,128]{1,0:T(8,128)S(1)} %bitcast.96), channel_id=1, source_target_pairs={{96,2},{112,6},{104,10},{120,14},{0,18},{16,22},{8,26},{24,30},{32... | collective-permute-start | bytes 786440 | tf_op jit(solution)/shard_map/ppermute | solution.py:424
  76.0 7.6 %collective-permute-done.4.p0 = f32[512,128]{1,0:T(8,128)S(1)} collective-permute-done((f32[512,128]{1,0:T(8,128)S(1)}, f32[512,128]{1,0:T(8,128)S(1)}, u32[]{:S(2)}, u32[]{:S(2)}) %collective-permute-start.4) | collective-permute-done | bytes 262176 | tf_op jit(solution)/shard_map/ppermute | solution.py:424
  83.6 1.5 %collective-permute-done.5.p1 = f32[512,128]{1,0:T(8,128)S(1)} collective-permute-done((f32[512,128]{1,0:T(8,128)S(1)}, f32[512,128]{1,0:T(8,128)S(1)}, u32[]{:S(2)}, u32[]{:S(2)}) %collective-permute-start.5) | collective-permute-done | bytes 262176 | tf_op jit(solution)/shard_map/ppermute | solution.py:424
  87.8 8.8 %shard_map.257 = (f32[2,280,128]{2,1,0:T(8,128)}, f32[2,280,128]{2,1,0:T(8,128)}) custom-call(s32[1]{0:T(128)} %bitcast.23.coil, f32[2048,128]{1,0:T(8,128)} %bitcast.90, f32[512,128]{1,0:T(8,128)} %copy-done.12, f32[512,128]{1,0:T(8,128)} %copy-done.13, f32[512,128]{1,0:T(8,128)} %copy-done.14, f32[512,128]{1,0:T(8,128)} %copy-done.15, ...), custom_call_target="tpu_custom_call" | custom-call | flops 6000000000 | bytes 5000000 | tf_op jit(solution)/shard_map/pallas_call | solution.py:358
  96.7 1.6 %collective-permute-done.8 = f32[2,280,128]{2,1,0:T(8,128)S(1)} collective-permute-done((f32[2,280,128]{2,1,0:T(8,128)}, f32[2,280,128]{2,1,0:T(8,128)S(1)}, u32[]{:S(2)}, u32[]{:S(2)}) %collective-permute-start.8) | collective-permute-done | bytes 286752 | tf_op jit(solution)/shard_map/ppermute | solution.py:430
  99.4 5.2 %collective-permute-start.9 = (f32[280,128]{1,0:T(8,128)S(1)}, f32[280,128]{1,0:T(8,128)S(1)}, u32[]{:S(2)}, u32[]{:S(2)}) collective-permute-start(f32[280,128]{1,0:T(8,128)S(1)} %get-tuple-element.43), channel_id=1, source_target_pairs={{0,96},{4,112},{8,104},{12,120},{16,0},{20,16},{24,8},{28,24},{32,... | collective-permute-start | bytes 430088 | tf_op jit(solution)/shard_map/ppermute | solution.py:431
  104.6 7.8 %collective-permute-start.10 = (f32[280,128]{1,0:T(8,128)S(1)}, f32[280,128]{1,0:T(8,128)S(1)}, u32[]{:S(2)}, u32[]{:S(2)}) collective-permute-start(f32[280,128]{1,0:T(8,128)S(1)} %get-tuple-element.42), channel_id=1, source_target_pairs={{2,96},{6,112},{10,104},{14,120},{18,0},{22,16},{26,8},{30,24},{34... | collective-permute-start | bytes 430088 | tf_op jit(solution)/shard_map/ppermute | solution.py:431
  112.5 4.9 %collective-permute-done.10 = f32[280,128]{1,0:T(8,128)S(1)} collective-permute-done((f32[280,128]{1,0:T(8,128)S(1)}, f32[280,128]{1,0:T(8,128)S(1)}, u32[]{:S(2)}, u32[]{:S(2)}) %collective-permute-start.10) | collective-permute-done | bytes 143392 | tf_op jit(solution)/shard_map/ppermute | solution.py:431
  118.2 7.3 %all-to-all-start.2 = ((f32[16,40,128]{2,1,0:T(8,128)}), f32[16,40,128]{2,1,0:T(8,128)S(1)}, u32[]{:S(2)}, u32[]{:S(2)}) async-start(f32[16,40,128]{2,1,0:T(8,128)} %pad_maximum_fusion), calls=%async_computation.2 | async-start | bytes 655360 | tf_op jit(solution)/shard_map/all_to_all | solution.py:436
  126.2 12.9 %all-to-all-done.2 = f32[16,40,128]{2,1,0:T(8,128)S(1)} async-done(((f32[16,40,128]{2,1,0:T(8,128)}), f32[16,40,128]{2,1,0:T(8,128)S(1)}, u32[]{:S(2)}, u32[]{:S(2)}) %all-to-all-start.2) | async-done | bytes 327712 | tf_op jit(solution)/shard_map/all_to_all | solution.py:436
  139.1 2.2 %collective-permute-start.13 = (f32[24,128]{1,0:T(8,128)S(1)}, f32[24,128]{1,0:T(8,128)S(1)}, u32[]{:S(2)}, u32[]{:S(2)}) collective-permute-start(f32[24,128]{1,0:T(8,128)S(1)} %slice_reduce_fusion), channel_id=1, source_target_pairs={{0,3},{1,0},{2,1},{3,2},{4,7},{5,4},{6,5},{7,6},{8,11},{9,8},{10,9... | collective-permute-start | bytes 36872 | tf_op jit(solution)/shard_map/ppermute | solution.py:443
  141.3 1.7 %collective-permute-start.12 = (f32[24,128]{1,0:T(8,128)S(1)}, f32[24,128]{1,0:T(8,128)S(1)}, u32[]{:S(2)}, u32[]{:S(2)}) collective-permute-start(f32[24,128]{1,0:T(8,128)S(1)} %slice_reduce_fusion), channel_id=1, source_target_pairs={{0,2},{1,3},{2,0},{3,1},{4,6},{5,7},{6,4},{7,5},{8,10},{9,11},{10,... | collective-permute-start | bytes 36872 | tf_op jit(solution)/shard_map/ppermute | solution.py:443
  143.0 3.4 %collective-permute-start.11 = (f32[24,128]{1,0:T(8,128)S(1)}, f32[24,128]{1,0:T(8,128)S(1)}, u32[]{:S(2)}, u32[]{:S(2)}) collective-permute-start(f32[24,128]{1,0:T(8,128)S(1)} %slice_reduce_fusion), channel_id=1, source_target_pairs={{0,1},{1,2},{2,3},{3,0},{4,5},{5,6},{6,7},{7,4},{8,9},{9,10},{10,1... | collective-permute-start | bytes 36872 | tf_op jit(solution)/shard_map/ppermute | solution.py:443
  (124 shorter events, 20.3 us)
Async XLA Ops:
  0.6 1.1 copy-start.2
  1.8 27.2 %collective-permute-start = (f32[2,16,3,256]{3,1,2,0:T(8,128)S(1)}, f32[2,16,3,256]{3,1,2,0:T(8,128)S(1)}, u32[]{:S(2)}, u32[]{:S(2)}) collective-permute-start(f32[2,16,3,256]{3,1,2,0:T(8,128)S(1)} %pad_maximum_fusion.2), channel_id=1, source_target_pairs={{0,4},{4,8},{8,12},{12,16},{16,20},{20,24},{24,28},{28,32},{32,36}... | collective-permute-start | bytes 294920 | tf_op jit(solution)/shard_map/ppermute | solution.py:381
  5.9 2.0 %copy-start.3 = (f32[2,16,4,256]{3,2,1,0:T(4,128)S(1)}, f32[2,16,4,256]{3,2,1,0:T(4,128)}, u32[]{:S(2)}) copy-start(f32[2,16,4,256]{3,2,1,0:T(4,128)} %grad.1) | copy-start | bytes 393220
  6.5 22.5 %collective-permute-start.1 = (f32[2,16,3,256]{3,1,2,0:T(8,128)}, f32[2,16,3,256]{3,1,2,0:T(8,128)S(1)}, u32[]{:S(2)}, u32[]{:S(2)}) collective-permute-start(f32[2,16,3,256]{3,1,2,0:T(8,128)} %pad_maximum_fusion.3), channel_id=1, source_target_pairs={{4,0},{8,4},{12,8},{16,12},{20,16},{24,20},{28,24},{32,28},{36,32}... | collective-permute-start | bytes 294920 | tf_op jit(solution)/shard_map/ppermute | solution.py:382
  9.0 24.0 %all-to-all-start = ((f32[16,32,128]{2,1,0:T(8,128)}), f32[16,32,128]{2,1,0:T(8,128)S(1)}, u32[]{:S(2)}, u32[]{:S(2)}) async-start(f32[16,32,128]{2,1,0:T(8,128)} %select_n.33), calls=%async_computation | async-start | bytes 524288 | tf_op jit(solution)/shard_map/all_to_all | solution.py:407
  23.4 1.2 copy-start
  32.9 53.8 %all-to-all-start.1 = ((f32[64,32,128]{2,1,0:T(8,128)}), f32[64,32,128]{2,1,0:T(8,128)S(1)}, u32[]{:S(2)}, u32[]{:S(2)}) async-start(f32[64,32,128]{2,1,0:T(8,128)} %reshape.216), calls=%async_computation.1 | async-start | bytes 2097152 | tf_op jit(solution)/shard_map/all_to_all | solution.py:413
  40.1 10.4 %collective-permute-start.2 = (f32[6,8,256]{2,1,0:T(8,128)S(1)}, f32[6,8,256]{2,1,0:T(8,128)S(1)}, u32[]{:S(2)}, u32[]{:S(2)}) collective-permute-start(f32[6,8,256]{2,1,0:T(8,128)S(1)} %pad_maximum_fusion.4), channel_id=1, source_target_pairs={{0,1},{1,2},{2,3},{4,5},{5,6},{6,7},{8,9},{9,10},{10,11},{12,13},{... | collective-permute-start | bytes 147464 | tf_op jit(solution)/shard_map/ppermute | solution.py:395
  46.5 7.4 %collective-permute-start.3 = (f32[6,8,256]{2,1,0:T(8,128)S(1)}, f32[6,8,256]{2,1,0:T(8,128)S(1)}, u32[]{:S(2)}, u32[]{:S(2)}) collective-permute-start(f32[6,8,256]{2,1,0:T(8,128)S(1)} %pad_maximum_fusion.5), channel_id=1, source_target_pairs={{1,0},{2,1},{3,2},{5,4},{6,5},{7,6},{9,8},{10,9},{11,10},{13,12},{... | collective-permute-start | bytes 147464 | tf_op jit(solution)/shard_map/ppermute | solution.py:396
  50.5 3.4 %copy-start.16 = (f32[6,8,256]{2,1,0:T(8,128)}, f32[6,8,256]{2,1,0:T(8,128)S(1)}, u32[]{:S(2)}) copy-start(f32[6,8,256]{2,1,0:T(8,128)S(1)} %collective-permute-done.2.lower) | copy-start | bytes 147460
  71.3 12.3 %collective-permute-start.4 = (f32[512,128]{1,0:T(8,128)S(1)}, f32[512,128]{1,0:T(8,128)S(1)}, u32[]{:S(2)}, u32[]{:S(2)}) collective-permute-start(f32[512,128]{1,0:T(8,128)S(1)} %bitcast.95), channel_id=1, source_target_pairs={{96,0},{112,4},{104,8},{120,12},{0,16},{16,20},{8,24},{24,28},{32,... | collective-permute-start | bytes 786440 | tf_op jit(solution)/shard_map/ppermute | solution.py:424
  73.2 12.0 %collective-permute-start.5 = (f32[512,128]{1,0:T(8,128)S(1)}, f32[512,128]{1,0:T(8,128)S(1)}, u32[]{:S(2)}, u32[]{:S(2)}) collective-permute-start(f32[512,128]{1,0:T(8,128)S(1)} %bitcast.96), channel_id=1, source_target_pairs={{96,2},{112,6},{104,10},{120,14},{0,18},{16,22},{8,26},{24,30},{32... | collective-permute-start | bytes 786440 | tf_op jit(solution)/shard_map/ppermute | solution.py:424
  83.6 3.1 %copy-start.12 = (f32[512,128]{1,0:T(8,128)}, f32[512,128]{1,0:T(8,128)S(1)}, u32[]{:S(2)}) copy-start(f32[512,128]{1,0:T(8,128)S(1)} %collective-permute-done.4.p0) | copy-start | bytes 786436
  83.6 2.3 %collective-permute-start.6 = (f32[512,128]{1,0:T(8,128)S(1)}, f32[512,128]{1,0:T(8,128)S(1)}, u32[]{:S(2)}, u32[]{:S(2)}) collective-permute-start(f32[512,128]{1,0:T(8,128)S(1)} %collective-permute-done.4.p0), channel_id=1, source_target_pairs={{0,1},{1,0},{2,3},{3,2},{4,5},{5,4},{6,7},{7,6},{8,9},{9,8},{10,11... | collective-permute-start | bytes 786440 | tf_op jit(solution)/shard_map/ppermute | solution.py:425
  85.2 1.6 %copy-start.13 = (f32[512,128]{1,0:T(8,128)}, f32[512,128]{1,0:T(8,128)S(1)}, u32[]{:S(2)}) copy-start(f32[512,128]{1,0:T(8,128)S(1)} %collective-permute-done.5.p1) | copy-start | bytes 786436
  85.2 1.5 %collective-permute-start.7 = (f32[512,128]{1,0:T(8,128)S(1)}, f32[512,128]{1,0:T(8,128)S(1)}, u32[]{:S(2)}, u32[]{:S(2)}) collective-permute-start(f32[512,128]{1,0:T(8,128)S(1)} %collective-permute-done.5.p1), channel_id=1, source_target_pairs={{0,1},{1,0},{2,3},{3,2},{4,5},{5,4},{6,7},{7,6},{8,9},{9,8},{10,11... | collective-permute-start | bytes 786440 | tf_op jit(solution)/shard_map/ppermute | solution.py:425
  86.7 1.1 copy-start.1
  96.6 1.8 %collective-permute-start.8 = (f32[2,280,128]{2,1,0:T(8,128)}, f32[2,280,128]{2,1,0:T(8,128)S(1)}, u32[]{:S(2)}, u32[]{:S(2)}) collective-permute-start(f32[2,280,128]{2,1,0:T(8,128)} %get-tuple-element.14), channel_id=1, source_target_pairs={{0,1},{1,0},{2,3},{3,2},{4,5},{5,4},{6,7},{7,6},{8,9},{9,8},{10,11... | collective-permute-start | bytes 860168 | tf_op jit(solution)/shard_map/ppermute | solution.py:430
  99.4 13.1 %collective-permute-start.9 = (f32[280,128]{1,0:T(8,128)S(1)}, f32[280,128]{1,0:T(8,128)S(1)}, u32[]{:S(2)}, u32[]{:S(2)}) collective-permute-start(f32[280,128]{1,0:T(8,128)S(1)} %get-tuple-element.43), channel_id=1, source_target_pairs={{0,96},{4,112},{8,104},{12,120},{16,0},{20,16},{24,8},{28,24},{32,... | collective-permute-start | bytes 430088 | tf_op jit(solution)/shard_map/ppermute | solution.py:431
  104.6 12.8 %collective-permute-start.10 = (f32[280,128]{1,0:T(8,128)S(1)}, f32[280,128]{1,0:T(8,128)S(1)}, u32[]{:S(2)}, u32[]{:S(2)}) collective-permute-start(f32[280,128]{1,0:T(8,128)S(1)} %get-tuple-element.42), channel_id=1, source_target_pairs={{2,96},{6,112},{10,104},{14,120},{18,0},{22,16},{26,8},{30,24},{34... | collective-permute-start | bytes 430088 | tf_op jit(solution)/shard_map/ppermute | solution.py:431
  118.2 20.8 %all-to-all-start.2 = ((f32[16,40,128]{2,1,0:T(8,128)}), f32[16,40,128]{2,1,0:T(8,128)S(1)}, u32[]{:S(2)}, u32[]{:S(2)}) async-start(f32[16,40,128]{2,1,0:T(8,128)} %pad_maximum_fusion), calls=%async_computation.2 | async-start | bytes 655360 | tf_op jit(solution)/shard_map/all_to_all | solution.py:436
  139.1 9.2 %collective-permute-start.13 = (f32[24,128]{1,0:T(8,128)S(1)}, f32[24,128]{1,0:T(8,128)S(1)}, u32[]{:S(2)}, u32[]{:S(2)}) collective-permute-start(f32[24,128]{1,0:T(8,128)S(1)} %slice_reduce_fusion), channel_id=1, source_target_pairs={{0,3},{1,0},{2,1},{3,2},{4,7},{5,4},{6,5},{7,6},{8,11},{9,8},{10,9... | collective-permute-start | bytes 36872 | tf_op jit(solution)/shard_map/ppermute | solution.py:443
  141.3 7.0 %collective-permute-start.12 = (f32[24,128]{1,0:T(8,128)S(1)}, f32[24,128]{1,0:T(8,128)S(1)}, u32[]{:S(2)}, u32[]{:S(2)}) collective-permute-start(f32[24,128]{1,0:T(8,128)S(1)} %slice_reduce_fusion), channel_id=1, source_target_pairs={{0,2},{1,3},{2,0},{3,1},{4,6},{5,7},{6,4},{7,5},{8,10},{9,11},{10,... | collective-permute-start | bytes 36872 | tf_op jit(solution)/shard_map/ppermute | solution.py:443
  143.0 5.3 %collective-permute-start.11 = (f32[24,128]{1,0:T(8,128)S(1)}, f32[24,128]{1,0:T(8,128)S(1)}, u32[]{:S(2)}, u32[]{:S(2)}) collective-permute-start(f32[24,128]{1,0:T(8,128)S(1)} %slice_reduce_fusion), channel_id=1, source_target_pairs={{0,1},{1,2},{2,3},{3,0},{4,5},{5,6},{6,7},{7,4},{8,9},{9,10},{10,1... | collective-permute-start | bytes 36872 | tf_op jit(solution)/shard_map/ppermute | solution.py:443
  (11 other events, 7.9 us)

commit v3 on v2

--- a/solution.py
+++ b/solution.py
@@ -94,21 +94,35 @@
     return wide, turned
 
 
+def window(packed, place, part):
+    start = pl.multiple_of(place * 16, 16)
+    return jnp.concatenate(
+        [packed[d, part, pl.ds(start, 48)] for d in range(3)], axis=0
+    )
+
+
+def forward(place, table, packed):
+    high = window(packed, place, 0)
+    low = window(packed, place, 1)
+    data = jnp.concatenate([high, high, low], axis=0)
+    return jnp.dot(table, data, preferred_element_type=F32), high, low
+
+
 def conv_kernel(
-    edge, init, grad, before, after, lower, upper, wide, turned, base, sums,
-    xs, gs, xb, gb, acc,
+    init, grad, before, after, lower, upper, wide, xb, sums, xs, gs, gb
 ):
     gs[:, :, 0:1] = jnp.zeros((18, 2, 1, 256), F32)
     gs[:, :, 7:8] = jnp.zeros((18, 2, 1, 256), F32)
     for i in range(2):
         xs[2:18, i, 2:6] = init[i]
-        xs[2:18, i, 0:2] = before[i, :, 0:2]
-        xs[2:18, i, 6:8] = after[i, :, 0:2]
+        for k in range(2):
+            xs[2:18, i, k : k + 1] = before[2 * k + i].reshape(16, 1, 256)
+            xs[2:18, i, k + 6 : k + 7] = after[2 * k + i].reshape(16, 1, 256)
         xs[0:2, i] = lower[2 * i : 2 * i + 2]
         xs[18:20, i] = upper[2 * i : 2 * i + 2]
         gs[1:17, i, 2:6] = grad[i]
-        gs[1:17, i, 1:2] = before[i, :, 2:3]
-        gs[1:17, i, 6:7] = after[i, :, 2:3]
+        gs[1:17, i, 1:2] = before[4 + i].reshape(16, 1, 256)
+        gs[1:17, i, 6:7] = after[4 + i].reshape(16, 1, 256)
         gs[0:1, i, 1:7] = lower[4 + i : 5 + i, 0:6]
         gs[17:18, i, 1:7] = upper[4 + i : 5 + i, 0:6]
     for plain, packed, count in ((xs, xb, 320), (gs, gb, 288)):
@@ -117,24 +131,34 @@
             high, low = split(shifted(value, 1 - d))
             packed[d, 0] = high
             packed[d, 1] = low
+    sums[...] = jnp.zeros_like(sums)
+
+    def step(r, carry):
+        response, xh, xl = forward(r + 1, wide[48:240], xb)
+        linear, gh, gl = forward(r, wide[48:240], gb)
+        core = jnp.tanh(response)
+        weighted = (1.0 - core * core) * linear
+        ch, cl = split(core)
+        wh, wl = split(weighted)
+        left = jnp.concatenate([gh, gh, gl, xh, xh, xl], axis=1)
+        right = jnp.concatenate([ch, cl, ch, wh, wl, wh], axis=1)
+        sums[...] += lax.dot_general(
+            left, right, (((1,), (1,)), ((), ())), preferred_element_type=F32
+        )
+        return carry
+
+    lax.fori_loop(0, 16, step, 0)
+
+
+def adjoint_kernel(edge, init, xb, wide, turned, base, acc):
     acc[...] = jnp.zeros_like(acc)
-    sums[...] = jnp.zeros_like(sums)
     row = lax.broadcasted_iota(jnp.int32, (288, 256), 0)
     keep = jnp.where(row < 48, edge[0], jnp.where(row >= 240, edge[1], 1.0))
 
-    def window(packed, place, part):
-        start = pl.multiple_of(place * 16, 16)
-        return jnp.concatenate(
-            [packed[d, part, pl.ds(start, 48)] for d in range(3)], axis=0
-        )
-
-    def forward(place, table, packed):
-        high = window(packed, place, 0)
-        low = window(packed, place, 1)
-        data = jnp.concatenate([high, high, low], axis=0)
-        return jnp.dot(table, data, preferred_element_type=F32), high, low
-
-    def scatter(place, high, low):
+    def step(place, carry):
+        scale = jnp.where(place == 0, edge[2], jnp.where(place == 17, edge[3], 1.0))
+        response, _, _ = forward(place, wide[...], xb)
+        high, low = split(jnp.tanh(response) * (keep * scale))
         data = jnp.concatenate([high, low], axis=0)
         product = jnp.dot(turned[...], data, preferred_element_type=F32)
         product = product[:72] + product[72:]
@@ -142,34 +166,9 @@
             for d in range(3):
                 first = (r * 3 + d) * 8
                 acc[d, pl.ds(place + r, 1)] += product[first : first + 8][None]
-
-    def border(k, carry):
-        place = 17 * k
-        scale = jnp.where(k == 0, edge[2], edge[3])
-        response, _, _ = forward(place, wide[...], xb)
-        high, low = split(jnp.tanh(response) * (keep * scale))
-        scatter(place, high, low)
         return carry
 
-    def step(r, carry):
-        response, xh, xl = forward(r + 1, wide[...], xb)
-        linear, gh, gl = forward(r, wide[48:240], gb)
-        active = jnp.tanh(response) * keep
-        core = active[48:240]
-        weighted = (1.0 - core * core) * linear
-        high, low = split(active)
-        wh, wl = split(weighted)
-        ch, cl = high[48:240], low[48:240]
-        left = jnp.concatenate([gh, gh, gl, xh, xh, xl], axis=1)
-        right = jnp.concatenate([ch, cl, ch, wh, wl, wh], axis=1)
-        sums[...] += lax.dot_general(
-            left, right, (((1,), (1,)), ((), ())), preferred_element_type=F32
-        )
-        scatter(r + 1, high, low)
-        return carry
-
-    lax.fori_loop(0, 2, border, 0)
-    lax.fori_loop(0, 16, step, 0)
+    lax.fori_loop(0, 18, step, 0)
     total = (
         shifted(acc[0, 2:18].reshape(128, 256), -1)
         + acc[1, 2:18].reshape(128, 256)
@@ -179,27 +178,41 @@
         base[i] = init[i] - total[:, 4 * i : 4 * i + 4]
 
 
-def conv_call(edge, init, grad, before, after, lower, upper, wide, turned):
-    vm = pl.BlockSpec(memory_space=pltpu.VMEM)
+VM = pl.BlockSpec(memory_space=pltpu.VMEM)
+SM = pl.BlockSpec(memory_space=pltpu.SMEM)
+
+
+def conv_call(init, grad, before, after, lower, upper, wide):
     return pl.pallas_call(
         conv_kernel,
         out_shape=(
-            jax.ShapeDtypeStruct((2, 16, 4, 256), F32),
+            jax.ShapeDtypeStruct((3, 2, 320, 256), BF),
             jax.ShapeDtypeStruct((144, 192), F32),
         ),
-        in_specs=[pl.BlockSpec(memory_space=pltpu.SMEM)] + [vm] * 8,
-        out_specs=(vm, vm),
+        in_specs=[VM] * 7,
+        out_specs=(VM, VM),
         scratch_shapes=[
             pltpu.VMEM((20, 2, 8, 256), F32),
             pltpu.VMEM((18, 2, 8, 256), F32),
-            pltpu.VMEM((3, 2, 320, 256), BF),
             pltpu.VMEM((3, 2, 288, 256), BF),
-            pltpu.VMEM((3, 20, 8, 256), F32),
         ],
         cost_estimate=pl.CostEstimate(
-            flops=6000000000, bytes_accessed=2000000, transcendentals=1300000
+            flops=4000000000, bytes_accessed=2000000, transcendentals=800000
         ),
-    )(edge, init, grad, before, after, lower, upper, wide, turned)
+    )(init, grad, before, after, lower, upper, wide)
+
+
+def adjoint_call(edge, init, xb, wide, turned):
+    return pl.pallas_call(
+        adjoint_kernel,
+        out_shape=jax.ShapeDtypeStruct((2, 16, 4, 256), F32),
+        in_specs=[SM] + [VM] * 4,
+        out_specs=VM,
+        scratch_shapes=[pltpu.VMEM((3, 20, 8, 256), F32)],
+        cost_estimate=pl.CostEstimate(
+            flops=4000000000, bytes_accessed=2000000, transcendentals=1300000
+        ),
+    )(edge, init, xb, wide, turned)
 
 
 def diagonal(sums):
@@ -222,12 +235,11 @@
             high = table.astype(BF)
             made.append(high)
             made.append((table - high.astype(np.float32)).astype(BF))
-    return made
+    return np.stack(made)
 
 
 def transform_kernel(
-    coil, maps, p0, p1, p2, p3, kspace, mask, extra, ch, cl, sh, sl, yh, yl, zh, zl,
-    uh, ul, wh, wl, kept, sent, rows, right, left, lhs, rhs,
+    coil, maps, p0, p1, p2, p3, kspace, mask, extra, table, kept, sent, rows, right, left, lhs, rhs,
 ):
     here = coil[0]
     pieces = (p0, p1, p2, p3)
@@ -240,16 +252,19 @@
         def _():
             for q in range(4):
                 rows[q] = pieces[slot(a, q)][...]
-    for part, cosine, sine in ((0, ch, sh), (1, cl, sl)):
-        right[part, :256, :256] = cosine[...]
-        right[part, :256, 256:] = -sine[...]
-        right[part, 256:, :256] = sine[...]
-        right[part, 256:, 256:] = cosine[...]
-    for part, cosine, sine in ((0, yh, zh), (1, yl, zl), (2, uh, wh), (3, ul, wl)):
-        left[part, :256, :256] = cosine[...]
-        left[part, :256, 256:] = sine[...]
-        left[part, 256:, :256] = -sine[...]
-        left[part, 256:, 256:] = cosine[...]
+    for part in range(2):
+        cosine, sine = table[part], table[2 + part]
+        right[part, :256, :256] = cosine
+        right[part, :256, 256:] = -sine
+        right[part, 256:, :256] = sine
+        right[part, 256:, 256:] = cosine
+    for part in range(4):
+        first = 4 + part // 2 * 4 + part % 2
+        cosine, sine = table[first], table[first + 2]
+        left[part, :256, :256] = cosine
+        left[part, :256, 256:] = sine
+        left[part, 256:, :256] = -sine
+        left[part, 256:, 256:] = cosine
 
     def halves(load):
         return jnp.concatenate(
@@ -354,11 +369,10 @@
 
 def transform_call(coil, maps, pieces, kspace, mask, extra):
     vm = pl.BlockSpec(memory_space=pltpu.VMEM)
-    consts = tables()
     return pl.pallas_call(
         transform_kernel,
         out_shape=tuple(jax.ShapeDtypeStruct((2, 280, 128), F32) for _ in range(2)),
-        in_specs=[pl.BlockSpec(memory_space=pltpu.SMEM)] + [vm] * 20,
+        in_specs=[pl.BlockSpec(memory_space=pltpu.SMEM)] + [vm] * 9,
         out_specs=(vm,) * 2,
         scratch_shapes=[
             pltpu.VMEM((4, 512, 128), F32),
@@ -370,23 +384,27 @@
         cost_estimate=pl.CostEstimate(
             flops=6000000000, bytes_accessed=5000000, transcendentals=0
         ),
-    )(coil, maps, *pieces, kspace, mask, extra, *[jnp.asarray(t) for t in consts])
+    )(coil, maps, *pieces, kspace, mask, extra, jnp.asarray(tables()))
 
 
 def halos(state, grad, slab_count):
     up = [(i, i + 1) for i in range(slab_count - 1)]
     down = [(i + 1, i) for i in range(slab_count - 1)]
-    high = jnp.concatenate([state[:, :, 2:], grad[:, :, 3:]], axis=2)
-    low = jnp.concatenate([state[:, :, :2], grad[:, :, :1]], axis=2)
-    before = lax.ppermute(high, "slab", up)
-    after = lax.ppermute(low, "slab", down)
+
+    def pack(first, second, third):
+        return jnp.concatenate(
+            [state[:, :, first], state[:, :, second], grad[:, :, third]], axis=0
+        )
+
+    before = lax.ppermute(pack(2, 3, 3), "slab", up)
+    after = lax.ppermute(pack(0, 1, 0), "slab", down)
 
     def planes(at, last):
-        rows = jnp.concatenate(
-            [before[:, at, :2], state[:, at], after[:, at, :2]], axis=2
-        ).reshape(4, 8, 256)
+        head = before[:4, at].reshape(2, 2, 2, 256).transpose(1, 2, 0, 3)
+        tail = after[:4, at].reshape(2, 2, 2, 256).transpose(1, 2, 0, 3)
+        rows = jnp.concatenate([head, state[:, at], tail], axis=2).reshape(4, 8, 256)
         edge = jnp.concatenate(
-            [before[:, last, 2:], grad[:, last], after[:, last, 2:]], axis=1
+            [before[4:, last, None], grad[:, last], after[4:, last, None]], axis=1
         )
         return jnp.concatenate([rows, jnp.pad(edge, ((0, 0), (0, 2), (0, 0)))], axis=0)
 
@@ -415,8 +433,8 @@
     before, after, lower, upper = halos(init_image, recon_cotangent, slab_count)
     wide, turned = filter_tables(weights)
     edge = jnp.stack([slab > 0, slab < slab_count - 1, coil > 0, coil < 3]).astype(F32)
-    base, sums = conv_call(
-        edge, init_image, recon_cotangent, before, after, lower, upper, wide, turned
+    packed, sums = conv_call(
+        init_image, recon_cotangent, before, after, lower, upper, wide
     )
     extra = jnp.pad(-diagonal(sums).reshape(2592), (0, 480)).reshape(24, 128)
 
@@ -437,6 +455,7 @@
         sent, "slab", split_axis=0, concat_axis=0, tiled=True,
         axis_index_groups=GROUPS,
     )
+    base = adjoint_call(edge, init_image, packed, wide, turned)
     own = jnp.sum(arrived[:, 16:], axis=0)
     riders = own
     for turn in range(1, 4):

time: 150 us -> 146 us (0.973)
  Pallas kernels: 24.4 us -> 32.7 us
  waiting for transfers between devices: 36.5 us -> 28.6 us
  starting transfers between devices: 65.7 us -> 61.8 us
  local copies, waits for them, and re-layouts: 14.4 us -> 12.6 us
    all_to_all x1, waiting for transfers between devices: 12.9 us -> 0.11 us  [on_device(): lax.all_to_all(sent, 'slab', split_axis=0, concat_axis=0, tiled=True, axi...]
    pallas_call x1 -> x2, Pallas kernels: 15.6 us -> 23.8 us  [the longest x1 12 us: conv_call(): pl.pallas_call(conv_kernel, out_shape=(jax.ShapeDtypeStruct((3, 2, 320, 2...]
    unnamed x41 -> x39, local copies, waits for them, and re-layouts: 5.4 us -> 2.37 us
    all_to_all x1, waiting for transfers between devices: 3.71 us -> 6.46 us  [on_device(): lax.all_to_all(images, 'slab', split_axis=0, concat_axis=0, tiled=True, a...]
    all_to_all x1, starting transfers between devices: 7.2 us -> 5.42 us  [on_device(): lax.all_to_all(maps, 'slab', split_axis=0, concat_axis=0, tiled=True)]
  transfers between devices with their start and end apart: 17 -> 17, of which waited for: 8 -> 8; matrix products, arithmetic and copies ran while one was open for 8% -> 9% of each run, Pallas kernels for 10% -> 16%
where the time goes in v3:
time: 146 us; the launch traced here: 145 us
  starting transfers between devices  61.8 us (42%)
  Pallas kernels  32.7 us (22%)
  waiting for transfers between devices  28.6 us (20%)
  local copies, waits for them, and re-layouts  12.6 us (9%)
  other arithmetic  7.18 us (5%)
  between operations  1.96 us (1%)
    all_to_all x1, starting transfers between devices, on_device(): lax.all_to_all(images, 'slab', split_axis=0, concat_axis=0, tiled=True, a...  12.4 us
    pallas_call x1, Pallas kernels, conv_call(): pl.pallas_call(conv_kernel, out_shape=(jax.ShapeDtypeStruct((3, 2, 320, 2...  12 us
    pallas_call x1, Pallas kernels, adjoint_call(): pl.pallas_call(adjoint_kernel, out_shape=jax.ShapeDtypeStruct((2, 16, 4,...  11.8 us
    ppermute x2, waiting for transfers between devices, on_device(): pieces = [lax.ppermute(held, AXES, far_pairs(turn)) for turn in range(2)]  9.82 us
    pallas_call x1, Pallas kernels, transform_call(): pl.pallas_call(transform_kernel, out_shape=tuple((jax.ShapeDtypeStruct((2...  8.89 us
    ppermute x1, starting transfers between devices, on_device(): lax.ppermute(kept[1], AXES, back_pairs(1))  7.65 us
    all_to_all x1, starting transfers between devices, on_device(): lax.all_to_all(sent, 'slab', split_axis=0, concat_axis=0, tiled=True, axi...  7.04 us
    ppermute x1, starting transfers between devices, halos(): lower = lax.ppermute(planes(slice(14, 16), 15), 'coil', up)  6.83 us
  transfers between devices with their start and end apart: 17, of which 8 were waited for; matrix products, arithmetic and copies ran while one was open for 9% of the time, Pallas kernels for 16%

profile of v3, /device:TPU:1, one launch (start us, length us, event | category | flops | bytes accessed | tf_op | source)
XLA Modules:
  0.0 144.8 jit_solution(1807978201430378303)
XLA Ops:
  1.7 1.4 fusion.11
  3.1 4.0 %collective-permute-start = (f32[6,16,256]{2,1,0:T(8,128)S(1)}, f32[6,16,256]{2,1,0:T(8,128)S(1)}, u32[]{:S(2)}, u32[]{:S(2)}) collective-permute-start(f32[6,16,256]{2,1,0:T(8,128)S(1)} %pad_maximum_fusion.2), channel_id=1, source_target_pairs={{0,4},{4,8},{8,12},{12,16},{16,20},{20,24},{24,28},{28,32},{32,36}... | collective-permute-start | bytes 294920 | tf_op jit(solution)/shard_map/ppermute | solution.py:399
  7.2 1.3 collective-permute-start.1
  10.6 12.4 %all-to-all-start = ((f32[16,32,128]{2,1,0:T(8,128)}), f32[16,32,128]{2,1,0:T(8,128)S(1)}, u32[]{:S(2)}, u32[]{:S(2)}) async-start(f32[16,32,128]{2,1,0:T(8,128)} %select_n.33), calls=%async_computation | async-start | bytes 524288 | tf_op jit(solution)/shard_map/all_to_all | solution.py:425
  26.1 1.8 %reshape.232 = f32[64,32,128]{2,1,0:T(8,128)} reshape(f32[64,4,2,2,256]{4,3,2,1,0:T(2,128)S(1)} %copy.125) | data formatting | bytes 2097152 | tf_op jit(solution)/shard_map/reshape | solution.py:429
  28.1 6.5 %all-to-all-done = f32[16,32,128]{2,1,0:T(8,128)S(1)} async-done(((f32[16,32,128]{2,1,0:T(8,128)}), f32[16,32,128]{2,1,0:T(8,128)S(1)}, u32[]{:S(2)}, u32[]{:S(2)}) %all-to-all-start) | async-done | bytes 262176 | tf_op jit(solution)/shard_map/all_to_all | solution.py:425
  34.6 5.4 %all-to-all-start.1 = ((f32[64,32,128]{2,1,0:T(8,128)}), f32[64,32,128]{2,1,0:T(8,128)S(1)}, u32[]{:S(2)}, u32[]{:S(2)}) async-start(f32[64,32,128]{2,1,0:T(8,128)} %reshape.232), calls=%async_computation.1 | async-start | bytes 2097152 | tf_op jit(solution)/shard_map/all_to_all | solution.py:431
  40.0 6.8 %collective-permute-start.2 = (f32[6,8,256]{2,1,0:T(8,128)S(1)}, f32[6,8,256]{2,1,0:T(8,128)S(1)}, u32[]{:S(2)}, u32[]{:S(2)}) collective-permute-start(f32[6,8,256]{2,1,0:T(8,128)S(1)} %pad_maximum_fusion.4), channel_id=1, source_target_pairs={{0,1},{1,2},{2,3},{4,5},{5,6},{6,7},{8,9},{9,10},{10,11},{12,13},{... | collective-permute-start | bytes 147464 | tf_op jit(solution)/shard_map/ppermute | solution.py:413
  46.9 1.9 %collective-permute-start.3 = (f32[6,8,256]{2,1,0:T(8,128)S(1)}, f32[6,8,256]{2,1,0:T(8,128)S(1)}, u32[]{:S(2)}, u32[]{:S(2)}) collective-permute-start(f32[6,8,256]{2,1,0:T(8,128)S(1)} %pad_maximum_fusion.5), channel_id=1, source_target_pairs={{1,0},{2,1},{3,2},{5,4},{6,5},{7,6},{9,8},{10,9},{11,10},{13,12},{... | collective-permute-start | bytes 147464 | tf_op jit(solution)/shard_map/ppermute | solution.py:414
  49.8 4.8 %collective-permute-done.3.upper = f32[6,8,256]{2,1,0:T(8,128)S(1)} collective-permute-done((f32[6,8,256]{2,1,0:T(8,128)S(1)}, f32[6,8,256]{2,1,0:T(8,128)S(1)}, u32[]{:S(2)}, u32[]{:S(2)}) %collective-permute-start.3) | collective-permute-done | bytes 49184 | tf_op jit(solution)/shard_map/ppermute | solution.py:414
  55.2 12.0 %shard_map.157 = (bf16[3,2,320,256]{3,2,1,0:T(8,128)(2,1)}, f32[144,192]{1,0:T(8,128)}) custom-call(f32[2,16,4,256]{3,2,1,0:T(4,128)} %init.3, f32[2,16,4,256]{3,2,1,0:T(4,128)} %grad.1, f32[6,16,256]{2,1,0:T(8,128)} %copy-done.4, f32[6,16,256]{2,1,0:T(8,128)} %copy-done.5, f32[6,8,256]{2,1,0:T(8,128)} %copy-done.16, f32[6,8,256]{2,1,0:T(8,128)} %copy-done.17, ...), custom_call_target="tpu_custom_call" | custom-call | flops 4000000000 | bytes 2000000 | tf_op jit(solution)/shard_map/pallas_call | solution.py:186
  68.4 1.9 %collective-permute-start.4 = (f32[512,128]{1,0:T(8,128)S(1)}, f32[512,128]{1,0:T(8,128)S(1)}, u32[]{:S(2)}, u32[]{:S(2)}) collective-permute-start(f32[512,128]{1,0:T(8,128)S(1)} %bitcast.117), channel_id=1, source_target_pairs={{96,0},{112,4},{104,8},{120,12},{0,16},{16,20},{8,24},{24,28},{32,... | collective-permute-start | bytes 786440 | tf_op jit(solution)/shard_map/ppermute | solution.py:442
  70.3 1.9 %collective-permute-start.5 = (f32[512,128]{1,0:T(8,128)S(1)}, f32[512,128]{1,0:T(8,128)S(1)}, u32[]{:S(2)}, u32[]{:S(2)}) collective-permute-start(f32[512,128]{1,0:T(8,128)S(1)} %bitcast.118), channel_id=1, source_target_pairs={{96,2},{112,6},{104,10},{120,14},{0,18},{16,22},{8,26},{24,30},{32... | collective-permute-start | bytes 786440 | tf_op jit(solution)/shard_map/ppermute | solution.py:442
  72.2 8.5 %collective-permute-done.4.p0 = f32[512,128]{1,0:T(8,128)S(1)} collective-permute-done((f32[512,128]{1,0:T(8,128)S(1)}, f32[512,128]{1,0:T(8,128)S(1)}, u32[]{:S(2)}, u32[]{:S(2)}) %collective-permute-start.4) | collective-permute-done | bytes 262176 | tf_op jit(solution)/shard_map/ppermute | solution.py:442
  84.7 8.9 %shard_map.159 = (f32[2,280,128]{2,1,0:T(8,128)}, f32[2,280,128]{2,1,0:T(8,128)}) custom-call(s32[1]{0:T(128)} %bitcast.33.coil, f32[2048,128]{1,0:T(8,128)} %bitcast.112, f32[512,128]{1,0:T(8,128)} %copy-done.12, f32[512,128]{1,0:T(8,128)} %copy-done.13, f32[512,128]{1,0:T(8,128)} %copy-done.14, f32[512,128]{1,0:T(8,128)} %copy-done.15, ...), custom_call_target="tpu_custom_call" | custom-call | flops 6000000000 | bytes 5000000 | tf_op jit(solution)/shard_map/pallas_call | solution.py:372
  93.7 1.7 %collective-permute-done.8 = f32[2,280,128]{2,1,0:T(8,128)S(1)} collective-permute-done((f32[2,280,128]{2,1,0:T(8,128)}, f32[2,280,128]{2,1,0:T(8,128)S(1)}, u32[]{:S(2)}, u32[]{:S(2)}) %collective-permute-start.8) | collective-permute-done | bytes 286752 | tf_op jit(solution)/shard_map/ppermute | solution.py:448
  96.4 5.0 %collective-permute-start.9 = (f32[280,128]{1,0:T(8,128)S(1)}, f32[280,128]{1,0:T(8,128)S(1)}, u32[]{:S(2)}, u32[]{:S(2)}) collective-permute-start(f32[280,128]{1,0:T(8,128)S(1)} %get-tuple-element.43), channel_id=1, source_target_pairs={{0,96},{4,112},{8,104},{12,120},{16,0},{20,16},{24,8},{28,24},{32,... | collective-permute-start | bytes 430088 | tf_op jit(solution)/shard_map/ppermute | solution.py:449
  101.4 7.7 %collective-permute-start.10 = (f32[280,128]{1,0:T(8,128)S(1)}, f32[280,128]{1,0:T(8,128)S(1)}, u32[]{:S(2)}, u32[]{:S(2)}) collective-permute-start(f32[280,128]{1,0:T(8,128)S(1)} %get-tuple-element.42), channel_id=1, source_target_pairs={{2,96},{6,112},{10,104},{14,120},{18,0},{22,16},{26,8},{30,24},{34... | collective-permute-start | bytes 430088 | tf_op jit(solution)/shard_map/ppermute | solution.py:449
  109.4 4.9 %collective-permute-done.10 = f32[280,128]{1,0:T(8,128)S(1)} collective-permute-done((f32[280,128]{1,0:T(8,128)S(1)}, f32[280,128]{1,0:T(8,128)S(1)}, u32[]{:S(2)}, u32[]{:S(2)}) %collective-permute-start.10) | collective-permute-done | bytes 143392 | tf_op jit(solution)/shard_map/ppermute | solution.py:449
  115.1 7.0 %all-to-all-start.2 = ((f32[16,40,128]{2,1,0:T(8,128)}), f32[16,40,128]{2,1,0:T(8,128)S(1)}, u32[]{:S(2)}, u32[]{:S(2)}) async-start(f32[16,40,128]{2,1,0:T(8,128)} %pad_maximum_fusion), calls=%async_computation.2 | async-start | bytes 655360 | tf_op jit(solution)/shard_map/all_to_all | solution.py:454
  124.2 11.8 %shard_map.158 = f32[2,16,4,256]{3,2,1,0:T(4,128)} custom-call(f32[4]{0:T(128)} %add_convert_fusion.edge, f32[2,16,4,256]{3,2,1,0:T(4,128)} %init.3, bf16[3,2,320,256]{3,2,1,0:T(8,128)(2,1)} %get-tuple-element.9.xb, bf16[288,432]{1,0:T(8,128)(2,1)} %pad_maximum_fusion.1.wide, bf16[144,576]{1,0:T(8,128)(2,1)} %fusion.1.turned), custom_call_target="tpu_custom_call" | custom-call | flops 4000000000 | bytes 2000000 | tf_op jit(solution)/shard_map/pallas_call | solution.py:206
  136.2 2.1 %collective-permute-start.13 = (f32[24,128]{1,0:T(8,128)S(1)}, f32[24,128]{1,0:T(8,128)S(1)}, u32[]{:S(2)}, u32[]{:S(2)}) collective-permute-start(f32[24,128]{1,0:T(8,128)S(1)} %slice_reduce_fusion), channel_id=1, source_target_pairs={{0,3},{1,0},{2,1},{3,2},{4,7},{5,4},{6,5},{7,6},{8,11},{9,8},{10,9... | collective-permute-start | bytes 36872 | tf_op jit(solution)/shard_map/ppermute | solution.py:462
  138.2 2.5 %collective-permute-start.12 = (f32[24,128]{1,0:T(8,128)S(1)}, f32[24,128]{1,0:T(8,128)S(1)}, u32[]{:S(2)}, u32[]{:S(2)}) collective-permute-start(f32[24,128]{1,0:T(8,128)S(1)} %slice_reduce_fusion), channel_id=1, source_target_pairs={{0,2},{1,3},{2,0},{3,1},{4,6},{5,7},{6,4},{7,5},{8,10},{9,11},{10,... | collective-permute-start | bytes 36872 | tf_op jit(solution)/shard_map/ppermute | solution.py:462
  140.8 1.7 %collective-permute-start.11 = (f32[24,128]{1,0:T(8,128)S(1)}, f32[24,128]{1,0:T(8,128)S(1)}, u32[]{:S(2)}, u32[]{:S(2)}) collective-permute-start(f32[24,128]{1,0:T(8,128)S(1)} %slice_reduce_fusion), channel_id=1, source_target_pairs={{0,1},{1,2},{2,3},{3,0},{4,5},{5,6},{6,7},{7,4},{8,9},{9,10},{10,1... | collective-permute-start | bytes 36872 | tf_op jit(solution)/shard_map/ppermute | solution.py:462
  (124 shorter events, 18.9 us)
Async XLA Ops:
  3.1 24.9 %collective-permute-start = (f32[6,16,256]{2,1,0:T(8,128)S(1)}, f32[6,16,256]{2,1,0:T(8,128)S(1)}, u32[]{:S(2)}, u32[]{:S(2)}) collective-permute-start(f32[6,16,256]{2,1,0:T(8,128)S(1)} %pad_maximum_fusion.2), channel_id=1, source_target_pairs={{0,4},{4,8},{8,12},{12,16},{16,20},{20,24},{24,28},{28,32},{32,36}... | collective-permute-start | bytes 294920 | tf_op jit(solution)/shard_map/ppermute | solution.py:399
  7.2 20.8 %collective-permute-start.1 = (f32[6,16,256]{2,1,0:T(8,128)S(1)}, f32[6,16,256]{2,1,0:T(8,128)S(1)}, u32[]{:S(2)}, u32[]{:S(2)}) collective-permute-start(f32[6,16,256]{2,1,0:T(8,128)S(1)} %pad_maximum_fusion.3), channel_id=1, source_target_pairs={{4,0},{8,4},{12,8},{16,12},{20,16},{24,20},{28,24},{32,28},{36,32}... | collective-permute-start | bytes 294920 | tf_op jit(solution)/shard_map/ppermute | solution.py:400
  9.5 14.2 %copy-start.6 = (f32[6,8]{0,1:T(8,128)S(1)}, f32[6,8]{0,1:T(8,128)}, u32[]{:S(2)}) copy-start(f32[6,8]{0,1:T(8,128)} %constant.50.clone) | copy-start | bytes 580
  9.5 14.2 %copy-start.7 = (f32[6,8]{0,1:T(8,128)S(1)}, f32[6,8]{0,1:T(8,128)}, u32[]{:S(2)}) copy-start(f32[6,8]{0,1:T(8,128)} %constant.49.clone) | copy-start | bytes 580
  10.6 24.0 %all-to-all-start = ((f32[16,32,128]{2,1,0:T(8,128)}), f32[16,32,128]{2,1,0:T(8,128)S(1)}, u32[]{:S(2)}, u32[]{:S(2)}) async-start(f32[16,32,128]{2,1,0:T(8,128)} %select_n.33), calls=%async_computation | async-start | bytes 524288 | tf_op jit(solution)/shard_map/all_to_all | solution.py:425
  27.9 21.8 %copy-start.5 = (f32[6,16,256]{2,1,0:T(8,128)}, f32[6,16,256]{2,1,0:T(8,128)S(1)}, u32[]{:S(2)}) copy-start(f32[6,16,256]{2,1,0:T(8,128)S(1)} %collective-permute-done.1.after) | copy-start | bytes 294916
  28.0 21.8 %copy-start.4 = (f32[6,16,256]{2,1,0:T(8,128)}, f32[6,16,256]{2,1,0:T(8,128)S(1)}, u32[]{:S(2)}) copy-start(f32[6,16,256]{2,1,0:T(8,128)S(1)} %collective-permute-done.before) | copy-start | bytes 294916
  34.6 49.1 %all-to-all-start.1 = ((f32[64,32,128]{2,1,0:T(8,128)}), f32[64,32,128]{2,1,0:T(8,128)S(1)}, u32[]{:S(2)}, u32[]{:S(2)}) async-start(f32[64,32,128]{2,1,0:T(8,128)} %reshape.232), calls=%async_computation.1 | async-start | bytes 2097152 | tf_op jit(solution)/shard_map/all_to_all | solution.py:431
  40.0 9.7 %collective-permute-start.2 = (f32[6,8,256]{2,1,0:T(8,128)S(1)}, f32[6,8,256]{2,1,0:T(8,128)S(1)}, u32[]{:S(2)}, u32[]{:S(2)}) collective-permute-start(f32[6,8,256]{2,1,0:T(8,128)S(1)} %pad_maximum_fusion.4), channel_id=1, source_target_pairs={{0,1},{1,2},{2,3},{4,5},{5,6},{6,7},{8,9},{9,10},{10,11},{12,13},{... | collective-permute-start | bytes 147464 | tf_op jit(solution)/shard_map/ppermute | solution.py:413
  46.9 7.7 %collective-permute-start.3 = (f32[6,8,256]{2,1,0:T(8,128)S(1)}, f32[6,8,256]{2,1,0:T(8,128)S(1)}, u32[]{:S(2)}, u32[]{:S(2)}) collective-permute-start(f32[6,8,256]{2,1,0:T(8,128)S(1)} %pad_maximum_fusion.5), channel_id=1, source_target_pairs={{1,0},{2,1},{3,2},{5,4},{6,5},{7,6},{9,8},{10,9},{11,10},{13,12},{... | collective-permute-start | bytes 147464 | tf_op jit(solution)/shard_map/ppermute | solution.py:414
  68.4 12.4 %collective-permute-start.4 = (f32[512,128]{1,0:T(8,128)S(1)}, f32[512,128]{1,0:T(8,128)S(1)}, u32[]{:S(2)}, u32[]{:S(2)}) collective-permute-start(f32[512,128]{1,0:T(8,128)S(1)} %bitcast.117), channel_id=1, source_target_pairs={{96,0},{112,4},{104,8},{120,12},{0,16},{16,20},{8,24},{24,28},{32,... | collective-permute-start | bytes 786440 | tf_op jit(solution)/shard_map/ppermute | solution.py:442
  70.3 11.7 %collective-permute-start.5 = (f32[512,128]{1,0:T(8,128)S(1)}, f32[512,128]{1,0:T(8,128)S(1)}, u32[]{:S(2)}, u32[]{:S(2)}) collective-permute-start(f32[512,128]{1,0:T(8,128)S(1)} %bitcast.118), channel_id=1, source_target_pairs={{96,2},{112,6},{104,10},{120,14},{0,18},{16,22},{8,26},{24,30},{32... | collective-permute-start | bytes 786440 | tf_op jit(solution)/shard_map/ppermute | solution.py:442
  80.8 2.0 %collective-permute-start.6 = (f32[512,128]{1,0:T(8,128)S(1)}, f32[512,128]{1,0:T(8,128)S(1)}, u32[]{:S(2)}, u32[]{:S(2)}) collective-permute-start(f32[512,128]{1,0:T(8,128)S(1)} %collective-permute-done.4.p0), channel_id=1, source_target_pairs={{0,1},{1,0},{2,3},{3,2},{4,5},{5,4},{6,7},{7,6},{8,9},{9,8},{10,11... | collective-permute-start | bytes 786440 | tf_op jit(solution)/shard_map/ppermute | solution.py:443
  82.1 1.5 %collective-permute-start.7 = (f32[512,128]{1,0:T(8,128)S(1)}, f32[512,128]{1,0:T(8,128)S(1)}, u32[]{:S(2)}, u32[]{:S(2)}) collective-permute-start(f32[512,128]{1,0:T(8,128)S(1)} %collective-permute-done.5.p1), channel_id=1, source_target_pairs={{0,1},{1,0},{2,3},{3,2},{4,5},{5,4},{6,7},{7,6},{8,9},{9,8},{10,11... | collective-permute-start | bytes 786440 | tf_op jit(solution)/shard_map/ppermute | solution.py:443
  84.7 24.4 %copy-start.9 = (f32[4,6]{1,0:T(4,128)S(1)}, f32[4,6]{1,0:T(4,128)}, u32[]{:S(2)}) copy-start(f32[4,6]{1,0:T(4,128)} %constant.53.clone) | copy-start | bytes 292
  84.7 24.4 %copy-start.10 = (f32[4,6]{1,0:T(4,128)S(1)}, f32[4,6]{1,0:T(4,128)}, u32[]{:S(2)}) copy-start(f32[4,6]{1,0:T(4,128)} %constant.52.clone) | copy-start | bytes 292
  84.7 24.4 %copy-start.11 = (f32[4,6]{1,0:T(4,128)S(1)}, f32[4,6]{1,0:T(4,128)}, u32[]{:S(2)}) copy-start(f32[4,6]{1,0:T(4,128)} %constant.51.clone) | copy-start | bytes 292
  93.6 1.8 %collective-permute-start.8 = (f32[2,280,128]{2,1,0:T(8,128)}, f32[2,280,128]{2,1,0:T(8,128)S(1)}, u32[]{:S(2)}, u32[]{:S(2)}) collective-permute-start(f32[2,280,128]{2,1,0:T(8,128)} %get-tuple-element.14), channel_id=1, source_target_pairs={{0,1},{1,0},{2,3},{3,2},{4,5},{5,4},{6,7},{7,6},{8,9},{9,8},{10,11... | collective-permute-start | bytes 860168 | tf_op jit(solution)/shard_map/ppermute | solution.py:448
  96.4 13.0 %collective-permute-start.9 = (f32[280,128]{1,0:T(8,128)S(1)}, f32[280,128]{1,0:T(8,128)S(1)}, u32[]{:S(2)}, u32[]{:S(2)}) collective-permute-start(f32[280,128]{1,0:T(8,128)S(1)} %get-tuple-element.43), channel_id=1, source_target_pairs={{0,96},{4,112},{8,104},{12,120},{16,0},{20,16},{24,8},{28,24},{32,... | collective-permute-start | bytes 430088 | tf_op jit(solution)/shard_map/ppermute | solution.py:449
  101.4 12.8 %collective-permute-start.10 = (f32[280,128]{1,0:T(8,128)S(1)}, f32[280,128]{1,0:T(8,128)S(1)}, u32[]{:S(2)}, u32[]{:S(2)}) collective-permute-start(f32[280,128]{1,0:T(8,128)S(1)} %get-tuple-element.42), channel_id=1, source_target_pairs={{2,96},{6,112},{10,104},{14,120},{18,0},{22,16},{26,8},{30,24},{34... | collective-permute-start | bytes 430088 | tf_op jit(solution)/shard_map/ppermute | solution.py:449
  115.1 21.1 %all-to-all-start.2 = ((f32[16,40,128]{2,1,0:T(8,128)}), f32[16,40,128]{2,1,0:T(8,128)S(1)}, u32[]{:S(2)}, u32[]{:S(2)}) async-start(f32[16,40,128]{2,1,0:T(8,128)} %pad_maximum_fusion), calls=%async_computation.2 | async-start | bytes 655360 | tf_op jit(solution)/shard_map/all_to_all | solution.py:454
  136.2 7.3 %collective-permute-start.13 = (f32[24,128]{1,0:T(8,128)S(1)}, f32[24,128]{1,0:T(8,128)S(1)}, u32[]{:S(2)}, u32[]{:S(2)}) collective-permute-start(f32[24,128]{1,0:T(8,128)S(1)} %slice_reduce_fusion), channel_id=1, source_target_pairs={{0,3},{1,0},{2,1},{3,2},{4,7},{5,4},{6,5},{7,6},{8,11},{9,8},{10,9... | collective-permute-start | bytes 36872 | tf_op jit(solution)/shard_map/ppermute | solution.py:462
  138.2 5.2 %collective-permute-start.12 = (f32[24,128]{1,0:T(8,128)S(1)}, f32[24,128]{1,0:T(8,128)S(1)}, u32[]{:S(2)}, u32[]{:S(2)}) collective-permute-start(f32[24,128]{1,0:T(8,128)S(1)} %slice_reduce_fusion), channel_id=1, source_target_pairs={{0,2},{1,3},{2,0},{3,1},{4,6},{5,7},{6,4},{7,5},{8,10},{9,11},{10,... | collective-permute-start | bytes 36872 | tf_op jit(solution)/shard_map/ppermute | solution.py:462
  140.8 2.7 %collective-permute-start.11 = (f32[24,128]{1,0:T(8,128)S(1)}, f32[24,128]{1,0:T(8,128)S(1)}, u32[]{:S(2)}, u32[]{:S(2)}) collective-permute-start(f32[24,128]{1,0:T(8,128)S(1)} %slice_reduce_fusion), channel_id=1, source_target_pairs={{0,1},{1,2},{2,3},{3,0},{4,5},{5,6},{6,7},{7,4},{8,9},{9,10},{10,1... | collective-permute-start | bytes 36872 | tf_op jit(solution)/shard_map/ppermute | solution.py:462
  (11 other events, 48.9 us)

commit v4 on v3

--- a/solution.py
+++ b/solution.py
@@ -12,9 +12,8 @@
 
 
 def holder(coil, quarter, low):
-    z = (low // 4 * 2 - 2 + 4 * (coil % 2) + low % 2) % 8
-    y = low % 4 // 2 * 2 + quarter % 2
-    return (quarter // 2 * 32 + z * 4 + y) * 4 + coil
+    z = (low // 4 - 1 + 2 * (coil % 2)) % 4 * 2 + quarter % 2
+    return (quarter // 2 * 32 + z * 4 + low % 4) * 4 + coil
 
 
 def reader(coil, group, low):
@@ -35,7 +34,6 @@
 
 
 CORES = [(i, i ^ 1) for i in range(4)]
-GROUPS = [[x * 32 + e + 2 * k for k in range(16)] for x in range(2) for e in range(2)]
 
 
 def turned_by_core(data, coil, axis, sign):
@@ -225,8 +223,7 @@
 
 def tables():
     place = np.arange(256)
-    mixed = (place // 128 * 32 + place // 64 % 2 + place % 16 * 2) * 4
-    mixed = mixed + place // 16 % 4
+    mixed = place % 64 * 4 + place // 64
     made = []
     for first, second in ((place, place), (place, mixed), (mixed, place)):
         angle = (first[:, None] * second[None, :] % 256) * (2.0 * np.pi / 256)
@@ -269,25 +266,19 @@
     def halves(load):
         return jnp.concatenate(
             [
-                jnp.concatenate([load(q, y, h) for h in range(2)], axis=1)
-                for q in range(4)
+                jnp.concatenate([load(y, h) for h in range(2)], axis=1)
                 for y in range(4)
             ],
             axis=0,
         )
 
     def map_of(part, c):
-        def load(q, y, h):
-            first = (q // 2 * 32 + q % 2) * 32 + (y * 4 + part * 2 + c) * 2 + h
-            return maps[pl.ds(first, 16, stride=64), :]
-
-        return halves(load)
-
-    def image_of(which, part):
-        def load(q, y, h):
-            return rows[q, pl.ds((which * 8 + part * 4 + y) * 2 + h, 16, stride=32), :]
-
-        return halves(load)
+        return halves(
+            lambda y, h: maps[pl.ds((y * 4 + part * 2 + c) * 2 + h, 64, stride=40), :]
+        )
+
+    def image_of(part):
+        return halves(lambda y, h: rows[y, pl.ds(part * 2 + h, 64, stride=4), :])
 
     def transform(pairs, side):
         for c in range(2):
@@ -319,7 +310,7 @@
             for c in range(2)
         ]
 
-    vr, vi = image_of(0, 0), image_of(0, 1)
+    vr, vi = image_of(0), image_of(1)
     pairs = []
     for c in range(2):
         sr, si = map_of(0, c), map_of(1, c)
@@ -343,14 +334,9 @@
         back_re = back_re + sr * xr + si * xi
         back_im = back_im + sr * xi - si * xr
     back = (back_re, back_im)
-    product = jnp.sum(
-        back_re * image_of(1, 0) + back_im * image_of(1, 1), axis=0, keepdims=True
-    )
-    product = product[:, :128] + product[:, 128:]
     for out in (kept, sent):
         for t in range(2):
             out[t, 256:280] = extra[...]
-            out[t, 278:279] = -product
     for a in range(4):
         @pl.when(here == a)
         def _():
@@ -358,13 +344,10 @@
                 place = slot(a, q)
                 out = sent if place >= 2 else kept
                 for part in range(2):
-                    for y in range(4):
-                        for h in range(2):
-                            first = (part * 4 + y) * 2 + h
-                            out[place % 2, pl.ds(first, 16, stride=16), :] = back[part][
-                                q * 64 + y * 16 : q * 64 + y * 16 + 16,
-                                h * 128 : h * 128 + 128,
-                            ]
+                    for h in range(2):
+                        out[place % 2, pl.ds(part * 2 + h, 64, stride=4), :] = back[
+                            part
+                        ][q * 64 : q * 64 + 64, h * 128 : h * 128 + 128]
 
 
 def transform_call(coil, maps, pieces, kspace, mask, extra):
@@ -375,7 +358,7 @@
         in_specs=[pl.BlockSpec(memory_space=pltpu.SMEM)] + [vm] * 9,
         out_specs=(vm,) * 2,
         scratch_shapes=[
-            pltpu.VMEM((4, 512, 128), F32),
+            pltpu.VMEM((4, 256, 128), F32),
             pltpu.VMEM((2, 512, 512), BF),
             pltpu.VMEM((4, 512, 512), BF),
             pltpu.VMEM((2, 512, 512), BF),
@@ -419,16 +402,12 @@
     slab_count = lax.axis_size("slab")
     coil = lax.axis_index("coil")
     slab = lax.axis_index("slab")
-    images = jnp.stack([init_image, recon_cotangent]).reshape(2, 2, 4, 2, 2, 4, 256)
-    images = images.transpose(2, 4, 3, 0, 1, 5, 6)
-    images = turned_by_core(images, coil, 0, -1).reshape(16, 32, 128)
-    images = lax.all_to_all(
-        images, "slab", split_axis=0, concat_axis=0, tiled=True,
-        axis_index_groups=GROUPS,
-    )
-    maps = sens.transpose(2, 3, 0, 1, 4).reshape(64, 32, 128)
-    maps, images = lax.optimization_barrier((maps, images))
-    received = lax.all_to_all(maps, "slab", split_axis=0, concat_axis=0, tiled=True)
+    maps = sens.transpose(2, 3, 0, 1, 4).reshape(64, 16, 2, 128)
+    images = jnp.stack([init_image, recon_cotangent]).reshape(2, 2, 4, 4, 2, 2, 256)
+    images = images.transpose(4, 2, 5, 3, 0, 1, 6)
+    images = turned_by_core(images, coil, 1, -1).reshape(64, 4, 2, 128)
+    payload = jnp.concatenate([maps, images], axis=1)
+    received = lax.all_to_all(payload, "slab", split_axis=0, concat_axis=0, tiled=True)
 
     before, after, lower, upper = halos(init_image, recon_cotangent, slab_count)
     wide, turned = filter_tables(weights)
@@ -436,37 +415,43 @@
     packed, sums = conv_call(
         init_image, recon_cotangent, before, after, lower, upper, wide
     )
-    extra = jnp.pad(-diagonal(sums).reshape(2592), (0, 480)).reshape(24, 128)
-
-    held = images.reshape(512, 128)
+    extra = jnp.pad(-diagonal(sums).reshape(4, 648), ((0, 0), (0, 120)))
+    extra = extra.reshape(24, 128)
+
+    held = received[:, 16:18].reshape(256, 128)
     pieces = [lax.ppermute(held, AXES, far_pairs(turn)) for turn in range(2)]
     pieces = pieces + [lax.ppermute(piece, "coil", CORES) for piece in pieces]
     kept, sent = transform_call(
-        coil.reshape(1), received.reshape(2048, 128), pieces, kspace[:, :, 0], mask,
+        coil.reshape(1), received.reshape(2560, 128), pieces, kspace[:, :, 0], mask,
         extra,
     )
     kept = kept + lax.ppermute(sent, "coil", CORES)
     total = lax.ppermute(kept[0], AXES, back_pairs(0)) + lax.ppermute(
         kept[1], AXES, back_pairs(1)
     )
-    rider = jnp.broadcast_to(total[None, 256:], (16, 24, 128))
-    sent = jnp.concatenate([total[:256].reshape(16, 16, 128), rider], axis=1)
-    arrived = lax.all_to_all(
-        sent, "slab", split_axis=0, concat_axis=0, tiled=True,
-        axis_index_groups=GROUPS,
-    )
+    product = jnp.sum(total[:256] * received[:, 18:20].reshape(256, 128))
+    quarter = slab // 32 * 2 + slab // 4 % 2
+    rider = lax.dynamic_slice_in_dim(total, 256 + 6 * quarter, 6, axis=0)
+    corner = np.zeros((6, 128), np.float32)
+    corner[5, 127] = 1.0
+    rider = rider - product * corner
+    rider = jnp.broadcast_to(rider.reshape(1, 3, 2, 128), (64, 3, 2, 128))
+    sent = jnp.concatenate([total[:256].reshape(64, 2, 2, 128), rider], axis=1)
+    arrived = lax.all_to_all(sent, "slab", split_axis=0, concat_axis=0, tiled=True)
     base = adjoint_call(edge, init_image, packed, wide, turned)
-    own = jnp.sum(arrived[:, 16:], axis=0)
+    own = jnp.sum(arrived[:, 2:].reshape(2, 4, 2, 4, 6, 128), axis=(1, 3))
+    own = own.reshape(24, 128)
     riders = own
     for turn in range(1, 4):
         riders = riders + lax.ppermute(
             own, "coil", [(i, (i + turn) % 4) for i in range(4)]
         )
-    combined = arrived[:, :16].reshape(4, 2, 2, 2, 4, 256)
-    combined = turned_by_core(combined, coil, 0, 1).transpose(3, 0, 2, 1, 4, 5)
+    combined = arrived[:, :2].reshape(2, 4, 2, 4, 2, 256)
+    combined = turned_by_core(combined, coil, 1, 1).transpose(4, 1, 3, 0, 2, 5)
     recon = base - step_sizes[0] * combined.reshape(2, 16, 4, 256)
-    step_grads = jnp.sum(riders[22])[None]
-    grads = riders[:21].reshape(2688)[:2592]
+    riders = riders.reshape(4, 768)
+    step_grads = jnp.sum(riders[:, 767])[None]
+    grads = riders[:, :648].reshape(2592)
     grads = grads.reshape(3, 3, 2, 3, 48).transpose(4, 2, 1, 3, 0)
     return recon, grads[None], step_grads
 

time: 146 us -> 129 us (0.88)
  waiting for transfers between devices: 28.6 us -> 18 us
  starting transfers between devices: 61.8 us -> 57.2 us
  Pallas kernels: 32.7 us -> 31.2 us
    ppermute x1, starting transfers between devices: 7.65 us -> 0.08 us  [on_device(): lax.ppermute(kept[1], AXES, back_pairs(1))]
    ppermute x2, waiting for transfers between devices: 9.82 us -> 4.33 us  [on_device(): pieces = [lax.ppermute(held, AXES, far_pairs(turn)) for turn in range(2)]]
    ppermute x2, starting transfers between devices: 3.78 us -> 8.1 us  [on_device(): pieces = [lax.ppermute(held, AXES, far_pairs(turn)) for turn in range(2)]]
    all_to_all x3 -> x2, starting transfers between devices: 24.9 us -> 20.6 us  [the longest x1 14.4 us: on_device(): lax.all_to_all(payload, 'slab', split_axis=0, concat_axis=0, tiled=True)]
    ppermute x2, starting transfers between devices: 0.01 us -> 4.21 us  [on_device(): pieces = pieces + [lax.ppermute(piece, 'coil', CORES) for piece in pieces]]
    all_to_all x3 -> x2, waiting for transfers between devices: 6.57 us -> 3.25 us  [the longest x1 3.25 us: on_device(): lax.all_to_all(payload, 'slab', split_axis=0, concat_axis=0, tiled=True)]
    concatenate x0 -> x1, local copies, waits for them, and re-layouts: none -> 1.56 us  [on_device(): payload = jnp.concatenate([maps, images], axis=1)]
  transfers between devices with their start and end apart: 17 -> 16, of which waited for: 8 -> 7; matrix products, arithmetic and copies ran while one was open for 9% -> 8% of each run, Pallas kernels for 16% -> 19%
where the time goes in v4:
time: 129 us; the launch traced here: 128 us
  starting transfers between devices  57.2 us (44%)
  Pallas kernels  31.2 us (24%)
  waiting for transfers between devices  18 us (14%)
  local copies, waits for them, and re-layouts  11.3 us (9%)
  other arithmetic  8.38 us (6%)
  between operations  2.11 us (2%)
    all_to_all x1, starting transfers between devices, on_device(): lax.all_to_all(payload, 'slab', split_axis=0, concat_axis=0, tiled=True)  14.4 us
    pallas_call x1, Pallas kernels, conv_call(): pl.pallas_call(conv_kernel, out_shape=(jax.ShapeDtypeStruct((3, 2, 320, 2...  12 us
    pallas_call x1, Pallas kernels, adjoint_call(): pl.pallas_call(adjoint_kernel, out_shape=jax.ShapeDtypeStruct((2, 16, 4,...  11.8 us
    ppermute x2, starting transfers between devices, on_device(): pieces = [lax.ppermute(held, AXES, far_pairs(turn)) for turn in range(2)]  8.1 us
    pallas_call x1, Pallas kernels, transform_call(): pl.pallas_call(transform_kernel, out_shape=tuple((jax.ShapeDtypeStruct((2...  7.44 us
    all_to_all x1, starting transfers between devices, on_device(): lax.all_to_all(sent, 'slab', split_axis=0, concat_axis=0, tiled=True)  6.27 us
    ppermute x3, starting transfers between devices, on_device(): lax.ppermute(own, 'coil', [(i, (i + turn) % 4) for i in range(4)])  6.23 us
    ppermute x1, starting transfers between devices, halos(): lower = lax.ppermute(planes(slice(14, 16), 15), 'coil', up)  5.76 us
  transfers between devices with their start and end apart: 16, of which 7 were waited for; matrix products, arithmetic and copies ran while one was open for 8% of the time, Pallas kernels for 19%

profile of v4, /device:TPU:1, one launch (start us, length us, event | category | flops | bytes accessed | tf_op | source)
XLA Modules:
  0.0 128.2 jit_solution(2169972482433239446)
XLA Ops:
  1.8 1.4 %fusion.13 = (f32[2,16,1,256]{3,2,1,0:T(1,128)S(1)}, f32[2,16,1,256]{3,2,1,0:T(1,128)S(1)}, f32[2,16,1,256]{3,2,1,0:T(1,128)S(1)}, f32[2,16,1,256]{3,2,1,0:T(1,128)S(1)}) fusion(f32[2,16,4,256]{3,2,1,0:T(4,128)} %init.3), kind=kLoop, calls=%fused_computation.65 | loop fusion | bytes 262144 | tf_op jit(solution)/shard_map/slice | solution.py:379
  3.2 4.0 %collective-permute-start = (f32[6,16,256]{2,1,0:T(8,128)S(1)}, f32[6,16,256]{2,1,0:T(8,128)S(1)}, u32[]{:S(2)}, u32[]{:S(2)}) collective-permute-start(f32[6,16,256]{2,1,0:T(8,128)S(1)} %pad_maximum_fusion.3), channel_id=1, source_target_pairs={{0,4},{4,8},{8,12},{12,16},{16,20},{20,24},{24,28},{28,32},{32,36}... | collective-permute-start | bytes 294920 | tf_op jit(solution)/shard_map/ppermute | solution.py:382
  7.2 1.3 %collective-permute-start.1 = (f32[6,16,256]{2,1,0:T(8,128)S(1)}, f32[6,16,256]{2,1,0:T(8,128)S(1)}, u32[]{:S(2)}, u32[]{:S(2)}) collective-permute-start(f32[6,16,256]{2,1,0:T(8,128)S(1)} %pad_maximum_fusion.4), channel_id=1, source_target_pairs={{4,0},{8,4},{12,8},{16,12},{20,16},{24,20},{28,24},{32,28},{36,32}... | collective-permute-start | bytes 294920 | tf_op jit(solution)/shard_map/ppermute | solution.py:383
  11.6 1.6 %copy.140 = f32[64,20,2,128]{3,2,1,0:T(2,128)} copy(f32[64,20,2,128]{3,2,0,1:T(2,128)S(1)} %pad_maximum_fusion) | data formatting | bytes 2621440 | tf_op jit(solution)/shard_map/concatenate | solution.py:409
  13.1 14.4 %all-to-all-start = ((f32[64,20,2,128]{3,2,1,0:T(2,128)}), f32[64,20,2,128]{3,2,1,0:T(2,128)S(1)}, u32[]{:S(2)}, u32[]{:S(2)}) async-start(f32[64,20,2,128]{3,2,1,0:T(2,128)} %copy.140), calls=%async_computation | async-start | bytes 2621440 | tf_op jit(solution)/shard_map/all_to_all | solution.py:410
  28.6 5.8 %collective-permute-start.2 = (f32[6,8,256]{2,1,0:T(8,128)S(1)}, f32[6,8,256]{2,1,0:T(8,128)S(1)}, u32[]{:S(2)}, u32[]{:S(2)}) collective-permute-start(f32[6,8,256]{2,1,0:T(8,128)S(1)} %pad_maximum_fusion.5), channel_id=1, source_target_pairs={{0,1},{1,2},{2,3},{4,5},{5,6},{6,7},{8,9},{9,10},{10,11},{12,13},{... | collective-permute-start | bytes 147464 | tf_op jit(solution)/shard_map/ppermute | solution.py:396
  34.4 1.9 %collective-permute-start.3 = (f32[6,8,256]{2,1,0:T(8,128)S(1)}, f32[6,8,256]{2,1,0:T(8,128)S(1)}, u32[]{:S(2)}, u32[]{:S(2)}) collective-permute-start(f32[6,8,256]{2,1,0:T(8,128)S(1)} %pad_maximum_fusion.6), channel_id=1, source_target_pairs={{1,0},{2,1},{3,2},{5,4},{6,5},{7,6},{9,8},{10,9},{11,10},{13,12},{... | collective-permute-start | bytes 147464 | tf_op jit(solution)/shard_map/ppermute | solution.py:397
  37.2 4.9 %collective-permute-done.3.upper = f32[6,8,256]{2,1,0:T(8,128)S(1)} collective-permute-done((f32[6,8,256]{2,1,0:T(8,128)S(1)}, f32[6,8,256]{2,1,0:T(8,128)S(1)}, u32[]{:S(2)}, u32[]{:S(2)}) %collective-permute-start.3) | collective-permute-done | bytes 49184 | tf_op jit(solution)/shard_map/ppermute | solution.py:397
  42.7 12.0 %shard_map.166 = (bf16[3,2,320,256]{3,2,1,0:T(8,128)(2,1)}, f32[144,192]{1,0:T(8,128)}) custom-call(f32[2,16,4,256]{3,2,1,0:T(4,128)} %init.3, f32[2,16,4,256]{3,2,1,0:T(4,128)} %grad.1, f32[6,16,256]{2,1,0:T(8,128)} %copy-done.6, f32[6,16,256]{2,1,0:T(8,128)} %copy-done.7, f32[6,8,256]{2,1,0:T(8,128)} %copy-done.19, f32[6,8,256]{2,1,0:T(8,128)} %copy-done.20, ...), custom_call_target="tpu_custom_call" | custom-call | flops 4000000000 | bytes 2000000 | tf_op jit(solution)/shard_map/pallas_call | solution.py:184
  55.9 3.2 %all-to-all-done = f32[64,20,2,128]{3,2,1,0:T(2,128)S(1)} async-done(((f32[64,20,2,128]{3,2,1,0:T(2,128)}), f32[64,20,2,128]{3,2,1,0:T(2,128)S(1)}, u32[]{:S(2)}, u32[]{:S(2)}) %all-to-all-start) | async-done | bytes 1310752 | tf_op jit(solution)/shard_map/all_to_all | solution.py:410
  59.2 6.2 %collective-permute-start.5 = (f32[256,128]{1,0:T(8,128)S(1)}, f32[256,128]{1,0:T(8,128)S(1)}, u32[]{:S(2)}, u32[]{:S(2)}) collective-permute-start(f32[256,128]{1,0:T(8,128)S(1)} %bitcast.122), channel_id=1, source_target_pairs={{96,2},{100,6},{104,10},{108,14},{0,18},{4,22},{8,26},{12,30},{32,... | collective-permute-start | bytes 393224 | tf_op jit(solution)/shard_map/ppermute | solution.py:422
  65.4 1.9 %collective-permute-start.4 = (f32[256,128]{1,0:T(8,128)S(1)}, f32[256,128]{1,0:T(8,128)S(1)}, u32[]{:S(2)}, u32[]{:S(2)}) collective-permute-start(f32[256,128]{1,0:T(8,128)S(1)} %bitcast.123), channel_id=1, source_target_pairs={{96,0},{100,4},{104,8},{108,12},{0,16},{4,20},{8,24},{12,28},{32,3... | collective-permute-start | bytes 393224 | tf_op jit(solution)/shard_map/ppermute | solution.py:422
  67.3 1.4 %collective-permute-done.5.p1 = f32[256,128]{1,0:T(8,128)S(1)} collective-permute-done((f32[256,128]{1,0:T(8,128)S(1)}, f32[256,128]{1,0:T(8,128)S(1)}, u32[]{:S(2)}, u32[]{:S(2)}) %collective-permute-start.5) | collective-permute-done | bytes 131104 | tf_op jit(solution)/shard_map/ppermute | solution.py:422
  69.9 2.9 %collective-permute-done.4.p0 = f32[256,128]{1,0:T(8,128)S(1)} collective-permute-done((f32[256,128]{1,0:T(8,128)S(1)}, f32[256,128]{1,0:T(8,128)S(1)}, u32[]{:S(2)}, u32[]{:S(2)}) %collective-permute-start.4) | collective-permute-done | bytes 131104 | tf_op jit(solution)/shard_map/ppermute | solution.py:422
  72.9 3.0 %collective-permute-start.6 = (f32[256,128]{1,0:T(8,128)S(1)}, f32[256,128]{1,0:T(8,128)S(1)}, u32[]{:S(2)}, u32[]{:S(2)}) collective-permute-start(f32[256,128]{1,0:T(8,128)S(1)} %collective-permute-done.4.p0), channel_id=1, source_target_pairs={{0,1},{1,0},{2,3},{3,2},{4,5},{5,4},{6,7},{7,6},{8,9},{9,8},{10,11... | collective-permute-start | bytes 393224 | tf_op jit(solution)/shard_map/ppermute | solution.py:423
  77.5 7.4 %shard_map.168 = (f32[2,280,128]{2,1,0:T(8,128)}, f32[2,280,128]{2,1,0:T(8,128)}) custom-call(s32[1]{0:T(128)} %bitcast.33.coil, f32[2560,128]{1,0:T(8,128)} %bitcast.112, f32[256,128]{1,0:T(8,128)} %copy-done.16, f32[256,128]{1,0:T(8,128)} %copy-done.15, f32[256,128]{1,0:T(8,128)} %copy-done.18, f32[256,128]{1,0:T(8,128)} %copy-done.17, ...), custom_call_target="tpu_custom_call" | custom-call | flops 6000000000 | bytes 5000000 | tf_op jit(solution)/shard_map/pallas_call | solution.py:355
  85.4 1.4 %collective-permute-done.8 = f32[2,280,128]{2,1,0:T(8,128)S(1)} collective-permute-done((f32[2,280,128]{2,1,0:T(8,128)}, f32[2,280,128]{2,1,0:T(8,128)S(1)}, u32[]{:S(2)}, u32[]{:S(2)}) %collective-permute-start.8) | collective-permute-done | bytes 286752 | tf_op jit(solution)/shard_map/ppermute | solution.py:428
  88.0 4.5 %collective-permute-start.9 = (f32[280,128]{1,0:T(8,128)S(1)}, f32[280,128]{1,0:T(8,128)S(1)}, u32[]{:S(2)}, u32[]{:S(2)}) collective-permute-start(f32[280,128]{1,0:T(8,128)S(1)} %get-tuple-element.37), channel_id=1, source_target_pairs={{0,96},{4,100},{8,104},{12,108},{16,0},{20,4},{24,8},{28,12},{32,3... | collective-permute-start | bytes 430088 | tf_op jit(solution)/shard_map/ppermute | solution.py:429
  92.7 3.9 %collective-permute-done.10 = f32[280,128]{1,0:T(8,128)S(1)} collective-permute-done((f32[280,128]{1,0:T(8,128)S(1)}, f32[280,128]{1,0:T(8,128)S(1)}, u32[]{:S(2)}, u32[]{:S(2)}) %collective-permute-start.10) | collective-permute-done | bytes 143392 | tf_op jit(solution)/shard_map/ppermute | solution.py:429
  98.9 6.3 %all-to-all-start.1 = ((f32[64,5,2,128]{3,2,1,0:T(2,128)}), f32[64,5,2,128]{3,2,1,0:T(2,128)S(1)}, u32[]{:S(2)}, u32[]{:S(2)}) async-start(f32[64,5,2,128]{3,2,1,0:T(2,128)} %pad_maximum_fusion.1), calls=%async_computation.1 | async-start | bytes 655360 | tf_op jit(solution)/shard_map/all_to_all | solution.py:440
  107.3 11.8 %shard_map.167 = f32[2,16,4,256]{3,2,1,0:T(4,128)} custom-call(f32[4]{0:T(128)} %add_convert_fusion.edge, f32[2,16,4,256]{3,2,1,0:T(4,128)} %init.3, bf16[3,2,320,256]{3,2,1,0:T(8,128)(2,1)} %get-tuple-element.7.xb, bf16[288,432]{1,0:T(8,128)(2,1)} %pad_maximum_fusion.2.wide, bf16[144,576]{1,0:T(8,128)(2,1)} %fusion.1.turned), custom_call_target="tpu_custom_call" | custom-call | flops 4000000000 | bytes 2000000 | tf_op jit(solution)/shard_map/pallas_call | solution.py:204
  119.2 3.0 %collective-permute-start.13 = (f32[24,128]{1,0:T(8,128)S(1)}, f32[24,128]{1,0:T(8,128)S(1)}, u32[]{:S(2)}, u32[]{:S(2)}) collective-permute-start(f32[24,128]{1,0:T(8,128)S(1)} %reshape.246), channel_id=1, source_target_pairs={{0,3},{1,0},{2,1},{3,2},{4,7},{5,4},{6,5},{7,6},{8,11},{9,8},{10,9... | collective-permute-start | bytes 36872 | tf_op jit(solution)/shard_map/ppermute | solution.py:446
  122.2 1.2 collective-permute-start.12
  123.5 2.0 %collective-permute-start.11 = (f32[24,128]{1,0:T(8,128)S(1)}, f32[24,128]{1,0:T(8,128)S(1)}, u32[]{:S(2)}, u32[]{:S(2)}) collective-permute-start(f32[24,128]{1,0:T(8,128)S(1)} %reshape.246), channel_id=1, source_target_pairs={{0,1},{1,2},{2,3},{3,0},{4,5},{5,6},{6,7},{7,4},{8,9},{9,10},{10,1... | collective-permute-start | bytes 36872 | tf_op jit(solution)/shard_map/ppermute | solution.py:446
  (139 shorter events, 18.7 us)
Async XLA Ops:
  3.2 25.2 %collective-permute-start = (f32[6,16,256]{2,1,0:T(8,128)S(1)}, f32[6,16,256]{2,1,0:T(8,128)S(1)}, u32[]{:S(2)}, u32[]{:S(2)}) collective-permute-start(f32[6,16,256]{2,1,0:T(8,128)S(1)} %pad_maximum_fusion.3), channel_id=1, source_target_pairs={{0,4},{4,8},{8,12},{12,16},{16,20},{20,24},{24,28},{28,32},{32,36}... | collective-permute-start | bytes 294920 | tf_op jit(solution)/shard_map/ppermute | solution.py:382
  7.2 21.2 %collective-permute-start.1 = (f32[6,16,256]{2,1,0:T(8,128)S(1)}, f32[6,16,256]{2,1,0:T(8,128)S(1)}, u32[]{:S(2)}, u32[]{:S(2)}) collective-permute-start(f32[6,16,256]{2,1,0:T(8,128)S(1)} %pad_maximum_fusion.4), channel_id=1, source_target_pairs={{4,0},{8,4},{12,8},{16,12},{20,16},{24,20},{28,24},{32,28},{36,32}... | collective-permute-start | bytes 294920 | tf_op jit(solution)/shard_map/ppermute | solution.py:383
  13.1 14.4 %copy-start.5 = (f32[1,48,2,3,3,3]{1,2,5,4,3,0:T(2,128)S(1)}, f32[1,48,2,3,3,3]{1,2,5,4,3,0:T(2,128)}, u32[]{:S(2)}) copy-start(f32[1,48,2,3,3,3]{1,2,5,4,3,0:T(2,128)} %param.19) | copy-start | bytes 31108
  13.1 14.4 %copy-start.8 = (f32[6,8]{0,1:T(8,128)S(1)}, f32[6,8]{0,1:T(8,128)}, u32[]{:S(2)}) copy-start(f32[6,8]{0,1:T(8,128)} %constant.86.clone) | copy-start | bytes 580
  13.1 14.4 %copy-start.9 = (f32[6,8]{0,1:T(8,128)S(1)}, f32[6,8]{0,1:T(8,128)}, u32[]{:S(2)}) copy-start(f32[6,8]{0,1:T(8,128)} %constant.85.clone) | copy-start | bytes 580
  13.1 14.5 %copy-start.10 = (f32[6,8]{0,1:T(8,128)S(1)}, f32[6,8]{0,1:T(8,128)}, u32[]{:S(2)}) copy-start(f32[6,8]{0,1:T(8,128)} %constant.84.clone) | copy-start | bytes 580
  13.1 46.0 %all-to-all-start = ((f32[64,20,2,128]{3,2,1,0:T(2,128)}), f32[64,20,2,128]{3,2,1,0:T(2,128)S(1)}, u32[]{:S(2)}, u32[]{:S(2)}) async-start(f32[64,20,2,128]{3,2,1,0:T(2,128)} %copy.140), calls=%async_computation | async-start | bytes 2621440 | tf_op jit(solution)/shard_map/all_to_all | solution.py:410
  28.4 13.7 %copy-start.6 = (f32[6,16,256]{2,1,0:T(8,128)}, f32[6,16,256]{2,1,0:T(8,128)S(1)}, u32[]{:S(2)}) copy-start(f32[6,16,256]{2,1,0:T(8,128)S(1)} %collective-permute-done.before) | copy-start | bytes 294916
  28.4 13.7 %copy-start.7 = (f32[6,16,256]{2,1,0:T(8,128)}, f32[6,16,256]{2,1,0:T(8,128)S(1)}, u32[]{:S(2)}) copy-start(f32[6,16,256]{2,1,0:T(8,128)S(1)} %collective-permute-done.1.after) | copy-start | bytes 294916
  28.6 8.7 %collective-permute-start.2 = (f32[6,8,256]{2,1,0:T(8,128)S(1)}, f32[6,8,256]{2,1,0:T(8,128)S(1)}, u32[]{:S(2)}, u32[]{:S(2)}) collective-permute-start(f32[6,8,256]{2,1,0:T(8,128)S(1)} %pad_maximum_fusion.5), channel_id=1, source_target_pairs={{0,1},{1,2},{2,3},{4,5},{5,6},{6,7},{8,9},{9,10},{10,11},{12,13},{... | collective-permute-start | bytes 147464 | tf_op jit(solution)/shard_map/ppermute | solution.py:396
  34.4 7.7 %collective-permute-start.3 = (f32[6,8,256]{2,1,0:T(8,128)S(1)}, f32[6,8,256]{2,1,0:T(8,128)S(1)}, u32[]{:S(2)}, u32[]{:S(2)}) collective-permute-start(f32[6,8,256]{2,1,0:T(8,128)S(1)} %pad_maximum_fusion.6), channel_id=1, source_target_pairs={{1,0},{2,1},{3,2},{5,4},{6,5},{7,6},{9,8},{10,9},{11,10},{13,12},{... | collective-permute-start | bytes 147464 | tf_op jit(solution)/shard_map/ppermute | solution.py:397
  59.2 17.7 %copy-start = (f32[64,20,2,128]{3,2,1,0:T(2,128)}, f32[64,20,2,128]{3,2,1,0:T(2,128)S(1)}, u32[]{:S(2)}) copy-start(f32[64,20,2,128]{3,2,1,0:T(2,128)S(1)} %all-to-all-done) | copy-start | bytes 3932164
  59.2 9.5 %collective-permute-start.5 = (f32[256,128]{1,0:T(8,128)S(1)}, f32[256,128]{1,0:T(8,128)S(1)}, u32[]{:S(2)}, u32[]{:S(2)}) collective-permute-start(f32[256,128]{1,0:T(8,128)S(1)} %bitcast.122), channel_id=1, source_target_pairs={{96,2},{100,6},{104,10},{108,14},{0,18},{4,22},{8,26},{12,30},{32,... | collective-permute-start | bytes 393224 | tf_op jit(solution)/shard_map/ppermute | solution.py:422
  65.4 7.5 %collective-permute-start.4 = (f32[256,128]{1,0:T(8,128)S(1)}, f32[256,128]{1,0:T(8,128)S(1)}, u32[]{:S(2)}, u32[]{:S(2)}) collective-permute-start(f32[256,128]{1,0:T(8,128)S(1)} %bitcast.123), channel_id=1, source_target_pairs={{96,0},{100,4},{104,8},{108,12},{0,16},{4,20},{8,24},{12,28},{32,3... | collective-permute-start | bytes 393224 | tf_op jit(solution)/shard_map/ppermute | solution.py:422
  68.7 7.9 %collective-permute-start.7 = (f32[256,128]{1,0:T(8,128)S(1)}, f32[256,128]{1,0:T(8,128)S(1)}, u32[]{:S(2)}, u32[]{:S(2)}) collective-permute-start(f32[256,128]{1,0:T(8,128)S(1)} %collective-permute-done.5.p1), channel_id=1, source_target_pairs={{0,1},{1,0},{2,3},{3,2},{4,5},{5,4},{6,7},{7,6},{8,9},{9,8},{10,11... | collective-permute-start | bytes 393224 | tf_op jit(solution)/shard_map/ppermute | solution.py:423
  72.9 4.0 %collective-permute-start.6 = (f32[256,128]{1,0:T(8,128)S(1)}, f32[256,128]{1,0:T(8,128)S(1)}, u32[]{:S(2)}, u32[]{:S(2)}) collective-permute-start(f32[256,128]{1,0:T(8,128)S(1)} %collective-permute-done.4.p0), channel_id=1, source_target_pairs={{0,1},{1,0},{2,3},{3,2},{4,5},{5,4},{6,7},{7,6},{8,9},{9,8},{10,11... | collective-permute-start | bytes 393224 | tf_op jit(solution)/shard_map/ppermute | solution.py:423
  85.0 1.9 %collective-permute-start.8 = (f32[2,280,128]{2,1,0:T(8,128)}, f32[2,280,128]{2,1,0:T(8,128)S(1)}, u32[]{:S(2)}, u32[]{:S(2)}) collective-permute-start(f32[2,280,128]{2,1,0:T(8,128)} %get-tuple-element.10), channel_id=1, source_target_pairs={{0,1},{1,0},{2,3},{3,2},{4,5},{5,4},{6,7},{7,6},{8,9},{9,8},{10,11... | collective-permute-start | bytes 860168 | tf_op jit(solution)/shard_map/ppermute | solution.py:428
  86.8 10.5 %copy-start.11 = (f32[6,128]{1,0:T(8,128)S(1)}, f32[6,128]{1,0:T(8,128)}, u32[]{:S(2)}) copy-start(f32[6,128]{1,0:T(8,128)} %constant.91.clone) | copy-start | bytes 9220
  87.9 8.8 %collective-permute-start.10 = (f32[280,128]{1,0:T(8,128)S(1)}, f32[280,128]{1,0:T(8,128)S(1)}, u32[]{:S(2)}, u32[]{:S(2)}) collective-permute-start(f32[280,128]{1,0:T(8,128)S(1)} %get-tuple-element.36), channel_id=1, source_target_pairs={{2,96},{6,100},{10,104},{14,108},{18,0},{22,4},{26,8},{30,12},{34,... | collective-permute-start | bytes 430088 | tf_op jit(solution)/shard_map/ppermute | solution.py:429
  88.0 8.7 %collective-permute-start.9 = (f32[280,128]{1,0:T(8,128)S(1)}, f32[280,128]{1,0:T(8,128)S(1)}, u32[]{:S(2)}, u32[]{:S(2)}) collective-permute-start(f32[280,128]{1,0:T(8,128)S(1)} %get-tuple-element.37), channel_id=1, source_target_pairs={{0,96},{4,100},{8,104},{12,108},{16,0},{20,4},{24,8},{28,12},{32,3... | collective-permute-start | bytes 430088 | tf_op jit(solution)/shard_map/ppermute | solution.py:429
  98.9 20.2 %all-to-all-start.1 = ((f32[64,5,2,128]{3,2,1,0:T(2,128)}), f32[64,5,2,128]{3,2,1,0:T(2,128)S(1)}, u32[]{:S(2)}, u32[]{:S(2)}) async-start(f32[64,5,2,128]{3,2,1,0:T(2,128)} %pad_maximum_fusion.1), calls=%async_computation.1 | async-start | bytes 655360 | tf_op jit(solution)/shard_map/all_to_all | solution.py:440
  119.2 7.5 %collective-permute-start.13 = (f32[24,128]{1,0:T(8,128)S(1)}, f32[24,128]{1,0:T(8,128)S(1)}, u32[]{:S(2)}, u32[]{:S(2)}) collective-permute-start(f32[24,128]{1,0:T(8,128)S(1)} %reshape.246), channel_id=1, source_target_pairs={{0,3},{1,0},{2,1},{3,2},{4,7},{5,4},{6,5},{7,6},{8,11},{9,8},{10,9... | collective-permute-start | bytes 36872 | tf_op jit(solution)/shard_map/ppermute | solution.py:446
  122.2 4.5 %collective-permute-start.12 = (f32[24,128]{1,0:T(8,128)S(1)}, f32[24,128]{1,0:T(8,128)S(1)}, u32[]{:S(2)}, u32[]{:S(2)}) collective-permute-start(f32[24,128]{1,0:T(8,128)S(1)} %reshape.246), channel_id=1, source_target_pairs={{0,2},{1,3},{2,0},{3,1},{4,6},{5,7},{6,4},{7,5},{8,10},{9,11},{10,... | collective-permute-start | bytes 36872 | tf_op jit(solution)/shard_map/ppermute | solution.py:446
  123.5 3.3 %collective-permute-start.11 = (f32[24,128]{1,0:T(8,128)S(1)}, f32[24,128]{1,0:T(8,128)S(1)}, u32[]{:S(2)}, u32[]{:S(2)}) collective-permute-start(f32[24,128]{1,0:T(8,128)S(1)} %reshape.246), channel_id=1, source_target_pairs={{0,1},{1,2},{2,3},{3,0},{4,5},{5,6},{6,7},{7,4},{8,9},{9,10},{10,1... | collective-permute-start | bytes 36872 | tf_op jit(solution)/shard_map/ppermute | solution.py:446
  (13 other events, 65.5 us)

commit v5 on v4

--- a/solution.py
+++ b/solution.py
@@ -34,6 +34,103 @@
 
 
 CORES = [(i, i ^ 1) for i in range(4)]
+
+
+VM = pl.BlockSpec(memory_space=pltpu.VMEM)
+SM = pl.BlockSpec(memory_space=pltpu.SMEM)
+
+
+def edge_kernel(odd, state, grad, near, next_pair):
+    for parity in range(2):
+        high, low = (near, next_pair) if parity == 0 else (next_pair, near)
+
+        @pl.when(odd[0] == parity)
+        def _():
+            for i in range(2):
+                for k in range(2):
+                    high[2 * k + i] = state[i, :, 2 + k, :]
+                    low[2 * k + i] = state[i, :, k, :]
+                high[4 + i] = grad[i, :, 3, :]
+                low[4 + i] = grad[i, :, 0, :]
+
+
+def edge_call(odd, state, grad):
+    shape = jax.ShapeDtypeStruct((6, 16, 256), F32)
+    return pl.pallas_call(
+        edge_kernel,
+        out_shape=(shape, shape),
+        in_specs=[SM, VM, VM],
+        out_specs=(VM, VM),
+        cost_estimate=pl.CostEstimate(
+            flops=0, bytes_accessed=460000, transcendentals=0
+        ),
+    )(odd, state, grad)
+
+
+def payload_kernel(coil, state, grad, maps, out):
+    core = coil[0] % 2
+    for part in range(2):
+        for c in range(2):
+            for r in range(64):
+                for h in range(2):
+                    first = r * 40 + (part * 2 + c) * 2 + h
+                    out[pl.ds(first, 4, stride=8), :] = maps[
+                        part, c, r, :, h * 128 : h * 128 + 128
+                    ]
+    for kind in range(2):
+        for core_here in range(2):
+            @pl.when(core == core_here)
+            def _():
+                field = (state, grad)[kind]
+                for part in range(2):
+                    for low in range(16):
+                        z = (low // 4 - 1 + 2 * core_here) % 4
+                        for h in range(2):
+                            first = (z * 8 + low % 4) * 40 + (16 + kind * 2 + part) * 2 + h
+                            rows = field[part, low, :, h * 128 : h * 128 + 128]
+                            out[pl.ds(first, 2, stride=160), :] = rows[:2]
+                            out[pl.ds(first + 1280, 2, stride=160), :] = rows[2:]
+
+
+def payload_call(coil, state, grad, maps):
+    return pl.pallas_call(
+        payload_kernel,
+        out_shape=jax.ShapeDtypeStruct((2560, 128), F32),
+        in_specs=[SM, VM, VM, VM],
+        out_specs=VM,
+        cost_estimate=pl.CostEstimate(
+            flops=0, bytes_accessed=2600000, transcendentals=0
+        ),
+    )(coil, state, grad, maps)
+
+
+def combine_kernel(quarter, one, two, grad, out):
+    product = 0.0
+    for k in range(4):
+        rows = pl.ds(k, 64, stride=4)
+        total = one[rows, :] + two[rows, :]
+        out[pl.ds(k, 64, stride=10), :] = total
+        product = product + total * grad[rows, :]
+    product = jnp.sum(product)
+    first = 256 + 6 * quarter[0]
+    lane = lax.broadcasted_iota(jnp.int32, (1, 128), 1)
+    for k in range(6):
+        rider = one[pl.ds(first + k, 1), :] + two[pl.ds(first + k, 1), :]
+        if k == 5:
+            rider = jnp.where(lane == 127, -product, rider)
+        out[pl.ds(4 + k, 64, stride=10), :] = jnp.broadcast_to(rider, (64, 128))
+
+
+def combine_call(quarter, one, two, grad):
+    return pl.pallas_call(
+        combine_kernel,
+        out_shape=jax.ShapeDtypeStruct((640, 128), F32),
+        in_specs=[SM, VM, VM, VM],
+        out_specs=VM,
+        cost_estimate=pl.CostEstimate(
+            flops=100000, bytes_accessed=800000, transcendentals=0
+        ),
+    )(quarter, one, two, grad)
 
 
 def turned_by_core(data, coil, axis, sign):
@@ -174,10 +271,6 @@
     ).reshape(16, 8, 256)
     for i in range(2):
         base[i] = init[i] - total[:, 4 * i : 4 * i + 4]
-
-
-VM = pl.BlockSpec(memory_space=pltpu.VMEM)
-SM = pl.BlockSpec(memory_space=pltpu.SMEM)
 
 
 def conv_call(init, grad, before, after, lower, upper, wide):
@@ -364,23 +457,26 @@
             pltpu.VMEM((2, 512, 512), BF),
             pltpu.VMEM((2, 512, 512), BF),
         ],
+        compiler_params=pltpu.CompilerParams(vmem_limit_bytes=32 << 20),
         cost_estimate=pl.CostEstimate(
             flops=6000000000, bytes_accessed=5000000, transcendentals=0
         ),
     )(coil, maps, *pieces, kspace, mask, extra, jnp.asarray(tables()))
 
 
+def swapped(first, second):
+    return [(first, second), (second, first)]
+
+
 def halos(state, grad, slab_count):
-    up = [(i, i + 1) for i in range(slab_count - 1)]
-    down = [(i + 1, i) for i in range(slab_count - 1)]
-
-    def pack(first, second, third):
-        return jnp.concatenate(
-            [state[:, :, first], state[:, :, second], grad[:, :, third]], axis=0
-        )
-
-    before = lax.ppermute(pack(2, 3, 3), "slab", up)
-    after = lax.ppermute(pack(0, 1, 0), "slab", down)
+    odd = lax.axis_index("slab") % 2
+    pairs = [p for i in range(0, slab_count, 2) for p in swapped(i, i + 1)]
+    others = [p for i in range(1, slab_count - 1, 2) for p in swapped(i, i + 1)]
+    near, far = edge_call(odd.reshape(1), state, grad)
+    near = lax.ppermute(near, "slab", pairs)
+    far = lax.ppermute(far, "slab", others)
+    before = jnp.where(odd == 0, far, near)
+    after = jnp.where(odd == 0, near, far)
 
     def planes(at, last):
         head = before[:4, at].reshape(2, 2, 2, 256).transpose(1, 2, 0, 3)
@@ -391,10 +487,12 @@
         )
         return jnp.concatenate([rows, jnp.pad(edge, ((0, 0), (0, 2), (0, 0)))], axis=0)
 
-    up = [(i, i + 1) for i in range(3)]
-    down = [(i + 1, i) for i in range(3)]
-    lower = lax.ppermute(planes(slice(14, 16), 15), "coil", up)
-    upper = lax.ppermute(planes(slice(0, 2), 0), "coil", down)
+    odd = lax.axis_index("coil") % 2
+    high, low = planes(slice(14, 16), 15), planes(slice(0, 2), 0)
+    near = lax.ppermute(jnp.where(odd == 0, high, low), "coil", CORES)
+    far = lax.ppermute(jnp.where(odd == 0, low, high), "coil", swapped(1, 2))
+    lower = jnp.where(odd == 0, far, near)
+    upper = jnp.where(odd == 0, near, far)
     return before, after, lower, upper
 
 
@@ -402,16 +500,14 @@
     slab_count = lax.axis_size("slab")
     coil = lax.axis_index("coil")
     slab = lax.axis_index("slab")
-    maps = sens.transpose(2, 3, 0, 1, 4).reshape(64, 16, 2, 128)
-    images = jnp.stack([init_image, recon_cotangent]).reshape(2, 2, 4, 4, 2, 2, 256)
-    images = images.transpose(4, 2, 5, 3, 0, 1, 6)
-    images = turned_by_core(images, coil, 1, -1).reshape(64, 4, 2, 128)
-    payload = jnp.concatenate([maps, images], axis=1)
+    payload = payload_call(coil.reshape(1), init_image, recon_cotangent, sens)
+    payload = payload.reshape(64, 20, 2, 128)
     received = lax.all_to_all(payload, "slab", split_axis=0, concat_axis=0, tiled=True)
 
     before, after, lower, upper = halos(init_image, recon_cotangent, slab_count)
     wide, turned = filter_tables(weights)
     edge = jnp.stack([slab > 0, slab < slab_count - 1, coil > 0, coil < 3]).astype(F32)
+    lower, wide, turned, edge = lax.optimization_barrier((lower, wide, turned, edge))
     packed, sums = conv_call(
         init_image, recon_cotangent, before, after, lower, upper, wide
     )
@@ -426,17 +522,12 @@
         extra,
     )
     kept = kept + lax.ppermute(sent, "coil", CORES)
-    total = lax.ppermute(kept[0], AXES, back_pairs(0)) + lax.ppermute(
-        kept[1], AXES, back_pairs(1)
-    )
-    product = jnp.sum(total[:256] * received[:, 18:20].reshape(256, 128))
+    parts = [lax.ppermute(kept[t], AXES, back_pairs(t)) for t in range(2)]
     quarter = slab // 32 * 2 + slab // 4 % 2
-    rider = lax.dynamic_slice_in_dim(total, 256 + 6 * quarter, 6, axis=0)
-    corner = np.zeros((6, 128), np.float32)
-    corner[5, 127] = 1.0
-    rider = rider - product * corner
-    rider = jnp.broadcast_to(rider.reshape(1, 3, 2, 128), (64, 3, 2, 128))
-    sent = jnp.concatenate([total[:256].reshape(64, 2, 2, 128), rider], axis=1)
+    sent = combine_call(
+        quarter.reshape(1), *parts, received[:, 18:20].reshape(256, 128)
+    )
+    sent = sent.reshape(64, 5, 2, 128)
     arrived = lax.all_to_all(sent, "slab", split_axis=0, concat_axis=0, tiled=True)
     base = adjoint_call(edge, init_image, packed, wide, turned)
     own = jnp.sum(arrived[:, 2:].reshape(2, 4, 2, 4, 6, 128), axis=(1, 3))
@@ -444,7 +535,7 @@
     riders = own
     for turn in range(1, 4):
         riders = riders + lax.ppermute(
-            own, "coil", [(i, (i + turn) % 4) for i in range(4)]
+            own, "coil", [(i, i ^ turn) for i in range(4)]
         )
     combined = arrived[:, :2].reshape(2, 4, 2, 4, 2, 256)
     combined = turned_by_core(combined, coil, 1, 1).transpose(4, 1, 3, 0, 2, 5)

time: 129 us -> 121 us (0.938)
  starting transfers between devices: 57.2 us -> 52.6 us
  local copies, waits for them, and re-layouts: 11.3 us -> 7.61 us
  other arithmetic: 8.38 us -> 5.03 us
  Pallas kernels: 31.2 us -> 34.3 us
  waiting for transfers between devices: 18 us -> 19.3 us
    pallas_call x0 -> x3, Pallas kernels: none -> 6.51 us  [the longest x1 2.89 us: payload_call(): pl.pallas_call(payload_kernel, out_shape=jax.ShapeDtypeStruct((2560, 128)...]
    pallas_call x1, Pallas kernels: 7.44 us -> 3.98 us  [transform_call(): pl.pallas_call(transform_kernel, out_shape=tuple((jax.ShapeDtypeStruct((2...]
    all_to_all x1, starting transfers between devices: 14.4 us -> 11.7 us  [on_device(): lax.all_to_all(payload, 'slab', split_axis=0, concat_axis=0, tiled=True)]
    ppermute x9, starting transfers between devices: 23.8 us -> 21.8 us  [the longest x3 6 us: on_device(): lax.ppermute(own, 'coil', [(i, i ^ turn) for i in range(4)])]
    slice x5 -> x1, local copies, waits for them, and re-layouts: 2.52 us -> 0.7 us  [on_device(): received[:, 18:20].reshape(256, 128)]
    concatenate x1 -> x0, local copies, waits for them, and re-layouts: 1.56 us -> none  [on_device(): payload = jnp.concatenate([maps, images], axis=1)]
    concatenate x6 -> x0, other arithmetic: 1.51 us -> none  [the longest x1 0.86 us: on_device(): sent = jnp.concatenate([total[:256].reshape(64, 2, 2, 128), rider], axis=1)]
    unnamed x45 -> x31, local copies, waits for them, and re-layouts: 2.77 us -> 2.81 us
  transfers between devices with their start and end apart: 16 -> 16, of which waited for: 7 -> 8; matrix products, arithmetic and copies ran while one was open for 8% -> 7% of each run, Pallas kernels for 19% -> 22%
where the time goes in v5:
time: 121 us
  starting transfers between devices  52.6 us (43%)
  Pallas kernels  34.3 us (28%)
  waiting for transfers between devices  19.3 us (16%)
  local copies, waits for them, and re-layouts  7.61 us (6%)
  other arithmetic  5.03 us (4%)
  between operations  1.85 us (2%)
    pallas_call x1, Pallas kernels, conv_call(): pl.pallas_call(conv_kernel, out_shape=(jax.ShapeDtypeStruct((3, 2, 320, 2...  12 us
    pallas_call x1, Pallas kernels, adjoint_call(): pl.pallas_call(adjoint_kernel, out_shape=jax.ShapeDtypeStruct((2, 16, 4,...  11.8 us
    all_to_all x1, starting transfers between devices, on_device(): lax.all_to_all(payload, 'slab', split_axis=0, concat_axis=0, tiled=True)  11.7 us
    ppermute x2, starting transfers between devices, on_device(): pieces = [lax.ppermute(held, AXES, far_pairs(turn)) for turn in range(2)]  8.02 us
    all_to_all x1, starting transfers between devices, on_device(): lax.all_to_all(sent, 'slab', split_axis=0, concat_axis=0, tiled=True)  6.21 us
    ppermute x3, starting transfers between devices, on_device(): lax.ppermute(own, 'coil', [(i, i ^ turn) for i in range(4)])  6 us
    ppermute x1, starting transfers between devices, halos(): near = lax.ppermute(near, 'slab', pairs)  4.74 us
    ppermute x2, starting transfers between devices, on_device(): parts = [lax.ppermute(kept[t], AXES, back_pairs(t)) for t in range(2)]  4.56 us
  transfers between devices with their start and end apart: 16, of which 8 were waited for; matrix products, arithmetic and copies ran while one was open for 7% of the time, Pallas kernels for 22%

profile of v5, /device:TPU:1, one launch (start us, length us, event | category | flops | bytes accessed | tf_op | source)
XLA Modules:
  0.0 120.6 jit_solution(16830188441585944070)
XLA Ops:
  0.6 1.7 %shard_map.157 = (f32[6,16,256]{2,1,0:T(8,128)}, f32[6,16,256]{2,1,0:T(8,128)}) custom-call(s32[1]{0:T(128)} %bitcast.odd, f32[2,16,4,256]{3,2,1,0:T(4,128)} %state.3, f32[2,16,4,256]{3,2,1,0:T(4,128)} %grad.5), custom_call_target="tpu_custom_call" | custom-call | bytes 460000 | tf_op jit(solution)/shard_map/pallas_call | solution.py:59
  3.0 4.7 %collective-permute-start.1 = (f32[6,16,256]{2,1,0:T(8,128)}, f32[6,16,256]{2,1,0:T(8,128)S(1)}, u32[]{:S(2)}, u32[]{:S(2)}) collective-permute-start(f32[6,16,256]{2,1,0:T(8,128)} %get-tuple-element.14), channel_id=1, source_target_pairs={{0,4},{4,0},{8,12},{12,8},{16,20},{20,16},{24,28},{28,24},{32,36},... | collective-permute-start | bytes 294920 | tf_op jit(solution)/shard_map/ppermute | solution.py:476
  7.8 2.9 %shard_map.160 = f32[2560,128]{1,0:T(8,128)} custom-call(s32[1]{0:T(128)} %bitcast.29.coil, f32[2,16,4,256]{3,2,1,0:T(4,128)} %state.3, f32[2,16,4,256]{3,2,1,0:T(4,128)} %grad.5, f32[2,2,64,4,256]{4,3,2,1,0:T(4,128)} %maps.1), custom_call_target="tpu_custom_call" | custom-call | bytes 2600000 | tf_op jit(solution)/shard_map/pallas_call | solution.py:96
  10.7 11.7 %all-to-all-start = ((f32[64,20,2,128]{3,2,1,0:T(2,128)}), f32[64,20,2,128]{3,2,1,0:T(2,128)S(1)}, u32[]{:S(2)}, u32[]{:S(2)}) async-start(f32[64,20,2,128]{3,2,1,0:T(2,128)} %bitcast.94), calls=%async_computation | async-start | bytes 2621440 | tf_op jit(solution)/shard_map/all_to_all | solution.py:505
  26.9 1.6 %collective-permute-start.3 = (f32[6,8,256]{2,1,0:T(8,128)S(1)}, f32[6,8,256]{2,1,0:T(8,128)S(1)}, u32[]{:S(2)}, u32[]{:S(2)}) collective-permute-start(f32[6,8,256]{2,1,0:T(8,128)S(1)} %get-tuple-element.67), channel_id=1, source_target_pairs={{0,1},{1,0},{2,3},{3,2},{4,5},{5,4},{6,7},{7,6},{8,9},{9,8},{10,11... | collective-permute-start | bytes 147464 | tf_op jit(solution)/shard_map/ppermute | solution.py:492
  28.5 4.3 %collective-permute-start.2 = (f32[6,8,256]{2,1,0:T(8,128)S(1)}, f32[6,8,256]{2,1,0:T(8,128)S(1)}, u32[]{:S(2)}, u32[]{:S(2)}) collective-permute-start(f32[6,8,256]{2,1,0:T(8,128)S(1)} %get-tuple-element.68), channel_id=1, source_target_pairs={{1,2},{2,1},{5,6},{6,5},{9,10},{10,9},{13,14},{14,13},{17,18},{18,... | collective-permute-start | bytes 147464 | tf_op jit(solution)/shard_map/ppermute | solution.py:493
  33.4 2.9 %collective-permute-done.2 = f32[6,8,256]{2,1,0:T(8,128)S(1)} collective-permute-done((f32[6,8,256]{2,1,0:T(8,128)S(1)}, f32[6,8,256]{2,1,0:T(8,128)S(1)}, u32[]{:S(2)}, u32[]{:S(2)}) %collective-permute-start.2) | collective-permute-done | bytes 49184 | tf_op jit(solution)/shard_map/ppermute | solution.py:493
  36.9 12.0 %shard_map.158 = (bf16[3,2,320,256]{3,2,1,0:T(8,128)(2,1)}, f32[144,192]{1,0:T(8,128)}) custom-call(f32[2,16,4,256]{3,2,1,0:T(4,128)} %state.3, f32[2,16,4,256]{3,2,1,0:T(4,128)} %grad.5, f32[6,16,256]{2,1,0:T(8,128)} %copy-done.3, f32[6,16,256]{2,1,0:T(8,128)} %copy-done.4, f32[6,8,256]{2,1,0:T(8,128)} %get-tuple-element.16.lower, ...), custom_call_target="tpu_custom_call" | custom-call | flops 4000000000 | bytes 2000000 | tf_op jit(solution)/shard_map/pallas_call | solution.py:277
  50.3 3.8 %all-to-all-done = f32[64,20,2,128]{3,2,1,0:T(2,128)S(1)} async-done(((f32[64,20,2,128]{3,2,1,0:T(2,128)}), f32[64,20,2,128]{3,2,1,0:T(2,128)S(1)}, u32[]{:S(2)}, u32[]{:S(2)}) %all-to-all-start) | async-done | bytes 1310752 | tf_op jit(solution)/shard_map/all_to_all | solution.py:505
  54.7 6.1 %collective-permute-start.5 = (f32[256,128]{1,0:T(8,128)S(1)}, f32[256,128]{1,0:T(8,128)S(1)}, u32[]{:S(2)}, u32[]{:S(2)}) collective-permute-start(f32[256,128]{1,0:T(8,128)S(1)} %bitcast.101), channel_id=1, source_target_pairs={{96,2},{100,6},{104,10},{108,14},{0,18},{4,22},{8,26},{12,30},{32,... | collective-permute-start | bytes 393224 | tf_op jit(solution)/shard_map/ppermute | solution.py:518
  60.8 1.9 %collective-permute-start.4 = (f32[256,128]{1,0:T(8,128)S(1)}, f32[256,128]{1,0:T(8,128)S(1)}, u32[]{:S(2)}, u32[]{:S(2)}) collective-permute-start(f32[256,128]{1,0:T(8,128)S(1)} %bitcast.102), channel_id=1, source_target_pairs={{96,0},{100,4},{104,8},{108,12},{0,16},{4,20},{8,24},{12,28},{32,3... | collective-permute-start | bytes 393224 | tf_op jit(solution)/shard_map/ppermute | solution.py:518
  62.8 1.4 %collective-permute-done.5.p1 = f32[256,128]{1,0:T(8,128)S(1)} collective-permute-done((f32[256,128]{1,0:T(8,128)S(1)}, f32[256,128]{1,0:T(8,128)S(1)}, u32[]{:S(2)}, u32[]{:S(2)}) %collective-permute-start.5) | collective-permute-done | bytes 131104 | tf_op jit(solution)/shard_map/ppermute | solution.py:518
  64.2 1.2 %collective-permute-start.7 = (f32[256,128]{1,0:T(8,128)S(1)}, f32[256,128]{1,0:T(8,128)S(1)}, u32[]{:S(2)}, u32[]{:S(2)}) collective-permute-start(f32[256,128]{1,0:T(8,128)S(1)} %collective-permute-done.5.p1), channel_id=1, source_target_pairs={{0,1},{1,0},{2,3},{3,2},{4,5},{5,4},{6,7},{7,6},{8,9},{9,8},{10,11... | collective-permute-start | bytes 393224 | tf_op jit(solution)/shard_map/ppermute | solution.py:519
  65.4 2.9 %collective-permute-done.4.p0 = f32[256,128]{1,0:T(8,128)S(1)} collective-permute-done((f32[256,128]{1,0:T(8,128)S(1)}, f32[256,128]{1,0:T(8,128)S(1)}, u32[]{:S(2)}, u32[]{:S(2)}) %collective-permute-start.4) | collective-permute-done | bytes 131104 | tf_op jit(solution)/shard_map/ppermute | solution.py:518
  68.3 3.0 %collective-permute-start.6 = (f32[256,128]{1,0:T(8,128)S(1)}, f32[256,128]{1,0:T(8,128)S(1)}, u32[]{:S(2)}, u32[]{:S(2)}) collective-permute-start(f32[256,128]{1,0:T(8,128)S(1)} %collective-permute-done.4.p0), channel_id=1, source_target_pairs={{0,1},{1,0},{2,3},{3,2},{4,5},{5,4},{6,7},{7,6},{8,9},{9,8},{10,11... | collective-permute-start | bytes 393224 | tf_op jit(solution)/shard_map/ppermute | solution.py:519
  72.3 1.4 %copy-done.2 = bf16[12,256,256]{2,1,0:T(8,128)(2,1)S(1)} copy-done((bf16[12,256,256]{2,1,0:T(8,128)(2,1)S(1)}, bf16[12,256,256]{2,1,0:T(8,128)(2,1)}, u32[]{:S(2)}) %copy-start.2) | copy-done | bytes 1572888
  73.7 4.0 %shard_map.161 = (f32[2,280,128]{2,1,0:T(8,128)S(1)}, f32[2,280,128]{2,1,0:T(8,128)S(1)}) custom-call(s32[1]{0:T(128)} %bitcast.29.coil, f32[2560,128]{1,0:T(8,128)S(1)} %bitcast.92, f32[256,128]{1,0:T(8,128)S(1)} %collective-permute-done.4.p0, f32[256,128]{1,0:T(8,128)S(1)} %collective-permute-done.5.p1, f32[256,128]{1,0:T(8,128)S(1)} %collective-permute-done.6.p2, ...), custom_call_target="tpu_custom_call" | custom-call | flops 6000000000 | bytes 5000000 | tf_op jit(solution)/shard_map/pallas_call | solution.py:448
  79.7 4.5 %collective-permute-start.9 = (f32[280,128]{1,0:T(8,128)S(1)}, f32[280,128]{1,0:T(8,128)S(1)}, u32[]{:S(2)}, u32[]{:S(2)}) collective-permute-start(f32[280,128]{1,0:T(8,128)S(1)} %get-tuple-element.52), channel_id=1, source_target_pairs={{0,96},{4,100},{8,104},{12,108},{16,0},{20,4},{24,8},{28,12},{32,3... | collective-permute-start | bytes 430088 | tf_op jit(solution)/shard_map/ppermute | solution.py:525
  84.2 4.2 %collective-permute-done.10.two = f32[280,128]{1,0:T(8,128)S(1)} collective-permute-done((f32[280,128]{1,0:T(8,128)S(1)}, f32[280,128]{1,0:T(8,128)S(1)}, u32[]{:S(2)}, u32[]{:S(2)}) %collective-permute-start.10) | collective-permute-done | bytes 143392 | tf_op jit(solution)/shard_map/ppermute | solution.py:525
  89.1 1.9 %shard_map.162 = f32[640,128]{1,0:T(8,128)} custom-call(s32[1]{0:T(128)} %bitcast.28.quarter, f32[280,128]{1,0:T(8,128)} %copy-done.6, f32[280,128]{1,0:T(8,128)} %copy-done.5, f32[256,128]{1,0:T(8,128)} %bitcast.97), custom_call_target="tpu_custom_call" | custom-call | flops 100000 | bytes 800000 | tf_op jit(solution)/shard_map/pallas_call | solution.py:125
  91.0 6.2 %all-to-all-start.1 = ((f32[64,5,2,128]{3,2,1,0:T(2,128)}), f32[64,5,2,128]{3,2,1,0:T(2,128)S(1)}, u32[]{:S(2)}, u32[]{:S(2)}) async-start(f32[64,5,2,128]{3,2,1,0:T(2,128)} %bitcast.95), calls=%async_computation.1 | async-start | bytes 655360 | tf_op jit(solution)/shard_map/all_to_all | solution.py:531
  97.9 11.8 %shard_map.159 = f32[2,16,4,256]{3,2,1,0:T(4,128)} custom-call(f32[4]{0:T(128)} %add_convert_fusion.edge, f32[2,16,4,256]{3,2,1,0:T(4,128)} %state.3, bf16[3,2,320,256]{3,2,1,0:T(8,128)(2,1)} %get-tuple-element.18.xb, bf16[288,432]{1,0:T(8,128)(2,1)} %pad_maximum_fusion.wide, bf16[144,576]{1,0:T(8,128)(2,1)} %fusion.1.turned), custom_call_target="tpu_custom_call" | custom-call | flops 4000000000 | bytes 2000000 | tf_op jit(solution)/shard_map/pallas_call | solution.py:297
  109.8 5.3 %collective-permute-start.13 = (f32[24,128]{1,0:T(8,128)S(1)}, f32[24,128]{1,0:T(8,128)S(1)}, u32[]{:S(2)}, u32[]{:S(2)}) collective-permute-start(f32[24,128]{1,0:T(8,128)S(1)} %reshape.243), channel_id=1, source_target_pairs={{0,3},{1,2},{2,1},{3,0},{4,7},{5,6},{6,5},{7,4},{8,11},{9,10},{10,... | collective-permute-start | bytes 36872 | tf_op jit(solution)/shard_map/ppermute | solution.py:537
  117.1 2.1 %collective-permute-done.12 = f32[24,128]{1,0:T(8,128)S(1)} collective-permute-done((f32[24,128]{1,0:T(8,128)S(1)}, f32[24,128]{1,0:T(8,128)S(1)}, u32[]{:S(2)}, u32[]{:S(2)}) %collective-permute-start.12) | collective-permute-done | bytes 12320 | tf_op jit(solution)/shard_map/ppermute | solution.py:537
  (102 shorter events, 15.3 us)
Async XLA Ops:
  2.4 24.3 %collective-permute-start = (f32[6,16,256]{2,1,0:T(8,128)}, f32[6,16,256]{2,1,0:T(8,128)S(1)}, u32[]{:S(2)}, u32[]{:S(2)}) collective-permute-start(f32[6,16,256]{2,1,0:T(8,128)} %get-tuple-element.13), channel_id=1, source_target_pairs={{4,8},{8,4},{12,16},{16,12},{20,24},{24,20},{28,32},{32,28},{36,40... | collective-permute-start | bytes 294920 | tf_op jit(solution)/shard_map/ppermute | solution.py:477
  3.0 23.7 %collective-permute-start.1 = (f32[6,16,256]{2,1,0:T(8,128)}, f32[6,16,256]{2,1,0:T(8,128)S(1)}, u32[]{:S(2)}, u32[]{:S(2)}) collective-permute-start(f32[6,16,256]{2,1,0:T(8,128)} %get-tuple-element.14), channel_id=1, source_target_pairs={{0,4},{4,0},{8,12},{12,8},{16,20},{20,16},{24,28},{28,24},{32,36},... | collective-permute-start | bytes 294920 | tf_op jit(solution)/shard_map/ppermute | solution.py:476
  10.6 13.2 %copy-start.8 = (f32[1,48,2,3,3,3]{1,2,5,4,3,0:T(2,128)S(1)}, f32[1,48,2,3,3,3]{1,2,5,4,3,0:T(2,128)}, u32[]{:S(2)}) copy-start(f32[1,48,2,3,3,3]{1,2,5,4,3,0:T(2,128)} %param.18) | copy-start | bytes 31108
  10.6 13.3 %copy-start.9 = (f32[6,8]{0,1:T(8,128)S(1)}, f32[6,8]{0,1:T(8,128)}, u32[]{:S(2)}) copy-start(f32[6,8]{0,1:T(8,128)} %constant.81.clone) | copy-start | bytes 580
  10.6 13.3 %copy-start.10 = (f32[6,8]{0,1:T(8,128)S(1)}, f32[6,8]{0,1:T(8,128)}, u32[]{:S(2)}) copy-start(f32[6,8]{0,1:T(8,128)} %constant.80.clone) | copy-start | bytes 580
  10.6 13.3 %copy-start.11 = (f32[6,8]{0,1:T(8,128)S(1)}, f32[6,8]{0,1:T(8,128)}, u32[]{:S(2)}) copy-start(f32[6,8]{0,1:T(8,128)} %constant.79.clone) | copy-start | bytes 580
  10.7 43.4 %all-to-all-start = ((f32[64,20,2,128]{3,2,1,0:T(2,128)}), f32[64,20,2,128]{3,2,1,0:T(2,128)S(1)}, u32[]{:S(2)}, u32[]{:S(2)}) async-start(f32[64,20,2,128]{3,2,1,0:T(2,128)} %bitcast.94), calls=%async_computation | async-start | bytes 2621440 | tf_op jit(solution)/shard_map/all_to_all | solution.py:505
  26.7 10.2 %copy-start.3 = (f32[6,16,256]{2,1,0:T(8,128)}, f32[6,16,256]{2,1,0:T(8,128)S(1)}, u32[]{:S(2)}) copy-start(f32[6,16,256]{2,1,0:T(8,128)S(1)} %get-tuple-element.53.before) | copy-start | bytes 294916
  26.7 10.2 %copy-start.4 = (f32[6,16,256]{2,1,0:T(8,128)}, f32[6,16,256]{2,1,0:T(8,128)S(1)}, u32[]{:S(2)}) copy-start(f32[6,16,256]{2,1,0:T(8,128)S(1)} %get-tuple-element.54.after) | copy-start | bytes 294916
  26.9 6.4 %collective-permute-start.3 = (f32[6,8,256]{2,1,0:T(8,128)S(1)}, f32[6,8,256]{2,1,0:T(8,128)S(1)}, u32[]{:S(2)}, u32[]{:S(2)}) collective-permute-start(f32[6,8,256]{2,1,0:T(8,128)S(1)} %get-tuple-element.67), channel_id=1, source_target_pairs={{0,1},{1,0},{2,3},{3,2},{4,5},{5,4},{6,7},{7,6},{8,9},{9,8},{10,11... | collective-permute-start | bytes 147464 | tf_op jit(solution)/shard_map/ppermute | solution.py:492
  28.5 7.7 %collective-permute-start.2 = (f32[6,8,256]{2,1,0:T(8,128)S(1)}, f32[6,8,256]{2,1,0:T(8,128)S(1)}, u32[]{:S(2)}, u32[]{:S(2)}) collective-permute-start(f32[6,8,256]{2,1,0:T(8,128)S(1)} %get-tuple-element.68), channel_id=1, source_target_pairs={{1,2},{2,1},{5,6},{6,5},{9,10},{10,9},{13,14},{14,13},{17,18},{18,... | collective-permute-start | bytes 147464 | tf_op jit(solution)/shard_map/ppermute | solution.py:493
  48.9 23.4 %copy-start = (f32[2,2,1,256,256]{4,3,2,1,0:T(8,128)S(1)}, f32[2,2,1,256,256]{4,3,2,1,0:T(8,128)}, u32[]{:S(2)}) copy-start(f32[2,2,1,256,256]{4,3,2,1,0:T(8,128)} %param.16) | copy-start | bytes 3145732
  48.9 23.4 %copy-start.1 = (s32[256,256]{1,0:T(8,128)S(1)}, s32[256,256]{1,0:T(8,128)}, u32[]{:S(2)}) copy-start(s32[256,256]{1,0:T(8,128)} %mask.1) | copy-start | bytes 786436
  54.7 9.4 %collective-permute-start.5 = (f32[256,128]{1,0:T(8,128)S(1)}, f32[256,128]{1,0:T(8,128)S(1)}, u32[]{:S(2)}, u32[]{:S(2)}) collective-permute-start(f32[256,128]{1,0:T(8,128)S(1)} %bitcast.101), channel_id=1, source_target_pairs={{96,2},{100,6},{104,10},{108,14},{0,18},{4,22},{8,26},{12,30},{32,... | collective-permute-start | bytes 393224 | tf_op jit(solution)/shard_map/ppermute | solution.py:518
  60.8 7.5 %collective-permute-start.4 = (f32[256,128]{1,0:T(8,128)S(1)}, f32[256,128]{1,0:T(8,128)S(1)}, u32[]{:S(2)}, u32[]{:S(2)}) collective-permute-start(f32[256,128]{1,0:T(8,128)S(1)} %bitcast.102), channel_id=1, source_target_pairs={{96,0},{100,4},{104,8},{108,12},{0,16},{4,20},{8,24},{12,28},{32,3... | collective-permute-start | bytes 393224 | tf_op jit(solution)/shard_map/ppermute | solution.py:518
  64.2 7.3 %collective-permute-start.7 = (f32[256,128]{1,0:T(8,128)S(1)}, f32[256,128]{1,0:T(8,128)S(1)}, u32[]{:S(2)}, u32[]{:S(2)}) collective-permute-start(f32[256,128]{1,0:T(8,128)S(1)} %collective-permute-done.5.p1), channel_id=1, source_target_pairs={{0,1},{1,0},{2,3},{3,2},{4,5},{5,4},{6,7},{7,6},{8,9},{9,8},{10,11... | collective-permute-start | bytes 393224 | tf_op jit(solution)/shard_map/ppermute | solution.py:519
  68.3 4.0 %collective-permute-start.6 = (f32[256,128]{1,0:T(8,128)S(1)}, f32[256,128]{1,0:T(8,128)S(1)}, u32[]{:S(2)}, u32[]{:S(2)}) collective-permute-start(f32[256,128]{1,0:T(8,128)S(1)} %collective-permute-done.4.p0), channel_id=1, source_target_pairs={{0,1},{1,0},{2,3},{3,2},{4,5},{5,4},{6,7},{7,6},{8,9},{9,8},{10,11... | collective-permute-start | bytes 393224 | tf_op jit(solution)/shard_map/ppermute | solution.py:519
  77.7 1.8 %collective-permute-start.8 = (f32[2,280,128]{2,1,0:T(8,128)S(1)}, f32[2,280,128]{2,1,0:T(8,128)S(1)}, u32[]{:S(2)}, u32[]{:S(2)}) collective-permute-start(f32[2,280,128]{2,1,0:T(8,128)S(1)} %get-tuple-element.22), channel_id=1, source_target_pairs={{0,1},{1,0},{2,3},{3,2},{4,5},{5,4},{6,7},{7,6},{8,9},{9,8},{10,11... | collective-permute-start | bytes 860168 | tf_op jit(solution)/shard_map/ppermute | solution.py:524
  79.6 8.8 %collective-permute-start.10 = (f32[280,128]{1,0:T(8,128)S(1)}, f32[280,128]{1,0:T(8,128)S(1)}, u32[]{:S(2)}, u32[]{:S(2)}) collective-permute-start(f32[280,128]{1,0:T(8,128)S(1)} %get-tuple-element.51), channel_id=1, source_target_pairs={{2,96},{6,100},{10,104},{14,108},{18,0},{22,4},{26,8},{30,12},{34,... | collective-permute-start | bytes 430088 | tf_op jit(solution)/shard_map/ppermute | solution.py:525
  79.7 8.7 %collective-permute-start.9 = (f32[280,128]{1,0:T(8,128)S(1)}, f32[280,128]{1,0:T(8,128)S(1)}, u32[]{:S(2)}, u32[]{:S(2)}) collective-permute-start(f32[280,128]{1,0:T(8,128)S(1)} %get-tuple-element.52), channel_id=1, source_target_pairs={{0,96},{4,100},{8,104},{12,108},{16,0},{20,4},{24,8},{28,12},{32,3... | collective-permute-start | bytes 430088 | tf_op jit(solution)/shard_map/ppermute | solution.py:525
  91.0 18.6 %all-to-all-start.1 = ((f32[64,5,2,128]{3,2,1,0:T(2,128)}), f32[64,5,2,128]{3,2,1,0:T(2,128)S(1)}, u32[]{:S(2)}, u32[]{:S(2)}) async-start(f32[64,5,2,128]{3,2,1,0:T(2,128)} %bitcast.95), calls=%async_computation.1 | async-start | bytes 655360 | tf_op jit(solution)/shard_map/all_to_all | solution.py:531
  109.8 7.3 %collective-permute-start.13 = (f32[24,128]{1,0:T(8,128)S(1)}, f32[24,128]{1,0:T(8,128)S(1)}, u32[]{:S(2)}, u32[]{:S(2)}) collective-permute-start(f32[24,128]{1,0:T(8,128)S(1)} %reshape.243), channel_id=1, source_target_pairs={{0,3},{1,2},{2,1},{3,0},{4,7},{5,6},{6,5},{7,4},{8,11},{9,10},{10,... | collective-permute-start | bytes 36872 | tf_op jit(solution)/shard_map/ppermute | solution.py:537
  115.1 4.0 %collective-permute-start.12 = (f32[24,128]{1,0:T(8,128)S(1)}, f32[24,128]{1,0:T(8,128)S(1)}, u32[]{:S(2)}, u32[]{:S(2)}) collective-permute-start(f32[24,128]{1,0:T(8,128)S(1)} %reshape.243), channel_id=1, source_target_pairs={{0,2},{1,3},{2,0},{3,1},{4,6},{5,7},{6,4},{7,5},{8,10},{9,11},{10,... | collective-permute-start | bytes 36872 | tf_op jit(solution)/shard_map/ppermute | solution.py:537
  115.8 3.4 %collective-permute-start.11 = (f32[24,128]{1,0:T(8,128)S(1)}, f32[24,128]{1,0:T(8,128)S(1)}, u32[]{:S(2)}, u32[]{:S(2)}) collective-permute-start(f32[24,128]{1,0:T(8,128)S(1)} %reshape.243), channel_id=1, source_target_pairs={{0,1},{1,0},{2,3},{3,2},{4,5},{5,4},{6,7},{7,6},{8,9},{9,8},{10,11... | collective-permute-start | bytes 36872 | tf_op jit(solution)/shard_map/ppermute | solution.py:537
  (7 other events, 15.8 us)

commit v6 on v5

--- a/solution.py
+++ b/solution.py
@@ -40,11 +40,11 @@
 SM = pl.BlockSpec(memory_space=pltpu.SMEM)
 
 
-def edge_kernel(odd, state, grad, near, next_pair):
+def prepare_kernel(where, state, grad, maps, near, next_pair, out):
     for parity in range(2):
         high, low = (near, next_pair) if parity == 0 else (next_pair, near)
 
-        @pl.when(odd[0] == parity)
+        @pl.when(where[1] == parity)
         def _():
             for i in range(2):
                 for k in range(2):
@@ -53,22 +53,6 @@
                 high[4 + i] = grad[i, :, 3, :]
                 low[4 + i] = grad[i, :, 0, :]
 
-
-def edge_call(odd, state, grad):
-    shape = jax.ShapeDtypeStruct((6, 16, 256), F32)
-    return pl.pallas_call(
-        edge_kernel,
-        out_shape=(shape, shape),
-        in_specs=[SM, VM, VM],
-        out_specs=(VM, VM),
-        cost_estimate=pl.CostEstimate(
-            flops=0, bytes_accessed=460000, transcendentals=0
-        ),
-    )(odd, state, grad)
-
-
-def payload_kernel(coil, state, grad, maps, out):
-    core = coil[0] % 2
     for part in range(2):
         for c in range(2):
             for r in range(64):
@@ -77,14 +61,14 @@
                     out[pl.ds(first, 4, stride=8), :] = maps[
                         part, c, r, :, h * 128 : h * 128 + 128
                     ]
-    for kind in range(2):
-        for core_here in range(2):
-            @pl.when(core == core_here)
-            def _():
+    for core in range(2):
+        @pl.when(where[0] == core)
+        def _():
+            for kind in range(2):
                 field = (state, grad)[kind]
                 for part in range(2):
                     for low in range(16):
-                        z = (low // 4 - 1 + 2 * core_here) % 4
+                        z = (low // 4 - 1 + 2 * core) % 4
                         for h in range(2):
                             first = (z * 8 + low % 4) * 40 + (16 + kind * 2 + part) * 2 + h
                             rows = field[part, low, :, h * 128 : h * 128 + 128]
@@ -92,16 +76,17 @@
                             out[pl.ds(first + 1280, 2, stride=160), :] = rows[2:]
 
 
-def payload_call(coil, state, grad, maps):
+def prepare_call(where, state, grad, maps):
+    shape = jax.ShapeDtypeStruct((6, 16, 256), F32)
     return pl.pallas_call(
-        payload_kernel,
-        out_shape=jax.ShapeDtypeStruct((2560, 128), F32),
+        prepare_kernel,
+        out_shape=(shape, shape, jax.ShapeDtypeStruct((2560, 128), F32)),
         in_specs=[SM, VM, VM, VM],
-        out_specs=VM,
+        out_specs=(VM, VM, VM),
         cost_estimate=pl.CostEstimate(
-            flops=0, bytes_accessed=2600000, transcendentals=0
-        ),
-    )(coil, state, grad, maps)
+            flops=0, bytes_accessed=3000000, transcendentals=0
+        ),
+    )(where, state, grad, maps)
 
 
 def combine_kernel(quarter, one, two, grad, out):
@@ -127,6 +112,7 @@
         out_shape=jax.ShapeDtypeStruct((640, 128), F32),
         in_specs=[SM, VM, VM, VM],
         out_specs=VM,
+        compiler_params=pltpu.CompilerParams(vmem_limit_bytes=8 << 20),
         cost_estimate=pl.CostEstimate(
             flops=100000, bytes_accessed=800000, transcendentals=0
         ),
@@ -300,6 +286,7 @@
         in_specs=[SM] + [VM] * 4,
         out_specs=VM,
         scratch_shapes=[pltpu.VMEM((3, 20, 8, 256), F32)],
+        compiler_params=pltpu.CompilerParams(vmem_limit_bytes=20 << 20),
         cost_estimate=pl.CostEstimate(
             flops=4000000000, bytes_accessed=2000000, transcendentals=1300000
         ),
@@ -443,7 +430,7 @@
                         ][q * 64 : q * 64 + 64, h * 128 : h * 128 + 128]
 
 
-def transform_call(coil, maps, pieces, kspace, mask, extra):
+def transform_call(coil, maps, pieces, kspace, mask, extra, table):
     vm = pl.BlockSpec(memory_space=pltpu.VMEM)
     return pl.pallas_call(
         transform_kernel,
@@ -461,18 +448,17 @@
         cost_estimate=pl.CostEstimate(
             flops=6000000000, bytes_accessed=5000000, transcendentals=0
         ),
-    )(coil, maps, *pieces, kspace, mask, extra, jnp.asarray(tables()))
+    )(coil, maps, *pieces, kspace, mask, extra, table)
 
 
 def swapped(first, second):
     return [(first, second), (second, first)]
 
 
-def halos(state, grad, slab_count):
+def halos(state, grad, near, far, slab_count):
     odd = lax.axis_index("slab") % 2
     pairs = [p for i in range(0, slab_count, 2) for p in swapped(i, i + 1)]
     others = [p for i in range(1, slab_count - 1, 2) for p in swapped(i, i + 1)]
-    near, far = edge_call(odd.reshape(1), state, grad)
     near = lax.ppermute(near, "slab", pairs)
     far = lax.ppermute(far, "slab", others)
     before = jnp.where(odd == 0, far, near)
@@ -500,14 +486,21 @@
     slab_count = lax.axis_size("slab")
     coil = lax.axis_index("coil")
     slab = lax.axis_index("slab")
-    payload = payload_call(coil.reshape(1), init_image, recon_cotangent, sens)
+    near, far, payload = prepare_call(
+        jnp.stack([coil % 2, slab % 2]), init_image, recon_cotangent, sens
+    )
     payload = payload.reshape(64, 20, 2, 128)
     received = lax.all_to_all(payload, "slab", split_axis=0, concat_axis=0, tiled=True)
 
-    before, after, lower, upper = halos(init_image, recon_cotangent, slab_count)
+    before, after, lower, upper = halos(
+        init_image, recon_cotangent, near, far, slab_count
+    )
     wide, turned = filter_tables(weights)
     edge = jnp.stack([slab > 0, slab < slab_count - 1, coil > 0, coil < 3]).astype(F32)
-    lower, wide, turned, edge = lax.optimization_barrier((lower, wide, turned, edge))
+    table = jnp.asarray(tables())
+    lower, wide, turned, edge, table = lax.optimization_barrier(
+        (lower, wide, turned, edge, table)
+    )
     packed, sums = conv_call(
         init_image, recon_cotangent, before, after, lower, upper, wide
     )
@@ -515,14 +508,18 @@
     extra = extra.reshape(24, 128)
 
     held = received[:, 16:18].reshape(256, 128)
-    pieces = [lax.ppermute(held, AXES, far_pairs(turn)) for turn in range(2)]
+    pieces = []
+    for turn in range(2):
+        pieces.append(lax.ppermute(held, AXES, far_pairs(turn)))
     pieces = pieces + [lax.ppermute(piece, "coil", CORES) for piece in pieces]
     kept, sent = transform_call(
         coil.reshape(1), received.reshape(2560, 128), pieces, kspace[:, :, 0], mask,
-        extra,
+        extra, table,
     )
     kept = kept + lax.ppermute(sent, "coil", CORES)
-    parts = [lax.ppermute(kept[t], AXES, back_pairs(t)) for t in range(2)]
+    parts = []
+    for turn in range(2):
+        parts.append(lax.ppermute(kept[turn], AXES, back_pairs(turn)))
     quarter = slab // 32 * 2 + slab // 4 % 2
     sent = combine_call(
         quarter.reshape(1), *parts, received[:, 18:20].reshape(256, 128)

time: 121 us -> 122 us (level)
  waiting for transfers between devices: 19.3 us -> 24.2 us
  Pallas kernels: 34.3 us -> 30.2 us
  starting transfers between devices: 52.6 us -> 54.2 us
  local copies, waits for them, and re-layouts: 7.61 us -> 6.24 us
    ppermute x4, starting transfers between devices: 12.6 us -> 15.2 us  [the longest x2 8.11 us: on_device(): pieces.append(lax.ppermute(held, AXES, far_pairs(turn)))]
    ppermute x4, waiting for transfers between devices: 8.5 us -> 11.1 us  [the longest x2 7.13 us: on_device(): parts.append(lax.ppermute(kept[turn], AXES, back_pairs(turn)))]
    pallas_call x2 -> x1, Pallas kernels: 4.6 us -> 3.04 us  [prepare_call(): pl.pallas_call(prepare_kernel, out_shape=(shape, shape, jax.ShapeDtypeStr...]
    pallas_call x1, Pallas kernels: 11.8 us -> 10.3 us  [adjoint_call(): pl.pallas_call(adjoint_kernel, out_shape=jax.ShapeDtypeStruct((2, 16, 4,...]
  transfers between devices with their start and end apart: 16 -> 16, of which waited for: 8 -> 10; matrix products, arithmetic and copies ran while one was open for 7% -> 6% of each run, Pallas kernels for 22% -> 18%
where the time goes in v6:
time: 122 us; the launch traced here: 121 us
  starting transfers between devices  54.2 us (44%)
  Pallas kernels  30.2 us (25%)
  waiting for transfers between devices  24.2 us (20%)
  local copies, waits for them, and re-layouts  6.24 us (5%)
  other arithmetic  4.46 us (4%)
  between operations  1.84 us (2%)
    pallas_call x1, Pallas kernels, conv_call(): pl.pallas_call(conv_kernel, out_shape=(jax.ShapeDtypeStruct((3, 2, 320, 2...  12 us
    all_to_all x1, starting transfers between devices, on_device(): lax.all_to_all(payload, 'slab', split_axis=0, concat_axis=0, tiled=True)  11.7 us
    pallas_call x1, Pallas kernels, adjoint_call(): pl.pallas_call(adjoint_kernel, out_shape=jax.ShapeDtypeStruct((2, 16, 4,...  10.3 us
    ppermute x2, starting transfers between devices, on_device(): pieces.append(lax.ppermute(held, AXES, far_pairs(turn)))  8.11 us
    ppermute x2, waiting for transfers between devices, on_device(): parts.append(lax.ppermute(kept[turn], AXES, back_pairs(turn)))  7.13 us
    ppermute x2, starting transfers between devices, on_device(): parts.append(lax.ppermute(kept[turn], AXES, back_pairs(turn)))  7.09 us
    ppermute x3, starting transfers between devices, on_device(): lax.ppermute(own, 'coil', [(i, i ^ turn) for i in range(4)])  6.14 us
    all_to_all x1, starting transfers between devices, on_device(): lax.all_to_all(sent, 'slab', split_axis=0, concat_axis=0, tiled=True)  6.13 us
  transfers between devices with their start and end apart: 16, of which 10 were waited for; matrix products, arithmetic and copies ran while one was open for 6% of the time, Pallas kernels for 18%

profile of v6, /device:TPU:1, one launch (start us, length us, event | category | flops | bytes accessed | tf_op | source)
XLA Modules:
  0.0 121.2 jit_solution(5245612224760065647)
XLA Ops:
  1.2 3.0 %shard_map.157 = (f32[6,16,256]{2,1,0:T(8,128)}, f32[6,16,256]{2,1,0:T(8,128)}, f32[2560,128]{1,0:T(8,128)}) custom-call(s32[2]{0:T(128)} %pad_add_fusion.where, f32[2,16,4,256]{3,2,1,0:T(4,128)} %init.3, f32[2,16,4,256]{3,2,1,0:T(4,128)} %grad.3, f32[2,2,64,4,256]{4,3,2,1,0:T(4,128)} %maps.1), custom_call_target="tpu_custom_call" | custom-call | bytes 3000000 | tf_op jit(solution)/shard_map/pallas_call | solution.py:81
  5.0 4.7 %collective-permute-start.1 = (f32[6,16,256]{2,1,0:T(8,128)}, f32[6,16,256]{2,1,0:T(8,128)S(1)}, u32[]{:S(2)}, u32[]{:S(2)}) collective-permute-start(f32[6,16,256]{2,1,0:T(8,128)} %get-tuple-element.16), channel_id=1, source_target_pairs={{0,4},{4,0},{8,12},{12,8},{16,20},{20,16},{24,28},{28,24},{32,36},... | collective-permute-start | bytes 294920 | tf_op jit(solution)/shard_map/ppermute | solution.py:462
  9.7 11.7 %all-to-all-start = ((f32[64,20,2,128]{3,2,1,0:T(2,128)}), f32[64,20,2,128]{3,2,1,0:T(2,128)S(1)}, u32[]{:S(2)}, u32[]{:S(2)}) async-start(f32[64,20,2,128]{3,2,1,0:T(2,128)} %bitcast.96), calls=%async_computation | async-start | bytes 2621440 | tf_op jit(solution)/shard_map/all_to_all | solution.py:493
  25.3 1.6 %collective-permute-start.3 = (f32[6,8,256]{2,1,0:T(8,128)S(1)}, f32[6,8,256]{2,1,0:T(8,128)S(1)}, u32[]{:S(2)}, u32[]{:S(2)}) collective-permute-start(f32[6,8,256]{2,1,0:T(8,128)S(1)} %get-tuple-element.71), channel_id=1, source_target_pairs={{0,1},{1,0},{2,3},{3,2},{4,5},{5,4},{6,7},{7,6},{8,9},{9,8},{10,11... | collective-permute-start | bytes 147464 | tf_op jit(solution)/shard_map/ppermute | solution.py:478
  26.9 4.3 %collective-permute-start.2 = (f32[6,8,256]{2,1,0:T(8,128)S(1)}, f32[6,8,256]{2,1,0:T(8,128)S(1)}, u32[]{:S(2)}, u32[]{:S(2)}) collective-permute-start(f32[6,8,256]{2,1,0:T(8,128)S(1)} %get-tuple-element.72), channel_id=1, source_target_pairs={{1,2},{2,1},{5,6},{6,5},{9,10},{10,9},{13,14},{14,13},{17,18},{18,... | collective-permute-start | bytes 147464 | tf_op jit(solution)/shard_map/ppermute | solution.py:479
  31.3 3.5 %collective-permute-done.2 = f32[6,8,256]{2,1,0:T(8,128)S(1)} collective-permute-done((f32[6,8,256]{2,1,0:T(8,128)S(1)}, f32[6,8,256]{2,1,0:T(8,128)S(1)}, u32[]{:S(2)}, u32[]{:S(2)}) %collective-permute-start.2) | collective-permute-done | bytes 49184 | tf_op jit(solution)/shard_map/ppermute | solution.py:479
  35.4 12.0 %shard_map.158 = (bf16[3,2,320,256]{3,2,1,0:T(8,128)(2,1)}, f32[144,192]{1,0:T(8,128)}) custom-call(f32[2,16,4,256]{3,2,1,0:T(4,128)} %init.3, f32[2,16,4,256]{3,2,1,0:T(4,128)} %grad.3, f32[6,16,256]{2,1,0:T(8,128)} %copy-done.6, f32[6,16,256]{2,1,0:T(8,128)} %copy-done.7, f32[6,8,256]{2,1,0:T(8,128)} %get-tuple-element.18.lower, ...), custom_call_target="tpu_custom_call" | custom-call | flops 4000000000 | bytes 2000000 | tf_op jit(solution)/shard_map/pallas_call | solution.py:263
  47.4 1.2 reshape.232
  48.7 4.4 %all-to-all-done = f32[64,20,2,128]{3,2,1,0:T(2,128)S(1)} async-done(((f32[64,20,2,128]{3,2,1,0:T(2,128)}), f32[64,20,2,128]{3,2,1,0:T(2,128)S(1)}, u32[]{:S(2)}, u32[]{:S(2)}) %all-to-all-start) | async-done | bytes 1310752 | tf_op jit(solution)/shard_map/all_to_all | solution.py:493
  53.1 5.9 %collective-permute-start.4 = (f32[256,128]{1,0:T(8,128)S(1)}, f32[256,128]{1,0:T(8,128)S(1)}, u32[]{:S(2)}, u32[]{:S(2)}) collective-permute-start(f32[256,128]{1,0:T(8,128)S(1)} %bitcast.101), channel_id=1, source_target_pairs={{96,0},{100,4},{104,8},{108,12},{0,16},{4,20},{8,24},{12,28},{32,3... | collective-permute-start | bytes 393224 | tf_op jit(solution)/shard_map/ppermute | solution.py:513
  59.0 2.3 %collective-permute-start.5 = (f32[256,128]{1,0:T(8,128)S(1)}, f32[256,128]{1,0:T(8,128)S(1)}, u32[]{:S(2)}, u32[]{:S(2)}) collective-permute-start(f32[256,128]{1,0:T(8,128)S(1)} %bitcast.102), channel_id=1, source_target_pairs={{96,2},{100,6},{104,10},{108,14},{0,18},{4,22},{8,26},{12,30},{32,... | collective-permute-start | bytes 393224 | tf_op jit(solution)/shard_map/ppermute | solution.py:513
  61.6 3.1 %collective-permute-start.6 = (f32[256,128]{1,0:T(8,128)S(1)}, f32[256,128]{1,0:T(8,128)S(1)}, u32[]{:S(2)}, u32[]{:S(2)}) collective-permute-start(f32[256,128]{1,0:T(8,128)S(1)} %collective-permute-done.4.p0), channel_id=1, source_target_pairs={{0,1},{1,0},{2,3},{3,2},{4,5},{5,4},{6,7},{7,6},{8,9},{9,8},{10,11... | collective-permute-start | bytes 393224 | tf_op jit(solution)/shard_map/ppermute | solution.py:514
  64.8 3.6 %collective-permute-done.5.p1 = f32[256,128]{1,0:T(8,128)S(1)} collective-permute-done((f32[256,128]{1,0:T(8,128)S(1)}, f32[256,128]{1,0:T(8,128)S(1)}, u32[]{:S(2)}, u32[]{:S(2)}) %collective-permute-start.5) | collective-permute-done | bytes 131104 | tf_op jit(solution)/shard_map/ppermute | solution.py:513
  69.7 1.4 %copy-done.4 = bf16[12,256,256]{2,1,0:T(8,128)(2,1)S(1)} copy-done((bf16[12,256,256]{2,1,0:T(8,128)(2,1)S(1)}, bf16[12,256,256]{2,1,0:T(8,128)(2,1)}, u32[]{:S(2)}) %copy-start.4) | copy-done | bytes 1572888
  71.1 4.0 %shard_map.160 = (f32[2,280,128]{2,1,0:T(8,128)S(1)}, f32[2,280,128]{2,1,0:T(8,128)S(1)}) custom-call(s32[1]{0:T(128)} %bitcast.30.coil, f32[2560,128]{1,0:T(8,128)S(1)} %bitcast.93, f32[256,128]{1,0:T(8,128)S(1)} %collective-permute-done.4.p0, f32[256,128]{1,0:T(8,128)S(1)} %collective-permute-done.5.p1, f32[256,128]{1,0:T(8,128)S(1)} %collective-permute-done.6.p2, ...), custom_call_target="tpu_custom_call" | custom-call | flops 6000000000 | bytes 5000000 | tf_op jit(solution)/shard_map/pallas_call | solution.py:435
  75.6 1.4 %collective-permute-done.8 = f32[2,280,128]{2,1,0:T(8,128)S(1)} collective-permute-done((f32[2,280,128]{2,1,0:T(8,128)S(1)}, f32[2,280,128]{2,1,0:T(8,128)S(1)}, u32[]{:S(2)}, u32[]{:S(2)}) %collective-permute-start.8) | collective-permute-done | bytes 286752 | tf_op jit(solution)/shard_map/ppermute | solution.py:519
  77.1 2.1 %collective-permute-start.9 = (f32[280,128]{1,0:T(8,128)S(1)}, f32[280,128]{1,0:T(8,128)S(1)}, u32[]{:S(2)}, u32[]{:S(2)}) collective-permute-start(f32[280,128]{1,0:T(8,128)S(1)} %get-tuple-element.56), channel_id=1, source_target_pairs={{0,96},{4,100},{8,104},{12,108},{16,0},{20,4},{24,8},{28,12},{32,3... | collective-permute-start | bytes 430088 | tf_op jit(solution)/shard_map/ppermute | solution.py:522
  79.1 5.0 %collective-permute-start.10 = (f32[280,128]{1,0:T(8,128)S(1)}, f32[280,128]{1,0:T(8,128)S(1)}, u32[]{:S(2)}, u32[]{:S(2)}) collective-permute-start(f32[280,128]{1,0:T(8,128)S(1)} %get-tuple-element.55), channel_id=1, source_target_pairs={{2,96},{6,100},{10,104},{14,108},{18,0},{22,4},{26,8},{30,12},{34,... | collective-permute-start | bytes 430088 | tf_op jit(solution)/shard_map/ppermute | solution.py:522
  84.2 2.0 %collective-permute-done.9.one = f32[280,128]{1,0:T(8,128)S(1)} collective-permute-done((f32[280,128]{1,0:T(8,128)S(1)}, f32[280,128]{1,0:T(8,128)S(1)}, u32[]{:S(2)}, u32[]{:S(2)}) %collective-permute-start.9) | collective-permute-done | bytes 143392 | tf_op jit(solution)/shard_map/ppermute | solution.py:522
  86.2 5.1 %collective-permute-done.10.two = f32[280,128]{1,0:T(8,128)S(1)} collective-permute-done((f32[280,128]{1,0:T(8,128)S(1)}, f32[280,128]{1,0:T(8,128)S(1)}, u32[]{:S(2)}, u32[]{:S(2)}) %collective-permute-start.10) | collective-permute-done | bytes 143392 | tf_op jit(solution)/shard_map/ppermute | solution.py:522
  92.2 6.1 %all-to-all-start.1 = ((f32[64,5,2,128]{3,2,1,0:T(2,128)}), f32[64,5,2,128]{3,2,1,0:T(2,128)S(1)}, u32[]{:S(2)}, u32[]{:S(2)}) async-start(f32[64,5,2,128]{3,2,1,0:T(2,128)} %bitcast.41), calls=%async_computation.1 | async-start | bytes 655360 | tf_op jit(solution)/shard_map/all_to_all | solution.py:528
  99.0 10.3 %shard_map.159 = f32[2,16,4,256]{3,2,1,0:T(4,128)S(1)} custom-call(f32[4]{0:T(128)S(1)} %add_convert_fusion.edge, f32[2,16,4,256]{3,2,1,0:T(4,128)S(1)} %copy-done.1, bf16[3,2,320,256]{3,2,1,0:T(8,128)(2,1)S(1)} %copy-done.5, bf16[288,432]{1,0:T(8,128)(2,1)S(1)} %copy-done, bf16[144,576]{1,0:T(8,128)(2,1)S(1)} %fusion.1.turned), custom_call_target="tpu_custom_call" | custom-call | flops 4000000000 | bytes 2000000 | tf_op jit(solution)/shard_map/pallas_call | solution.py:283
  110.7 5.0 %collective-permute-start.13 = (f32[24,128]{1,0:T(8,128)S(1)}, f32[24,128]{1,0:T(8,128)S(1)}, u32[]{:S(2)}, u32[]{:S(2)}) collective-permute-start(f32[24,128]{1,0:T(8,128)S(1)} %reshape.238), channel_id=1, source_target_pairs={{0,3},{1,2},{2,1},{3,0},{4,7},{5,6},{6,5},{7,4},{8,11},{9,10},{10,... | collective-permute-start | bytes 36872 | tf_op jit(solution)/shard_map/ppermute | solution.py:534
  117.8 1.9 %collective-permute-done.12 = f32[24,128]{1,0:T(8,128)S(1)} collective-permute-done((f32[24,128]{1,0:T(8,128)S(1)}, f32[24,128]{1,0:T(8,128)S(1)}, u32[]{:S(2)}, u32[]{:S(2)}) %collective-permute-start.12) | collective-permute-done | bytes 12320 | tf_op jit(solution)/shard_map/ppermute | solution.py:534
  (102 shorter events, 13.6 us)
Async XLA Ops:
  4.3 20.7 %collective-permute-start = (f32[6,16,256]{2,1,0:T(8,128)}, f32[6,16,256]{2,1,0:T(8,128)S(1)}, u32[]{:S(2)}, u32[]{:S(2)}) collective-permute-start(f32[6,16,256]{2,1,0:T(8,128)} %get-tuple-element.15), channel_id=1, source_target_pairs={{4,8},{8,4},{12,16},{16,12},{20,24},{24,20},{28,32},{32,28},{36,40... | collective-permute-start | bytes 294920 | tf_op jit(solution)/shard_map/ppermute | solution.py:463
  5.0 20.1 %collective-permute-start.1 = (f32[6,16,256]{2,1,0:T(8,128)}, f32[6,16,256]{2,1,0:T(8,128)S(1)}, u32[]{:S(2)}, u32[]{:S(2)}) collective-permute-start(f32[6,16,256]{2,1,0:T(8,128)} %get-tuple-element.16), channel_id=1, source_target_pairs={{0,4},{4,0},{8,12},{12,8},{16,20},{20,16},{24,28},{28,24},{32,36},... | collective-permute-start | bytes 294920 | tf_op jit(solution)/shard_map/ppermute | solution.py:462
  9.7 13.2 %copy-start.9 = (f32[6,8]{0,1:T(8,128)S(1)}, f32[6,8]{0,1:T(8,128)}, u32[]{:S(2)}) copy-start(f32[6,8]{0,1:T(8,128)} %constant.85.clone) | copy-start | bytes 580
  9.7 13.2 %copy-start.10 = (f32[6,8]{0,1:T(8,128)S(1)}, f32[6,8]{0,1:T(8,128)}, u32[]{:S(2)}) copy-start(f32[6,8]{0,1:T(8,128)} %constant.84.clone) | copy-start | bytes 580
  9.7 13.2 %copy-start.11 = (f32[6,8]{0,1:T(8,128)S(1)}, f32[6,8]{0,1:T(8,128)}, u32[]{:S(2)}) copy-start(f32[6,8]{0,1:T(8,128)} %constant.83.clone) | copy-start | bytes 580
  9.7 43.4 %all-to-all-start = ((f32[64,20,2,128]{3,2,1,0:T(2,128)}), f32[64,20,2,128]{3,2,1,0:T(2,128)S(1)}, u32[]{:S(2)}, u32[]{:S(2)}) async-start(f32[64,20,2,128]{3,2,1,0:T(2,128)} %bitcast.96), calls=%async_computation | async-start | bytes 2621440 | tf_op jit(solution)/shard_map/all_to_all | solution.py:493
  25.3 6.0 %collective-permute-start.3 = (f32[6,8,256]{2,1,0:T(8,128)S(1)}, f32[6,8,256]{2,1,0:T(8,128)S(1)}, u32[]{:S(2)}, u32[]{:S(2)}) collective-permute-start(f32[6,8,256]{2,1,0:T(8,128)S(1)} %get-tuple-element.71), channel_id=1, source_target_pairs={{0,1},{1,0},{2,3},{3,2},{4,5},{5,4},{6,7},{7,6},{8,9},{9,8},{10,11... | collective-permute-start | bytes 147464 | tf_op jit(solution)/shard_map/ppermute | solution.py:478
  26.9 7.8 %collective-permute-start.2 = (f32[6,8,256]{2,1,0:T(8,128)S(1)}, f32[6,8,256]{2,1,0:T(8,128)S(1)}, u32[]{:S(2)}, u32[]{:S(2)}) collective-permute-start(f32[6,8,256]{2,1,0:T(8,128)S(1)} %get-tuple-element.72), channel_id=1, source_target_pairs={{1,2},{2,1},{5,6},{6,5},{9,10},{10,9},{13,14},{14,13},{17,18},{18,... | collective-permute-start | bytes 147464 | tf_op jit(solution)/shard_map/ppermute | solution.py:479
  47.4 22.3 %copy-start.2 = (f32[2,2,1,256,256]{4,3,2,1,0:T(8,128)S(1)}, f32[2,2,1,256,256]{4,3,2,1,0:T(8,128)}, u32[]{:S(2)}) copy-start(f32[2,2,1,256,256]{4,3,2,1,0:T(8,128)} %param.16) | copy-start | bytes 3145732
  47.4 22.3 %copy-start.3 = (s32[256,256]{1,0:T(8,128)S(1)}, s32[256,256]{1,0:T(8,128)}, u32[]{:S(2)}) copy-start(s32[256,256]{1,0:T(8,128)} %mask.1) | copy-start | bytes 786436
  53.1 8.5 %collective-permute-start.4 = (f32[256,128]{1,0:T(8,128)S(1)}, f32[256,128]{1,0:T(8,128)S(1)}, u32[]{:S(2)}, u32[]{:S(2)}) collective-permute-start(f32[256,128]{1,0:T(8,128)S(1)} %bitcast.101), channel_id=1, source_target_pairs={{96,0},{100,4},{104,8},{108,12},{0,16},{4,20},{8,24},{12,28},{32,3... | collective-permute-start | bytes 393224 | tf_op jit(solution)/shard_map/ppermute | solution.py:513
  59.0 9.4 %collective-permute-start.5 = (f32[256,128]{1,0:T(8,128)S(1)}, f32[256,128]{1,0:T(8,128)S(1)}, u32[]{:S(2)}, u32[]{:S(2)}) collective-permute-start(f32[256,128]{1,0:T(8,128)S(1)} %bitcast.102), channel_id=1, source_target_pairs={{96,2},{100,6},{104,10},{108,14},{0,18},{4,22},{8,26},{12,30},{32,... | collective-permute-start | bytes 393224 | tf_op jit(solution)/shard_map/ppermute | solution.py:513
  61.6 7.1 %collective-permute-start.6 = (f32[256,128]{1,0:T(8,128)S(1)}, f32[256,128]{1,0:T(8,128)S(1)}, u32[]{:S(2)}, u32[]{:S(2)}) collective-permute-start(f32[256,128]{1,0:T(8,128)S(1)} %collective-permute-done.4.p0), channel_id=1, source_target_pairs={{0,1},{1,0},{2,3},{3,2},{4,5},{5,4},{6,7},{7,6},{8,9},{9,8},{10,11... | collective-permute-start | bytes 393224 | tf_op jit(solution)/shard_map/ppermute | solution.py:514
  68.4 1.3 %collective-permute-start.7 = (f32[256,128]{1,0:T(8,128)S(1)}, f32[256,128]{1,0:T(8,128)S(1)}, u32[]{:S(2)}, u32[]{:S(2)}) collective-permute-start(f32[256,128]{1,0:T(8,128)S(1)} %collective-permute-done.5.p1), channel_id=1, source_target_pairs={{0,1},{1,0},{2,3},{3,2},{4,5},{5,4},{6,7},{7,6},{8,9},{9,8},{10,11... | collective-permute-start | bytes 393224 | tf_op jit(solution)/shard_map/ppermute | solution.py:514
  75.2 1.8 %collective-permute-start.8 = (f32[2,280,128]{2,1,0:T(8,128)S(1)}, f32[2,280,128]{2,1,0:T(8,128)S(1)}, u32[]{:S(2)}, u32[]{:S(2)}) collective-permute-start(f32[2,280,128]{2,1,0:T(8,128)S(1)} %get-tuple-element.26), channel_id=1, source_target_pairs={{0,1},{1,0},{2,3},{3,2},{4,5},{5,4},{6,7},{7,6},{8,9},{9,8},{10,11... | collective-permute-start | bytes 860168 | tf_op jit(solution)/shard_map/ppermute | solution.py:519
  77.0 22.0 %copy-start = (bf16[288,432]{1,0:T(8,128)(2,1)S(1)}, bf16[288,432]{1,0:T(8,128)(2,1)}, u32[]{:S(2)}) copy-start(bf16[288,432]{1,0:T(8,128)(2,1)} %pad_maximum_fusion.wide) | copy-start | bytes 746500
  77.0 22.0 %copy-start.1 = (f32[2,16,4,256]{3,2,1,0:T(4,128)S(1)}, f32[2,16,4,256]{3,2,1,0:T(4,128)}, u32[]{:S(2)}) copy-start(f32[2,16,4,256]{3,2,1,0:T(4,128)} %init.3) | copy-start | bytes 393220
  77.0 22.0 %copy-start.5 = (bf16[3,2,320,256]{3,2,1,0:T(8,128)(2,1)S(1)}, bf16[3,2,320,256]{3,2,1,0:T(8,128)(2,1)}, u32[]{:S(2)}) copy-start(bf16[3,2,320,256]{3,2,1,0:T(8,128)(2,1)} %get-tuple-element.20.xb) | copy-start | bytes 2949124
  77.1 9.1 %collective-permute-start.9 = (f32[280,128]{1,0:T(8,128)S(1)}, f32[280,128]{1,0:T(8,128)S(1)}, u32[]{:S(2)}, u32[]{:S(2)}) collective-permute-start(f32[280,128]{1,0:T(8,128)S(1)} %get-tuple-element.56), channel_id=1, source_target_pairs={{0,96},{4,100},{8,104},{12,108},{16,0},{20,4},{24,8},{28,12},{32,3... | collective-permute-start | bytes 430088 | tf_op jit(solution)/shard_map/ppermute | solution.py:522
  79.1 12.2 %collective-permute-start.10 = (f32[280,128]{1,0:T(8,128)S(1)}, f32[280,128]{1,0:T(8,128)S(1)}, u32[]{:S(2)}, u32[]{:S(2)}) collective-permute-start(f32[280,128]{1,0:T(8,128)S(1)} %get-tuple-element.55), channel_id=1, source_target_pairs={{2,96},{6,100},{10,104},{14,108},{18,0},{22,4},{26,8},{30,12},{34,... | collective-permute-start | bytes 430088 | tf_op jit(solution)/shard_map/ppermute | solution.py:522
  92.2 18.1 %all-to-all-start.1 = ((f32[64,5,2,128]{3,2,1,0:T(2,128)}), f32[64,5,2,128]{3,2,1,0:T(2,128)S(1)}, u32[]{:S(2)}, u32[]{:S(2)}) async-start(f32[64,5,2,128]{3,2,1,0:T(2,128)} %bitcast.41), calls=%async_computation.1 | async-start | bytes 655360 | tf_op jit(solution)/shard_map/all_to_all | solution.py:528
  110.7 7.1 %collective-permute-start.13 = (f32[24,128]{1,0:T(8,128)S(1)}, f32[24,128]{1,0:T(8,128)S(1)}, u32[]{:S(2)}, u32[]{:S(2)}) collective-permute-start(f32[24,128]{1,0:T(8,128)S(1)} %reshape.238), channel_id=1, source_target_pairs={{0,3},{1,2},{2,1},{3,0},{4,7},{5,6},{6,5},{7,4},{8,11},{9,10},{10,... | collective-permute-start | bytes 36872 | tf_op jit(solution)/shard_map/ppermute | solution.py:534
  115.7 4.0 %collective-permute-start.12 = (f32[24,128]{1,0:T(8,128)S(1)}, f32[24,128]{1,0:T(8,128)S(1)}, u32[]{:S(2)}, u32[]{:S(2)}) collective-permute-start(f32[24,128]{1,0:T(8,128)S(1)} %reshape.238), channel_id=1, source_target_pairs={{0,2},{1,3},{2,0},{3,1},{4,6},{5,7},{6,4},{7,5},{8,10},{9,11},{10,... | collective-permute-start | bytes 36872 | tf_op jit(solution)/shard_map/ppermute | solution.py:534
  116.8 3.0 %collective-permute-start.11 = (f32[24,128]{1,0:T(8,128)S(1)}, f32[24,128]{1,0:T(8,128)S(1)}, u32[]{:S(2)}, u32[]{:S(2)}) collective-permute-start(f32[24,128]{1,0:T(8,128)S(1)} %reshape.238), channel_id=1, source_target_pairs={{0,1},{1,0},{2,3},{3,2},{4,5},{5,4},{6,7},{7,6},{8,9},{9,8},{10,11... | collective-permute-start | bytes 36872 | tf_op jit(solution)/shard_map/ppermute | solution.py:534
  (7 other events, 37.4 us)

commit v7 on v6

--- a/solution.py
+++ b/solution.py
@@ -40,11 +40,11 @@
 SM = pl.BlockSpec(memory_space=pltpu.SMEM)
 
 
-def prepare_kernel(where, state, grad, maps, near, next_pair, out):
+def prepare_kernel(coil, slab, state, grad, maps, near, next_pair, out):
     for parity in range(2):
         high, low = (near, next_pair) if parity == 0 else (next_pair, near)
 
-        @pl.when(where[1] == parity)
+        @pl.when(slab[0] % 2 == parity)
         def _():
             for i in range(2):
                 for k in range(2):
@@ -62,7 +62,7 @@
                         part, c, r, :, h * 128 : h * 128 + 128
                     ]
     for core in range(2):
-        @pl.when(where[0] == core)
+        @pl.when(coil[0] % 2 == core)
         def _():
             for kind in range(2):
                 field = (state, grad)[kind]
@@ -76,17 +76,17 @@
                             out[pl.ds(first + 1280, 2, stride=160), :] = rows[2:]
 
 
-def prepare_call(where, state, grad, maps):
+def prepare_call(coil, slab, state, grad, maps):
     shape = jax.ShapeDtypeStruct((6, 16, 256), F32)
     return pl.pallas_call(
         prepare_kernel,
         out_shape=(shape, shape, jax.ShapeDtypeStruct((2560, 128), F32)),
-        in_specs=[SM, VM, VM, VM],
+        in_specs=[SM, SM, VM, VM, VM],
         out_specs=(VM, VM, VM),
         cost_estimate=pl.CostEstimate(
             flops=0, bytes_accessed=3000000, transcendentals=0
         ),
-    )(where, state, grad, maps)
+    )(coil, slab, state, grad, maps)
 
 
 def combine_kernel(quarter, one, two, grad, out):
@@ -487,7 +487,7 @@
     coil = lax.axis_index("coil")
     slab = lax.axis_index("slab")
     near, far, payload = prepare_call(
-        jnp.stack([coil % 2, slab % 2]), init_image, recon_cotangent, sens
+        coil.reshape(1), slab.reshape(1), init_image, recon_cotangent, sens
     )
     payload = payload.reshape(64, 20, 2, 128)
     received = lax.all_to_all(payload, "slab", split_axis=0, concat_axis=0, tiled=True)

time: 122 us -> 121 us (level)
  no operation moved by 1% of the time
where the time goes in v7:
time: 121 us
  starting transfers between devices  54.2 us (45%)
  Pallas kernels  30.2 us (25%)
  waiting for transfers between devices  24.2 us (20%)
  local copies, waits for them, and re-layouts  6.24 us (5%)
  other arithmetic  3.87 us (3%)
  between operations  1.82 us (2%)
    pallas_call x1, Pallas kernels, conv_call(): pl.pallas_call(conv_kernel, out_shape=(jax.ShapeDtypeStruct((3, 2, 320, 2...  12 us
    all_to_all x1, starting transfers between devices, on_device(): lax.all_to_all(payload, 'slab', split_axis=0, concat_axis=0, tiled=True)  11.7 us
    pallas_call x1, Pallas kernels, adjoint_call(): pl.pallas_call(adjoint_kernel, out_shape=jax.ShapeDtypeStruct((2, 16, 4,...  10.3 us
    ppermute x2, starting transfers between devices, on_device(): pieces.append(lax.ppermute(held, AXES, far_pairs(turn)))  8.11 us
    ppermute x2, waiting for transfers between devices, on_device(): parts.append(lax.ppermute(kept[turn], AXES, back_pairs(turn)))  7.13 us
    ppermute x2, starting transfers between devices, on_device(): parts.append(lax.ppermute(kept[turn], AXES, back_pairs(turn)))  7.1 us
    ppermute x3, starting transfers between devices, on_device(): lax.ppermute(own, 'coil', [(i, i ^ turn) for i in range(4)])  6.15 us
    all_to_all x1, starting transfers between devices, on_device(): lax.all_to_all(sent, 'slab', split_axis=0, concat_axis=0, tiled=True)  6.12 us
  transfers between devices with their start and end apart: 16, of which 10 were waited for; matrix products, arithmetic and copies ran while one was open for 6% of the time, Pallas kernels for 18%

profile of v7, /device:TPU:1, one launch (start us, length us, event | category | flops | bytes accessed | tf_op | source)
XLA Modules:
  0.0 120.6 jit_solution(1958591787310600431)
XLA Ops:
  0.6 3.0 %shard_map.157 = (f32[6,16,256]{2,1,0:T(8,128)}, f32[6,16,256]{2,1,0:T(8,128)}, f32[2560,128]{1,0:T(8,128)}) custom-call(s32[1]{0:T(128)} %bitcast.coil, s32[1]{0:T(128)} %bitcast.1.slab, f32[2,16,4,256]{3,2,1,0:T(4,128)} %init.3, f32[2,16,4,256]{3,2,1,0:T(4,128)} %grad.3, f32[2,2,64,4,256]{4,3,2,1,0:T(4,128)} %maps.1), custom_call_target="tpu_custom_call" | custom-call | bytes 3000000 | tf_op jit(solution)/shard_map/pallas_call | solution.py:81
  4.3 4.7 %collective-permute-start.1 = (f32[6,16,256]{2,1,0:T(8,128)}, f32[6,16,256]{2,1,0:T(8,128)S(1)}, u32[]{:S(2)}, u32[]{:S(2)}) collective-permute-start(f32[6,16,256]{2,1,0:T(8,128)} %get-tuple-element.16), channel_id=1, source_target_pairs={{0,4},{4,0},{8,12},{12,8},{16,20},{20,16},{24,28},{28,24},{32,36},... | collective-permute-start | bytes 294920 | tf_op jit(solution)/shard_map/ppermute | solution.py:462
  9.1 11.7 %all-to-all-start = ((f32[64,20,2,128]{3,2,1,0:T(2,128)}), f32[64,20,2,128]{3,2,1,0:T(2,128)S(1)}, u32[]{:S(2)}, u32[]{:S(2)}) async-start(f32[64,20,2,128]{3,2,1,0:T(2,128)} %bitcast.95), calls=%async_computation | async-start | bytes 2621440 | tf_op jit(solution)/shard_map/all_to_all | solution.py:493
  24.7 1.6 %collective-permute-start.3 = (f32[6,8,256]{2,1,0:T(8,128)S(1)}, f32[6,8,256]{2,1,0:T(8,128)S(1)}, u32[]{:S(2)}, u32[]{:S(2)}) collective-permute-start(f32[6,8,256]{2,1,0:T(8,128)S(1)} %get-tuple-element.71), channel_id=1, source_target_pairs={{0,1},{1,0},{2,3},{3,2},{4,5},{5,4},{6,7},{7,6},{8,9},{9,8},{10,11... | collective-permute-start | bytes 147464 | tf_op jit(solution)/shard_map/ppermute | solution.py:478
  26.3 4.3 %collective-permute-start.2 = (f32[6,8,256]{2,1,0:T(8,128)S(1)}, f32[6,8,256]{2,1,0:T(8,128)S(1)}, u32[]{:S(2)}, u32[]{:S(2)}) collective-permute-start(f32[6,8,256]{2,1,0:T(8,128)S(1)} %get-tuple-element.72), channel_id=1, source_target_pairs={{1,2},{2,1},{5,6},{6,5},{9,10},{10,9},{13,14},{14,13},{17,18},{18,... | collective-permute-start | bytes 147464 | tf_op jit(solution)/shard_map/ppermute | solution.py:479
  30.6 3.5 %collective-permute-done.2 = f32[6,8,256]{2,1,0:T(8,128)S(1)} collective-permute-done((f32[6,8,256]{2,1,0:T(8,128)S(1)}, f32[6,8,256]{2,1,0:T(8,128)S(1)}, u32[]{:S(2)}, u32[]{:S(2)}) %collective-permute-start.2) | collective-permute-done | bytes 49184 | tf_op jit(solution)/shard_map/ppermute | solution.py:479
  34.8 12.0 %shard_map.158 = (bf16[3,2,320,256]{3,2,1,0:T(8,128)(2,1)}, f32[144,192]{1,0:T(8,128)}) custom-call(f32[2,16,4,256]{3,2,1,0:T(4,128)} %init.3, f32[2,16,4,256]{3,2,1,0:T(4,128)} %grad.3, f32[6,16,256]{2,1,0:T(8,128)} %copy-done.6, f32[6,16,256]{2,1,0:T(8,128)} %copy-done.7, f32[6,8,256]{2,1,0:T(8,128)} %get-tuple-element.18.lower, ...), custom_call_target="tpu_custom_call" | custom-call | flops 4000000000 | bytes 2000000 | tf_op jit(solution)/shard_map/pallas_call | solution.py:263
  46.8 1.2 reshape.237
  48.1 4.4 %all-to-all-done = f32[64,20,2,128]{3,2,1,0:T(2,128)S(1)} async-done(((f32[64,20,2,128]{3,2,1,0:T(2,128)}), f32[64,20,2,128]{3,2,1,0:T(2,128)S(1)}, u32[]{:S(2)}, u32[]{:S(2)}) %all-to-all-start) | async-done | bytes 1310752 | tf_op jit(solution)/shard_map/all_to_all | solution.py:493
  52.5 5.9 %collective-permute-start.4 = (f32[256,128]{1,0:T(8,128)S(1)}, f32[256,128]{1,0:T(8,128)S(1)}, u32[]{:S(2)}, u32[]{:S(2)}) collective-permute-start(f32[256,128]{1,0:T(8,128)S(1)} %bitcast.100), channel_id=1, source_target_pairs={{96,0},{100,4},{104,8},{108,12},{0,16},{4,20},{8,24},{12,28},{32,3... | collective-permute-start | bytes 393224 | tf_op jit(solution)/shard_map/ppermute | solution.py:513
  58.4 2.3 %collective-permute-start.5 = (f32[256,128]{1,0:T(8,128)S(1)}, f32[256,128]{1,0:T(8,128)S(1)}, u32[]{:S(2)}, u32[]{:S(2)}) collective-permute-start(f32[256,128]{1,0:T(8,128)S(1)} %bitcast.101), channel_id=1, source_target_pairs={{96,2},{100,6},{104,10},{108,14},{0,18},{4,22},{8,26},{12,30},{32,... | collective-permute-start | bytes 393224 | tf_op jit(solution)/shard_map/ppermute | solution.py:513
  61.0 3.1 %collective-permute-start.6 = (f32[256,128]{1,0:T(8,128)S(1)}, f32[256,128]{1,0:T(8,128)S(1)}, u32[]{:S(2)}, u32[]{:S(2)}) collective-permute-start(f32[256,128]{1,0:T(8,128)S(1)} %collective-permute-done.4.p0), channel_id=1, source_target_pairs={{0,1},{1,0},{2,3},{3,2},{4,5},{5,4},{6,7},{7,6},{8,9},{9,8},{10,11... | collective-permute-start | bytes 393224 | tf_op jit(solution)/shard_map/ppermute | solution.py:514
  64.1 3.6 %collective-permute-done.5.p1 = f32[256,128]{1,0:T(8,128)S(1)} collective-permute-done((f32[256,128]{1,0:T(8,128)S(1)}, f32[256,128]{1,0:T(8,128)S(1)}, u32[]{:S(2)}, u32[]{:S(2)}) %collective-permute-start.5) | collective-permute-done | bytes 131104 | tf_op jit(solution)/shard_map/ppermute | solution.py:513
  69.1 1.4 %copy-done.4 = bf16[12,256,256]{2,1,0:T(8,128)(2,1)S(1)} copy-done((bf16[12,256,256]{2,1,0:T(8,128)(2,1)S(1)}, bf16[12,256,256]{2,1,0:T(8,128)(2,1)}, u32[]{:S(2)}) %copy-start.4) | copy-done | bytes 1572888
  70.5 4.0 %shard_map.160 = (f32[2,280,128]{2,1,0:T(8,128)S(1)}, f32[2,280,128]{2,1,0:T(8,128)S(1)}) custom-call(s32[1]{0:T(128)} %bitcast.coil, f32[2560,128]{1,0:T(8,128)S(1)} %bitcast.92, f32[256,128]{1,0:T(8,128)S(1)} %collective-permute-done.4.p0, f32[256,128]{1,0:T(8,128)S(1)} %collective-permute-done.5.p1, f32[256,128]{1,0:T(8,128)S(1)} %collective-permute-done.6.p2, ...), custom_call_target="tpu_custom_call" | custom-call | flops 6000000000 | bytes 5000000 | tf_op jit(solution)/shard_map/pallas_call | solution.py:435
  75.0 1.4 %collective-permute-done.8 = f32[2,280,128]{2,1,0:T(8,128)S(1)} collective-permute-done((f32[2,280,128]{2,1,0:T(8,128)S(1)}, f32[2,280,128]{2,1,0:T(8,128)S(1)}, u32[]{:S(2)}, u32[]{:S(2)}) %collective-permute-start.8) | collective-permute-done | bytes 286752 | tf_op jit(solution)/shard_map/ppermute | solution.py:519
  76.5 2.1 %collective-permute-start.9 = (f32[280,128]{1,0:T(8,128)S(1)}, f32[280,128]{1,0:T(8,128)S(1)}, u32[]{:S(2)}, u32[]{:S(2)}) collective-permute-start(f32[280,128]{1,0:T(8,128)S(1)} %get-tuple-element.56), channel_id=1, source_target_pairs={{0,96},{4,100},{8,104},{12,108},{16,0},{20,4},{24,8},{28,12},{32,3... | collective-permute-start | bytes 430088 | tf_op jit(solution)/shard_map/ppermute | solution.py:522
  78.5 5.0 %collective-permute-start.10 = (f32[280,128]{1,0:T(8,128)S(1)}, f32[280,128]{1,0:T(8,128)S(1)}, u32[]{:S(2)}, u32[]{:S(2)}) collective-permute-start(f32[280,128]{1,0:T(8,128)S(1)} %get-tuple-element.55), channel_id=1, source_target_pairs={{2,96},{6,100},{10,104},{14,108},{18,0},{22,4},{26,8},{30,12},{34,... | collective-permute-start | bytes 430088 | tf_op jit(solution)/shard_map/ppermute | solution.py:522
  83.6 2.0 %collective-permute-done.9.one = f32[280,128]{1,0:T(8,128)S(1)} collective-permute-done((f32[280,128]{1,0:T(8,128)S(1)}, f32[280,128]{1,0:T(8,128)S(1)}, u32[]{:S(2)}, u32[]{:S(2)}) %collective-permute-start.9) | collective-permute-done | bytes 143392 | tf_op jit(solution)/shard_map/ppermute | solution.py:522
  85.6 5.1 %collective-permute-done.10.two = f32[280,128]{1,0:T(8,128)S(1)} collective-permute-done((f32[280,128]{1,0:T(8,128)S(1)}, f32[280,128]{1,0:T(8,128)S(1)}, u32[]{:S(2)}, u32[]{:S(2)}) %collective-permute-start.10) | collective-permute-done | bytes 143392 | tf_op jit(solution)/shard_map/ppermute | solution.py:522
  91.6 6.1 %all-to-all-start.1 = ((f32[64,5,2,128]{3,2,1,0:T(2,128)}), f32[64,5,2,128]{3,2,1,0:T(2,128)S(1)}, u32[]{:S(2)}, u32[]{:S(2)}) async-start(f32[64,5,2,128]{3,2,1,0:T(2,128)} %bitcast.40), calls=%async_computation.1 | async-start | bytes 655360 | tf_op jit(solution)/shard_map/all_to_all | solution.py:528
  98.4 10.3 %shard_map.159 = f32[2,16,4,256]{3,2,1,0:T(4,128)S(1)} custom-call(f32[4]{0:T(128)S(1)} %add_convert_fusion.edge, f32[2,16,4,256]{3,2,1,0:T(4,128)S(1)} %copy-done.1, bf16[3,2,320,256]{3,2,1,0:T(8,128)(2,1)S(1)} %copy-done.5, bf16[288,432]{1,0:T(8,128)(2,1)S(1)} %copy-done, bf16[144,576]{1,0:T(8,128)(2,1)S(1)} %fusion.1.turned), custom_call_target="tpu_custom_call" | custom-call | flops 4000000000 | bytes 2000000 | tf_op jit(solution)/shard_map/pallas_call | solution.py:283
  110.0 5.0 %collective-permute-start.13 = (f32[24,128]{1,0:T(8,128)S(1)}, f32[24,128]{1,0:T(8,128)S(1)}, u32[]{:S(2)}, u32[]{:S(2)}) collective-permute-start(f32[24,128]{1,0:T(8,128)S(1)} %reshape.243), channel_id=1, source_target_pairs={{0,3},{1,2},{2,1},{3,0},{4,7},{5,6},{6,5},{7,4},{8,11},{9,10},{10,... | collective-permute-start | bytes 36872 | tf_op jit(solution)/shard_map/ppermute | solution.py:534
  117.2 1.9 %collective-permute-done.12 = f32[24,128]{1,0:T(8,128)S(1)} collective-permute-done((f32[24,128]{1,0:T(8,128)S(1)}, f32[24,128]{1,0:T(8,128)S(1)}, u32[]{:S(2)}, u32[]{:S(2)}) %collective-permute-start.12) | collective-permute-done | bytes 12320 | tf_op jit(solution)/shard_map/ppermute | solution.py:534
  (101 shorter events, 13.0 us)
Async XLA Ops:
  3.7 20.7 %collective-permute-start = (f32[6,16,256]{2,1,0:T(8,128)}, f32[6,16,256]{2,1,0:T(8,128)S(1)}, u32[]{:S(2)}, u32[]{:S(2)}) collective-permute-start(f32[6,16,256]{2,1,0:T(8,128)} %get-tuple-element.15), channel_id=1, source_target_pairs={{4,8},{8,4},{12,16},{16,12},{20,24},{24,20},{28,32},{32,28},{36,40... | collective-permute-start | bytes 294920 | tf_op jit(solution)/shard_map/ppermute | solution.py:463
  4.3 20.1 %collective-permute-start.1 = (f32[6,16,256]{2,1,0:T(8,128)}, f32[6,16,256]{2,1,0:T(8,128)S(1)}, u32[]{:S(2)}, u32[]{:S(2)}) collective-permute-start(f32[6,16,256]{2,1,0:T(8,128)} %get-tuple-element.16), channel_id=1, source_target_pairs={{0,4},{4,0},{8,12},{12,8},{16,20},{20,16},{24,28},{28,24},{32,36},... | collective-permute-start | bytes 294920 | tf_op jit(solution)/shard_map/ppermute | solution.py:462
  9.1 13.2 %copy-start.9 = (f32[6,8]{0,1:T(8,128)S(1)}, f32[6,8]{0,1:T(8,128)}, u32[]{:S(2)}) copy-start(f32[6,8]{0,1:T(8,128)} %constant.81.clone) | copy-start | bytes 580
  9.1 13.2 %copy-start.10 = (f32[6,8]{0,1:T(8,128)S(1)}, f32[6,8]{0,1:T(8,128)}, u32[]{:S(2)}) copy-start(f32[6,8]{0,1:T(8,128)} %constant.80.clone) | copy-start | bytes 580
  9.1 13.2 %copy-start.11 = (f32[6,8]{0,1:T(8,128)S(1)}, f32[6,8]{0,1:T(8,128)}, u32[]{:S(2)}) copy-start(f32[6,8]{0,1:T(8,128)} %constant.79.clone) | copy-start | bytes 580
  9.1 43.4 %all-to-all-start = ((f32[64,20,2,128]{3,2,1,0:T(2,128)}), f32[64,20,2,128]{3,2,1,0:T(2,128)S(1)}, u32[]{:S(2)}, u32[]{:S(2)}) async-start(f32[64,20,2,128]{3,2,1,0:T(2,128)} %bitcast.95), calls=%async_computation | async-start | bytes 2621440 | tf_op jit(solution)/shard_map/all_to_all | solution.py:493
  24.7 6.0 %collective-permute-start.3 = (f32[6,8,256]{2,1,0:T(8,128)S(1)}, f32[6,8,256]{2,1,0:T(8,128)S(1)}, u32[]{:S(2)}, u32[]{:S(2)}) collective-permute-start(f32[6,8,256]{2,1,0:T(8,128)S(1)} %get-tuple-element.71), channel_id=1, source_target_pairs={{0,1},{1,0},{2,3},{3,2},{4,5},{5,4},{6,7},{7,6},{8,9},{9,8},{10,11... | collective-permute-start | bytes 147464 | tf_op jit(solution)/shard_map/ppermute | solution.py:478
  26.3 7.8 %collective-permute-start.2 = (f32[6,8,256]{2,1,0:T(8,128)S(1)}, f32[6,8,256]{2,1,0:T(8,128)S(1)}, u32[]{:S(2)}, u32[]{:S(2)}) collective-permute-start(f32[6,8,256]{2,1,0:T(8,128)S(1)} %get-tuple-element.72), channel_id=1, source_target_pairs={{1,2},{2,1},{5,6},{6,5},{9,10},{10,9},{13,14},{14,13},{17,18},{18,... | collective-permute-start | bytes 147464 | tf_op jit(solution)/shard_map/ppermute | solution.py:479
  46.8 22.3 %copy-start.2 = (f32[2,2,1,256,256]{4,3,2,1,0:T(8,128)S(1)}, f32[2,2,1,256,256]{4,3,2,1,0:T(8,128)}, u32[]{:S(2)}) copy-start(f32[2,2,1,256,256]{4,3,2,1,0:T(8,128)} %param.16) | copy-start | bytes 3145732
  46.8 22.3 %copy-start.3 = (s32[256,256]{1,0:T(8,128)S(1)}, s32[256,256]{1,0:T(8,128)}, u32[]{:S(2)}) copy-start(s32[256,256]{1,0:T(8,128)} %mask.1) | copy-start | bytes 786436
  52.5 8.5 %collective-permute-start.4 = (f32[256,128]{1,0:T(8,128)S(1)}, f32[256,128]{1,0:T(8,128)S(1)}, u32[]{:S(2)}, u32[]{:S(2)}) collective-permute-start(f32[256,128]{1,0:T(8,128)S(1)} %bitcast.100), channel_id=1, source_target_pairs={{96,0},{100,4},{104,8},{108,12},{0,16},{4,20},{8,24},{12,28},{32,3... | collective-permute-start | bytes 393224 | tf_op jit(solution)/shard_map/ppermute | solution.py:513
  58.4 9.4 %collective-permute-start.5 = (f32[256,128]{1,0:T(8,128)S(1)}, f32[256,128]{1,0:T(8,128)S(1)}, u32[]{:S(2)}, u32[]{:S(2)}) collective-permute-start(f32[256,128]{1,0:T(8,128)S(1)} %bitcast.101), channel_id=1, source_target_pairs={{96,2},{100,6},{104,10},{108,14},{0,18},{4,22},{8,26},{12,30},{32,... | collective-permute-start | bytes 393224 | tf_op jit(solution)/shard_map/ppermute | solution.py:513
  61.0 7.1 %collective-permute-start.6 = (f32[256,128]{1,0:T(8,128)S(1)}, f32[256,128]{1,0:T(8,128)S(1)}, u32[]{:S(2)}, u32[]{:S(2)}) collective-permute-start(f32[256,128]{1,0:T(8,128)S(1)} %collective-permute-done.4.p0), channel_id=1, source_target_pairs={{0,1},{1,0},{2,3},{3,2},{4,5},{5,4},{6,7},{7,6},{8,9},{9,8},{10,11... | collective-permute-start | bytes 393224 | tf_op jit(solution)/shard_map/ppermute | solution.py:514
  67.8 1.3 %collective-permute-start.7 = (f32[256,128]{1,0:T(8,128)S(1)}, f32[256,128]{1,0:T(8,128)S(1)}, u32[]{:S(2)}, u32[]{:S(2)}) collective-permute-start(f32[256,128]{1,0:T(8,128)S(1)} %collective-permute-done.5.p1), channel_id=1, source_target_pairs={{0,1},{1,0},{2,3},{3,2},{4,5},{5,4},{6,7},{7,6},{8,9},{9,8},{10,11... | collective-permute-start | bytes 393224 | tf_op jit(solution)/shard_map/ppermute | solution.py:514
  74.5 1.8 %collective-permute-start.8 = (f32[2,280,128]{2,1,0:T(8,128)S(1)}, f32[2,280,128]{2,1,0:T(8,128)S(1)}, u32[]{:S(2)}, u32[]{:S(2)}) collective-permute-start(f32[2,280,128]{2,1,0:T(8,128)S(1)} %get-tuple-element.26), channel_id=1, source_target_pairs={{0,1},{1,0},{2,3},{3,2},{4,5},{5,4},{6,7},{7,6},{8,9},{9,8},{10,11... | collective-permute-start | bytes 860168 | tf_op jit(solution)/shard_map/ppermute | solution.py:519
  76.4 22.0 %copy-start = (bf16[288,432]{1,0:T(8,128)(2,1)S(1)}, bf16[288,432]{1,0:T(8,128)(2,1)}, u32[]{:S(2)}) copy-start(bf16[288,432]{1,0:T(8,128)(2,1)} %pad_maximum_fusion.wide) | copy-start | bytes 746500
  76.4 22.0 %copy-start.1 = (f32[2,16,4,256]{3,2,1,0:T(4,128)S(1)}, f32[2,16,4,256]{3,2,1,0:T(4,128)}, u32[]{:S(2)}) copy-start(f32[2,16,4,256]{3,2,1,0:T(4,128)} %init.3) | copy-start | bytes 393220
  76.4 22.0 %copy-start.5 = (bf16[3,2,320,256]{3,2,1,0:T(8,128)(2,1)S(1)}, bf16[3,2,320,256]{3,2,1,0:T(8,128)(2,1)}, u32[]{:S(2)}) copy-start(bf16[3,2,320,256]{3,2,1,0:T(8,128)(2,1)} %get-tuple-element.20.xb) | copy-start | bytes 2949124
  76.5 9.1 %collective-permute-start.9 = (f32[280,128]{1,0:T(8,128)S(1)}, f32[280,128]{1,0:T(8,128)S(1)}, u32[]{:S(2)}, u32[]{:S(2)}) collective-permute-start(f32[280,128]{1,0:T(8,128)S(1)} %get-tuple-element.56), channel_id=1, source_target_pairs={{0,96},{4,100},{8,104},{12,108},{16,0},{20,4},{24,8},{28,12},{32,3... | collective-permute-start | bytes 430088 | tf_op jit(solution)/shard_map/ppermute | solution.py:522
  78.5 12.2 %collective-permute-start.10 = (f32[280,128]{1,0:T(8,128)S(1)}, f32[280,128]{1,0:T(8,128)S(1)}, u32[]{:S(2)}, u32[]{:S(2)}) collective-permute-start(f32[280,128]{1,0:T(8,128)S(1)} %get-tuple-element.55), channel_id=1, source_target_pairs={{2,96},{6,100},{10,104},{14,108},{18,0},{22,4},{26,8},{30,12},{34,... | collective-permute-start | bytes 430088 | tf_op jit(solution)/shard_map/ppermute | solution.py:522
  91.6 18.1 %all-to-all-start.1 = ((f32[64,5,2,128]{3,2,1,0:T(2,128)}), f32[64,5,2,128]{3,2,1,0:T(2,128)S(1)}, u32[]{:S(2)}, u32[]{:S(2)}) async-start(f32[64,5,2,128]{3,2,1,0:T(2,128)} %bitcast.40), calls=%async_computation.1 | async-start | bytes 655360 | tf_op jit(solution)/shard_map/all_to_all | solution.py:528
  110.0 7.2 %collective-permute-start.13 = (f32[24,128]{1,0:T(8,128)S(1)}, f32[24,128]{1,0:T(8,128)S(1)}, u32[]{:S(2)}, u32[]{:S(2)}) collective-permute-start(f32[24,128]{1,0:T(8,128)S(1)} %reshape.243), channel_id=1, source_target_pairs={{0,3},{1,2},{2,1},{3,0},{4,7},{5,6},{6,5},{7,4},{8,11},{9,10},{10,... | collective-permute-start | bytes 36872 | tf_op jit(solution)/shard_map/ppermute | solution.py:534
  115.1 4.0 %collective-permute-start.12 = (f32[24,128]{1,0:T(8,128)S(1)}, f32[24,128]{1,0:T(8,128)S(1)}, u32[]{:S(2)}, u32[]{:S(2)}) collective-permute-start(f32[24,128]{1,0:T(8,128)S(1)} %reshape.243), channel_id=1, source_target_pairs={{0,2},{1,3},{2,0},{3,1},{4,6},{5,7},{6,4},{7,5},{8,10},{9,11},{10,... | collective-permute-start | bytes 36872 | tf_op jit(solution)/shard_map/ppermute | solution.py:534
  116.2 2.9 %collective-permute-start.11 = (f32[24,128]{1,0:T(8,128)S(1)}, f32[24,128]{1,0:T(8,128)S(1)}, u32[]{:S(2)}, u32[]{:S(2)}) collective-permute-start(f32[24,128]{1,0:T(8,128)S(1)} %reshape.243), channel_id=1, source_target_pairs={{0,1},{1,0},{2,3},{3,2},{4,5},{5,4},{6,7},{7,6},{8,9},{9,8},{10,11... | collective-permute-start | bytes 36872 | tf_op jit(solution)/shard_map/ppermute | solution.py:534
  (7 other events, 37.4 us)
